TPU v7x, 128 devices: a whole 4x4x4 slice. The times are simulated.
128 devices in a mesh: row: 4 (over z), col: 32 (over x, y, core).
Axes of the slice: x: 4, y: 4, z: 4, core: 2. Of those that a mesh axis runs over, the one named last changes fastest.
Arguments:
- queries: bfloat16 [1024, 4096], P(('row', 'col')), may hold values from -8 to 8
- passages: bfloat16 [65536, 4096], P(('row', 'col')), may hold values from -8 to 8
- adapter: bfloat16 [4096, 768], replicated, may hold values from -0.09375 to 0.09375
- positives: int32 [1024], replicated, may hold values from 0 to 65535
Outputs:
- adapter_grad: float32 [4096, 768], P(('row', 'col'))
- query_grad: bfloat16 [1024, 4096], P(('row', 'col'))
- losses: float32 [1024], P(('row', 'col'))
All inputs are finite; a program needn't handle non-finite values.
Results may differ from a plain program's by a relative error of at most 0.0088.
Values may be sent and summed in bfloat16 or wider, within the bound.
No kernel may reach another device: no remote copies, remote signals or barrier semaphores. Data moves between devices by JAX's collectives and lax.ppermute only.
A program may use at most 128 MiB of HBM per device.

v0:
```python
import functools
import itertools

import jax
import jax.numpy as jnp
from jax import lax
from jax.experimental import pallas as pl
from jax.experimental.pallas import tpu as pltpu
from jax.sharding import Mesh
from jax.sharding import PartitionSpec as P

CHIP = ("row", "col_0", "col_1")
CORE = "col_2"
ALL = (*CHIP, CORE)
SIDE = 4
SWAP = [(0, 1), (1, 0)]
HOPS = (2, 1, 3)
ROUTES = ((0, 1, 2), (1, 0, 2))
F32 = jnp.float32
BF16 = jnp.bfloat16


def dot(left, right, dims):
    return lax.dot_general(left, right, (dims, ((), ())), preferred_element_type=F32)


def to_partner(x):
    return lax.ppermute(x, CORE, SWAP)


def exchanged(blocks):
    return lax.all_to_all(blocks, CHIP, split_axis=0, concat_axis=0, tiled=True)


def number(place, core):
    return ((place[0] * SIDE + place[1]) * SIDE + place[2]) * 2 + core


def shift(stage, hops):
    pairs = []
    for *place, core in itertools.product(range(SIDE), range(SIDE), range(SIDE), range(2)):
        there = list(place)
        axis = ROUTES[core][stage]
        there[axis] = (there[axis] + hops) % SIDE
        pairs.append((number(place, core), number(there, core)))
    return pairs


def block(x, which, dim):
    size = x.shape[dim] // SIDE
    return lax.dynamic_slice_in_dim(x, which % SIDE * size, size, dim)


def dealt(x, place, stage, dim):
    sent = [
        lax.ppermute(block(x, place + hops, dim), ALL, shift(stage, hops)) for hops in HOPS
    ]
    return [block(x, place, dim), *sent]


def kernel_call(body, outs, scalars, ins, *, grid=(), scratch=(), limit=16):
    room = pl.BlockSpec(memory_space=pltpu.VMEM)
    arrays, in_specs = [], []
    for entry in ins:
        array, spec = entry if isinstance(entry, tuple) else (entry, room)
        place = pltpu.VMEM if spec is room else pltpu.HBM
        arrays.append(pltpu.with_memory_space_constraint(array, place))
        in_specs.append(spec)
    shapes, out_specs = [], []
    for shape, dtype, *spec in outs:
        shapes.append((pltpu.HBM if spec else pltpu.VMEM)(shape, dtype))
        out_specs.append(spec[0] if spec else room)
    return pl.pallas_call(
        body,
        grid_spec=pltpu.PrefetchScalarGridSpec(
            num_scalar_prefetch=1,
            grid=grid,
            in_specs=in_specs,
            out_specs=out_specs,
            scratch_shapes=list(scratch),
        ),
        out_shape=shapes,
        compiler_params=pltpu.CompilerParams(vmem_limit_bytes=limit << 20),
    )(scalars, *arrays)


def turn_kernel(core_ref, passages_ref, queries_ref, kept_ref, given_ref, kept_q_ref, given_q_ref):
    low = core_ref[0] == 0
    step = pl.program_id(0)
    lanes, width = 128, passages_ref.shape[1]
    run = 32
    base = pl.multiple_of(step * (width // 2), width // 2)
    unit = (
        lax.broadcasted_iota(jnp.int32, (lanes, lanes), 0)
        == lax.broadcasted_iota(jnp.int32, (lanes, lanes), 1)
    ).astype(BF16)
    for tile in range(width // lanes):
        here = passages_ref[:, tile * lanes : (tile + 1) * lanes]
        turned = dot(unit, here, ((1,), (1,))).astype(BF16)
        for part in range(2):
            first = turned[2 * part * run : (2 * part + 1) * run]
            second = turned[(2 * part + 1) * run : (2 * part + 2) * run]
            at = (2 * tile + part) * run
            kept_ref[pl.ds(base + at, run), :] = jnp.where(low, first, second)
            given_ref[at : at + run, :] = jnp.where(low, second, first)
    line = lax.broadcasted_iota(jnp.int32, (2 * lanes, lanes), 0)
    lane = lax.broadcasted_iota(jnp.int32, (2 * lanes, lanes), 1)
    source = lane // run * (2 * run) + lane % run
    mine = core_ref[0] * run
    pick = (line == source + mine).astype(BF16)
    leave = (line == source + run - mine).astype(BF16)
    for tile in range(width // (2 * lanes)):
        here = queries_ref[:, tile * 2 * lanes : (tile + 1) * 2 * lanes]
        to = pl.ds(pl.multiple_of(base + tile * lanes, lanes), lanes)
        kept_q_ref[:, to] = dot(here, pick, ((1,), (0,))).astype(BF16)
        given_q_ref[:, to] = dot(here, leave, ((1,), (0,))).astype(BF16)


def score_kernel(scale, here_ref, qa_ref, own_ref, other_ref, wanted_ref, scores_ref, stats_ref):
    slab = own_ref.shape[0]
    qa, wanted = qa_ref[...], wanted_ref[...]
    lines = lax.broadcasted_iota(jnp.int32, (slab, qa.shape[0]), 0)
    parts = []
    for k, ref in enumerate((own_ref, other_ref)):
        part = dot(ref[...], qa, ((1,), (1,))) * scale
        scores_ref[k * slab : (k + 1) * slab, :] = part
        hit = lines == wanted - here_ref[k]
        parts.append((part, jnp.sum(jnp.where(hit, part, 0.0), axis=0, keepdims=True)))
    top = jnp.maximum(*[jnp.max(part, axis=0, keepdims=True) for part, _ in parts])
    mass = sum(jnp.sum(jnp.exp(part - top), axis=0, keepdims=True) for part, _ in parts)
    lse = top + jnp.log(mass)
    picked = parts[0][1] + parts[1][1]
    lines = qa.shape[0] // 128
    for k in range(lines):
        at = slice(k * 128, (k + 1) * 128)
        stats_ref[k : k + 1, :] = lse[:, at]
        stats_ref[lines + k : lines + k + 1, :] = picked[:, at]


def soft_kernel(scale, here_ref, scores_ref, packet_ref, wanted_ref, qa_ref, own_ref, other_ref, dpa_ref, dqa_ref, stats_ref):
    slab, count = own_ref.shape[0], qa_ref.shape[0]
    lines = count // 128
    packet = packet_ref[...]
    each = packet[:, :lines]
    top = jnp.max(each, axis=0)
    lse = top + jnp.log(jnp.sum(jnp.exp(each - top[None]), axis=0))
    stats_ref[...] = lse - jnp.sum(packet[:, lines:], axis=0)
    row = jnp.concatenate([lse[k : k + 1] for k in range(lines)], axis=1)
    wanted = wanted_ref[...]
    rank = lax.broadcasted_iota(jnp.int32, (slab, count), 0)
    dqa = None
    for k, ref in enumerate((own_ref, other_ref)):
        at = slice(k * slab, (k + 1) * slab)
        probs = jnp.exp(scores_ref[at, :] - row)
        hit = (rank == wanted - here_ref[k]).astype(F32)
        dscores = ((probs - hit) * scale).astype(BF16)
        dpa_ref[at, :] = dot(dscores, qa_ref[...], ((1,), (0,))).astype(BF16)
        part = dot(dscores, ref[...], ((0,), (0,)))
        dqa = part if dqa is None else dqa + part
    dqa_ref[...] = dqa.astype(BF16)


def grad_kernel(where_ref, kept_ref, got_ref, mine_ref, theirs_ref, *refs):
    outs, (left_ref, sum_ref, sems) = refs[:-3], refs[-3:]
    slab = kept_ref.shape[1]
    piece = kept_ref.shape[0] // (SIDE * SIDE)
    low = where_ref[0] == 0
    copies = []
    for k, hops in enumerate((*HOPS, 0)):
        place = lax.rem(where_ref[1] + hops, SIDE)
        copies.append([])
        for j in range(SIDE):
            index = jnp.where(low, place * SIDE + j, j * SIDE + place)
            rows = pl.ds(pl.multiple_of(index * piece, piece), piece)
            for half, ref in enumerate((kept_ref, got_ref)):
                to = left_ref.at[k, j * piece : (j + 1) * piece, half * slab : (half + 1) * slab]
                copies[-1].append(pltpu.make_async_copy(ref.at[rows], to, sems.at[k, 2 * j + half]))
                copies[-1][-1].start()
    for k in range(2):
        ours, yours = slice(k * slab, (k + 1) * slab), slice((1 - k) * slab, (2 - k) * slab)
        both = mine_ref[ours, :].astype(F32) + theirs_ref[yours, :].astype(F32)
        sum_ref[ours, :] = both.astype(BF16)
    for k, out in enumerate(outs):
        for copy in copies[k]:
            copy.wait()
        out[...] = dot(left_ref[k], sum_ref[...], ((1,), (0,))).astype(BF16)


def join_kernel(stop_ref, own_ref, far_ref, next_ref, last_ref, line_ref, *outs):
    size = own_ref.shape[0]
    piece = outs[0].shape[0]
    for out, hops in zip(outs, (*HOPS, 0)):
        place = lax.rem(stop_ref[0] + hops, SIDE)
        rows = pl.ds(pl.multiple_of(place * piece, piece), piece)
        lanes = pl.ds(pl.multiple_of(place * piece, piece), piece)
        part = dot(line_ref[:, lanes], line_ref[:, size:], ((0,), (0,)))
        for ref in (own_ref, far_ref, next_ref, last_ref):
            part += ref[rows, :].astype(F32)
        out[...] = part.astype(BF16)


def line_block(x, which, core):
    cut = x.reshape(x.shape[0], SIDE, SIDE, -1)
    low = lax.dynamic_index_in_dim(cut, which % SIDE, 1, keepdims=False)
    high = lax.dynamic_index_in_dim(cut, which % SIDE, 2, keepdims=False)
    return jnp.where(core == 0, low, high).reshape(x.shape[0], -1)


def total(parts):
    first, *others = parts
    out = first.astype(F32)
    for part in others:
        out = out + part.astype(F32)
    return out


def per_device(queries, passages, adapter, positives):
    width = adapter.shape[1]
    scale = width ** (-0.5)
    din = adapter.shape[0]
    own_rows, slab_rows = queries.shape[0], passages.shape[0]
    chips = lax.axis_size(CHIP)
    half = chips * own_rows
    chip, core = lax.axis_index(CHIP), lax.axis_index(CORE)
    here = chip * 2 + core
    place = [lax.axis_index(axis) for axis in CHIP]
    stops = [
        jnp.where(core == 0, place[ROUTES[0][k]], place[ROUTES[1][k]]) for k in range(3)
    ]

    parts = 8
    span = din // parts
    local_qa = dot(queries, adapter, ((1,), (0,))).astype(BF16)
    qa = exchanged(jnp.broadcast_to(local_qa[None], (chips, own_rows, width)))
    qa = qa.reshape(half, width)
    pa = dot(passages, adapter, ((1,), (0,))).astype(BF16)
    pa_other = to_partner(pa)
    kept, given, kept_queries, given_queries = kernel_call(
        turn_kernel,
        [
            ((din // 2, slab_rows), BF16),
            ((din // 2, slab_rows), BF16, pl.BlockSpec((span // 2, slab_rows), lambda i, c: (i, 0))),
            ((own_rows, din // 2), BF16),
            ((own_rows, din // 2), BF16),
        ],
        core.reshape(1),
        [
            (passages, pl.BlockSpec((slab_rows, span), lambda i, c: (0, i))),
            (queries, pl.BlockSpec((own_rows, span), lambda i, c: (0, i))),
        ],
        grid=(parts,),
    )
    got = to_partner(given)
    chip_queries = jnp.concatenate([kept_queries, to_partner(given_queries)], axis=0)

    starts = jnp.stack([here * slab_rows, (here ^ 1) * slab_rows])
    wanted = lax.dynamic_index_in_dim(
        positives.reshape(chips, 2, own_rows), core, 1, keepdims=False
    ).reshape(1, half)
    lines = half // 128
    scores, stats = kernel_call(
        functools.partial(score_kernel, scale),
        [((2 * slab_rows, half), F32), ((2 * lines, 128), F32)],
        starts,
        [qa, pa, pa_other, wanted],
    )
    packet = jnp.broadcast_to(stats[None], (chips, *stats.shape))
    packet = exchanged(packet)
    dpa, dqa, losses = kernel_call(
        functools.partial(soft_kernel, scale),
        [((2 * slab_rows, width), BF16), ((half, width), BF16), ((lines, 128), F32)],
        starts,
        [scores, packet, wanted, qa, pa, pa_other],
    )
    losses = lax.dynamic_slice_in_dim(losses.reshape(half), chip * own_rows, own_rows, 0)
    dpa_got = to_partner(dpa)
    dqa = dqa.reshape(chips, own_rows, width)
    dqa_own = exchanged(dqa)
    dqa_own = jnp.sum(dqa_own.astype(F32), axis=0).astype(BF16)
    chip_dqa = jnp.concatenate([dqa_own, to_partner(dqa_own)], axis=0)
    loads = [
        jnp.concatenate([line_block(chip_queries, stops[0] + hops, core), chip_dqa], axis=1)
        for hops in (*HOPS, 0)
    ]
    line = [lax.ppermute(x, ALL, shift(0, hops)) for x, hops in zip(loads, HOPS)]
    line = jnp.concatenate([loads[-1], *line], axis=0)

    far = pl.BlockSpec(memory_space=pltpu.HBM)
    *sent, own = kernel_call(
        grad_kernel,
        [((kept.shape[0] // SIDE, width), BF16)] * SIDE,
        jnp.stack([core, stops[0]]),
        [(kept, far), (got, far), dpa, dpa_got],
        scratch=[
            pltpu.VMEM((SIDE, kept.shape[0] // SIDE, 2 * slab_rows), BF16),
            pltpu.VMEM(dpa.shape, BF16),
            pltpu.SemaphoreType.DMA((SIDE, 2 * SIDE)),
        ],
    )
    sent = [lax.ppermute(x, ALL, shift(0, hops)) for x, hops in zip(sent, HOPS)]
    *sent, own = kernel_call(
        join_kernel,
        [((own.shape[0] // SIDE, width), BF16)] * SIDE,
        stops[1].reshape(1),
        [own, *sent, line],
    )
    sent = [lax.ppermute(x, ALL, shift(1, hops)) for x, hops in zip(sent, HOPS)]
    grad = total([own, *sent]).astype(BF16)
    grad = total(dealt(grad, stops[2], 2, 0))

    query_grad = dot(dqa_own, adapter, ((1,), (1,))).astype(BF16)
    return (grad, query_grad, losses)


def solution(mesh):
    torus = Mesh(mesh.devices.reshape(mesh.shape["row"], SIDE, SIDE, 2), ALL)
    rows = P(ALL, None)
    return jax.shard_map(
        per_device,
        mesh=torus,
        in_specs=(rows, rows, P(), P()),
        out_specs=(rows, rows, P(ALL)),
        check_vma=False,
    )
```

profile of v0, /device:TPU:0, one launch (start us, length us, event | category | flops | bytes accessed | tf_op | source)
XLA Modules:
  0.0 137.1 jit_solution(8795953891861714984)
XLA Ops:
  0.7 7.6 %convolution_convert_fusion.1.own_ref = bf16[512,768]{1,0:T(8,128)(2,1)S(1)} fusion(bf16[512,4096]{1,0:T(8,128)(2,1)} %passages_ref.1, bf16[4096,768]{1,0:T(8,128)(2,1)} %param.6), kind=kOutput, calls=%fused_computation.1 | convolution fusion | flops 3221618688 | bytes 11272192 | tf_op jit(solution)/shard_map/dot_general | solution.py:24
  9.3 1.0 broadcast_in_dim.4
  10.3 11.5 %all-to-all-start = ((bf16[64,8,768]{2,1,0:T(8,128)(2,1)}), bf16[64,8,768]{2,1,0:T(8,128)(2,1)S(1)}, u32[]{:S(2)}, u32[]{:S(2)}) async-start(bf16[64,8,768]{2,1,0:T(8,128)(2,1)} %broadcast_in_dim.4), calls=%async_computation | async-start | bytes 1572864 | tf_op jit(solution)/shard_map/all_to_all | solution.py:32
  21.8 7.2 %shard_map.67 = (bf16[2048,512]{1,0:T(8,128)(2,1)S(1)}, bf16[2048,512]{1,0:T(8,128)(2,1)}, bf16[8,2048]{1,0:T(8,128)(2,1)S(1)}, bf16[8,2048]{1,0:T(8,128)(2,1)S(1)}) custom-call(s32[1]{0:T(128)} %bitcast.1.core_ref, bf16[512,4096]{1,0:T(8,128)(2,1)} %passages_ref.1, bf16[8,4096]{1,0:T(8,128)(2,1)} %queries_ref.1), custom_call_target="tpu_custom_call" | custom-call | tf_op jit(solution)/shard_map/pallas_call | solution.py:73
  29.0 1.3 copy-done
  30.9 7.5 %all-to-all-done = bf16[64,8,768]{2,1,0:T(8,128)(2,1)S(1)} async-done(((bf16[64,8,768]{2,1,0:T(8,128)(2,1)}), bf16[64,8,768]{2,1,0:T(8,128)(2,1)S(1)}, u32[]{:S(2)}, u32[]{:S(2)}) %all-to-all-start) | async-done | bytes 786464 | tf_op jit(solution)/shard_map/all_to_all | solution.py:32
  38.4 2.0 %shard_map.68 = (f32[1024,512]{1,0:T(8,128)S(1)}, f32[8,128]{1,0:T(8,128)S(1)}) custom-call(s32[2]{0:T(128)S(1)} %pad_add_fusion.1.here_ref, bf16[512,768]{1,0:T(8,128)(2,1)S(1)} %bitcast.50, bf16[512,768]{1,0:T(8,128)(2,1)S(1)} %convolution_convert_fusion.1.own_ref, bf16[512,768]{1,0:T(8,128)(2,1)S(1)} %collective-permute-done.1.other_ref, ...), custom_call_target="tpu_custom_call" | custom-call | tf_op jit(solution)/shard_map/pallas_call | solution.py:73
  40.5 15.1 %all_to_all.15.packet_ref = f32[64,8,128]{2,1,0:T(8,128)S(1)} all-to-all(f32[64,8,128]{2,1,0:T(8,128)S(1)} %broadcast_in_dim.5), channel_id=1, replica_groups=mesh['row'=4,'col_0'=4,'col_1'=4,'col_2'=2] {'row','col_0','col_1'}, dimensions={0} | all-to-all | bytes 524288 | tf_op jit(solution)/shard_map/all_to_all | solution.py:32
  55.6 3.7 %shard_map.69 = (bf16[1024,768]{1,0:T(8,128)(2,1)}, bf16[512,768]{1,0:T(8,128)(2,1)}, f32[4,128]{1,0:T(4,128)S(1)}) custom-call(s32[2]{0:T(128)S(1)} %pad_add_fusion.1.here_ref, f32[1024,512]{1,0:T(8,128)S(1)} %get-tuple-element.22.scores_ref, f32[64,8,128]{2,1,0:T(8,128)S(1)} %all_to_all.15.packet_ref, s32[1,512]{1,0:T(1,128)S(1)} %reshape.49.wanted_ref, ...), custom_call_target="tpu_custom_call" | custom-call | tf_op jit(solution)/shard_map/pallas_call | solution.py:73
  59.3 4.9 %all-to-all-start.2 = ((bf16[64,8,768]{2,1,0:T(8,128)(2,1)}), bf16[64,8,768]{2,1,0:T(8,128)(2,1)S(1)}, u32[]{:S(2)}, u32[]{:S(2)}) async-start(bf16[64,8,768]{2,1,0:T(8,128)(2,1)} %bitcast.6), calls=%async_computation.2 | async-start | bytes 1572864 | tf_op jit(solution)/shard_map/all_to_all | solution.py:32
  66.0 14.9 %all-to-all-done.2 = bf16[64,8,768]{2,1,0:T(8,128)(2,1)S(1)} async-done(((bf16[64,8,768]{2,1,0:T(8,128)(2,1)}), bf16[64,8,768]{2,1,0:T(8,128)(2,1)S(1)}, u32[]{:S(2)}, u32[]{:S(2)}) %all-to-all-start.2) | async-done | bytes 786464 | tf_op jit(solution)/shard_map/all_to_all | solution.py:32
  81.3 8.8 %shard_map.70 = (bf16[512,768]{1,0:T(8,128)(2,1)}, bf16[512,768]{1,0:T(8,128)(2,1)}, bf16[512,768]{1,0:T(8,128)(2,1)}, bf16[512,768]{1,0:T(8,128)(2,1)S(1)}) custom-call(s32[2]{0:T(128)S(1)} %pad_add_fusion.where_ref, bf16[2048,512]{1,0:T(8,128)(2,1)} %copy-done, bf16[2048,512]{1,0:T(8,128)(2,1)} %collective-permute-done.got_ref, ...), custom_call_target="tpu_custom_call" | custom-call | tf_op jit(solution)/shard_map/pallas_call | solution.py:73
  91.8 2.3 %collective-permute-start.5 = (bf16[512,768]{1,0:T(8,128)(2,1)}, bf16[512,768]{1,0:T(8,128)(2,1)S(1)}, u32[]{:S(2)}, u32[]{:S(2)}) collective-permute-start(bf16[512,768]{1,0:T(8,128)(2,1)} %get-tuple-element.28), channel_id=1, source_target_pairs={{0,96},{1,25},{2,98},{3,27},{4,100},{5,29},{6,102},{7,31},{8,104},... | collective-permute-start | bytes 2359304 | tf_op jit(solution)/shard_map/ppermute | solution.py:300
  94.1 1.8 %collective-permute-start.8 = (bf16[16,1280]{1,0:T(8,128)(2,1)S(1)}, bf16[16,1280]{1,0:T(8,128)(2,1)S(1)}, u32[]{:S(2)}, u32[]{:S(2)}) collective-permute-start(bf16[16,1280]{1,0:T(8,128)(2,1)S(1)} %get-tuple-element.48), channel_id=1, source_target_pairs={{0,64},{1,17},{2,66},{3,19},{4,68},{5,21},{6,70},{7,23},{8,72},{9,... | collective-permute-start | bytes 122888 | tf_op jit(solution)/shard_map/ppermute | solution.py:285
  96.0 16.9 %collective-permute-done.8 = bf16[16,1280]{1,0:T(8,128)(2,1)S(1)} collective-permute-done((bf16[16,1280]{1,0:T(8,128)(2,1)S(1)}, bf16[16,1280]{1,0:T(8,128)(2,1)S(1)}, u32[]{:S(2)}, u32[]{:S(2)}) %collective-permute-start.8) | collective-permute-done | bytes 40992 | tf_op jit(solution)/shard_map/ppermute | solution.py:285
  113.5 3.3 %collective-permute-done.10 = bf16[16,1280]{1,0:T(8,128)(2,1)S(1)} collective-permute-done((bf16[16,1280]{1,0:T(8,128)(2,1)S(1)}, bf16[16,1280]{1,0:T(8,128)(2,1)S(1)}, u32[]{:S(2)}, u32[]{:S(2)}) %collective-permute-start.10) | collective-permute-done | bytes 40992 | tf_op jit(solution)/shard_map/ppermute | solution.py:285
  116.9 1.2 shard_map.71
  118.1 1.0 collective-permute-start.11
  119.3 3.0 %collective-permute-start.13 = (bf16[128,768]{1,0:T(8,128)(2,1)S(1)}, bf16[128,768]{1,0:T(8,128)(2,1)S(1)}, u32[]{:S(2)}, u32[]{:S(2)}) collective-permute-start(bf16[128,768]{1,0:T(8,128)(2,1)S(1)} %get-tuple-element.35), channel_id=1, source_target_pairs={{0,24},{1,97},{2,26},{3,99},{4,28},{5,101},{6,30},{7,103},{8,0},{9... | collective-permute-start | bytes 589832 | tf_op jit(solution)/shard_map/ppermute | solution.py:307
  122.9 2.6 %collective-permute-done.11 = bf16[128,768]{1,0:T(8,128)(2,1)S(1)} collective-permute-done((bf16[128,768]{1,0:T(8,128)(2,1)}, bf16[128,768]{1,0:T(8,128)(2,1)S(1)}, u32[]{:S(2)}, u32[]{:S(2)}) %collective-permute-start.11) | collective-permute-done | bytes 196640 | tf_op jit(solution)/shard_map/ppermute | solution.py:307
  125.6 2.0 %collective-permute-done.12 = bf16[128,768]{1,0:T(8,128)(2,1)S(1)} collective-permute-done((bf16[128,768]{1,0:T(8,128)(2,1)}, bf16[128,768]{1,0:T(8,128)(2,1)S(1)}, u32[]{:S(2)}, u32[]{:S(2)}) %collective-permute-start.12) | collective-permute-done | bytes 196640 | tf_op jit(solution)/shard_map/ppermute | solution.py:307
  127.7 1.0 collective-permute-start.14
  128.7 2.5 %collective-permute-start.16 = (bf16[32,768]{1,0:T(8,128)(2,1)S(1)}, bf16[32,768]{1,0:T(8,128)(2,1)S(1)}, u32[]{:S(2)}, u32[]{:S(2)}) collective-permute-start(bf16[32,768]{1,0:T(8,128)(2,1)S(1)} %get-tuple-element.42), channel_id=1, source_target_pairs={{0,6},{1,7},{2,0},{3,1},{4,2},{5,3},{6,4},{7,5},{8,14},{9,15},{10,... | collective-permute-start | bytes 147464 | tf_op jit(solution)/shard_map/ppermute | solution.py:56
  131.2 5.2 %convolution_convert_fusion = bf16[8,4096]{1,0:T(8,128)(2,1)} fusion(bf16[8,768]{1,0:T(8,128)(2,1)S(1)} %reduce_sum.12, bf16[4096,768]{1,0:T(8,128)(2,1)} %param.6), kind=kOutput, calls=%fused_computation | convolution fusion | flops 50364416 | bytes 6369280 | tf_op jit(solution)/shard_map/dot_general | solution.py:24
  (52 shorter events, 8.1 us)
Async XLA Ops:
  0.6 7.7 %copy-start.1 = (bf16[4096,768]{1,0:T(8,128)(2,1)S(1)}, bf16[4096,768]{1,0:T(8,128)(2,1)}, u32[]{:S(2)}) copy-start(bf16[4096,768]{1,0:T(8,128)(2,1)} %param.6) | copy-start | bytes 18874372
  0.6 7.7 %copy-start.2 = (bf16[8,4096]{1,0:T(8,128)(2,1)S(1)}, bf16[8,4096]{1,0:T(8,128)(2,1)}, u32[]{:S(2)}) copy-start(bf16[8,4096]{1,0:T(8,128)(2,1)} %queries_ref.1) | copy-start | bytes 196612
  8.3 30.2 %collective-permute-start.1 = (bf16[512,768]{1,0:T(8,128)(2,1)S(1)}, bf16[512,768]{1,0:T(8,128)(2,1)S(1)}, u32[]{:S(2)}, u32[]{:S(2)}) collective-permute-start(bf16[512,768]{1,0:T(8,128)(2,1)S(1)} %convolution_convert_fusion.1.own_ref), channel_id=1, source_target_pairs={{0,1},{1,0},{2,3},{3,2},{4,5},{5,4},{6,7},{7,6},{8,9},{9,8},{10,11... | collective-permute-start | bytes 2359304 | tf_op jit(solution)/shard_map/ppermute | solution.py:28
  9.3 21.2 %copy-start.3 = (s32[1024]{0:T(1024)S(1)}, s32[1024]{0:T(1024)}, u32[]{:S(2)}) copy-start(s32[1024]{0:T(1024)} %param.7) | copy-start | bytes 12292
  10.3 28.2 %all-to-all-start = ((bf16[64,8,768]{2,1,0:T(8,128)(2,1)}), bf16[64,8,768]{2,1,0:T(8,128)(2,1)S(1)}, u32[]{:S(2)}, u32[]{:S(2)}) async-start(bf16[64,8,768]{2,1,0:T(8,128)(2,1)} %broadcast_in_dim.4), calls=%async_computation | async-start | bytes 1572864 | tf_op jit(solution)/shard_map/all_to_all | solution.py:32
  29.0 1.3 copy-start
  30.3 50.9 %collective-permute-start = (bf16[2048,512]{1,0:T(8,128)(2,1)}, bf16[2048,512]{1,0:T(8,128)(2,1)}, u32[]{:S(2)}, u32[]{:S(2)}) collective-permute-start(bf16[2048,512]{1,0:T(8,128)(2,1)} %get-tuple-element.21), channel_id=1, source_target_pairs={{0,1},{1,0},{2,3},{3,2},{4,5},{5,4},{6,7},{7,6},{8,9},{9,8},{10,11... | collective-permute-start | bytes 6291464 | tf_op jit(solution)/shard_map/ppermute | solution.py:28
  59.2 22.0 %collective-permute-start.2 = (bf16[1024,768]{1,0:T(8,128)(2,1)}, bf16[1024,768]{1,0:T(8,128)(2,1)S(1)}, u32[]{:S(2)}, u32[]{:S(2)}) collective-permute-start(bf16[1024,768]{1,0:T(8,128)(2,1)} %get-tuple-element.24.mine_ref), channel_id=1, source_target_pairs={{0,1},{1,0},{2,3},{3,2},{4,5},{5,4},{6,7},{7,6},{8,9},{9,8},{10,11... | collective-permute-start | bytes 4718600 | tf_op jit(solution)/shard_map/ppermute | solution.py:28
  59.3 21.6 %all-to-all-start.2 = ((bf16[64,8,768]{2,1,0:T(8,128)(2,1)}), bf16[64,8,768]{2,1,0:T(8,128)(2,1)S(1)}, u32[]{:S(2)}, u32[]{:S(2)}) async-start(bf16[64,8,768]{2,1,0:T(8,128)(2,1)} %bitcast.6), calls=%async_computation.2 | async-start | bytes 1572864 | tf_op jit(solution)/shard_map/all_to_all | solution.py:32
  64.2 1.3 collective-permute-start.6
  81.0 13.0 %collective-permute-start.7 = (bf16[8,768]{1,0:T(8,128)(2,1)S(1)}, bf16[8,768]{1,0:T(8,128)(2,1)S(1)}, u32[]{:S(2)}, u32[]{:S(2)}) collective-permute-start(bf16[8,768]{1,0:T(8,128)(2,1)S(1)} %reduce_sum.12), channel_id=1, source_target_pairs={{0,1},{1,0},{2,3},{3,2},{4,5},{5,4},{6,7},{7,6},{8,9},{9,8},{10,11... | collective-permute-start | bytes 36872 | tf_op jit(solution)/shard_map/ppermute | solution.py:28
  90.1 26.8 %collective-permute-start.3 = (bf16[512,768]{1,0:T(8,128)(2,1)}, bf16[512,768]{1,0:T(8,128)(2,1)S(1)}, u32[]{:S(2)}, u32[]{:S(2)}) collective-permute-start(bf16[512,768]{1,0:T(8,128)(2,1)} %get-tuple-element.26), channel_id=1, source_target_pairs={{0,64},{1,17},{2,66},{3,19},{4,68},{5,21},{6,70},{7,23},{8,72},{9,... | collective-permute-start | bytes 2359304 | tf_op jit(solution)/shard_map/ppermute | solution.py:300
  90.8 26.1 %collective-permute-start.4 = (bf16[512,768]{1,0:T(8,128)(2,1)}, bf16[512,768]{1,0:T(8,128)(2,1)S(1)}, u32[]{:S(2)}, u32[]{:S(2)}) collective-permute-start(bf16[512,768]{1,0:T(8,128)(2,1)} %get-tuple-element.27), channel_id=1, source_target_pairs={{0,32},{1,9},{2,34},{3,11},{4,36},{5,13},{6,38},{7,15},{8,40},{9,1... | collective-permute-start | bytes 2359304 | tf_op jit(solution)/shard_map/ppermute | solution.py:300
  91.8 25.2 %collective-permute-start.5 = (bf16[512,768]{1,0:T(8,128)(2,1)}, bf16[512,768]{1,0:T(8,128)(2,1)S(1)}, u32[]{:S(2)}, u32[]{:S(2)}) collective-permute-start(bf16[512,768]{1,0:T(8,128)(2,1)} %get-tuple-element.28), channel_id=1, source_target_pairs={{0,96},{1,25},{2,98},{3,27},{4,100},{5,29},{6,102},{7,31},{8,104},... | collective-permute-start | bytes 2359304 | tf_op jit(solution)/shard_map/ppermute | solution.py:300
  94.1 18.8 %collective-permute-start.8 = (bf16[16,1280]{1,0:T(8,128)(2,1)S(1)}, bf16[16,1280]{1,0:T(8,128)(2,1)S(1)}, u32[]{:S(2)}, u32[]{:S(2)}) collective-permute-start(bf16[16,1280]{1,0:T(8,128)(2,1)S(1)} %get-tuple-element.48), channel_id=1, source_target_pairs={{0,64},{1,17},{2,66},{3,19},{4,68},{5,21},{6,70},{7,23},{8,72},{9,... | collective-permute-start | bytes 122888 | tf_op jit(solution)/shard_map/ppermute | solution.py:285
  95.8 17.7 %collective-permute-start.9 = (bf16[16,1280]{1,0:T(8,128)(2,1)S(1)}, bf16[16,1280]{1,0:T(8,128)(2,1)S(1)}, u32[]{:S(2)}, u32[]{:S(2)}) collective-permute-start(bf16[16,1280]{1,0:T(8,128)(2,1)S(1)} %get-tuple-element.49), channel_id=1, source_target_pairs={{0,32},{1,9},{2,34},{3,11},{4,36},{5,13},{6,38},{7,15},{8,40},{9,1... | collective-permute-start | bytes 122888 | tf_op jit(solution)/shard_map/ppermute | solution.py:285
  112.9 4.0 %collective-permute-start.10 = (bf16[16,1280]{1,0:T(8,128)(2,1)S(1)}, bf16[16,1280]{1,0:T(8,128)(2,1)S(1)}, u32[]{:S(2)}, u32[]{:S(2)}) collective-permute-start(bf16[16,1280]{1,0:T(8,128)(2,1)S(1)} %get-tuple-element.50), channel_id=1, source_target_pairs={{0,96},{1,25},{2,98},{3,27},{4,100},{5,29},{6,102},{7,31},{8,104},... | collective-permute-start | bytes 122888 | tf_op jit(solution)/shard_map/ppermute | solution.py:285
  118.1 7.5 %collective-permute-start.11 = (bf16[128,768]{1,0:T(8,128)(2,1)}, bf16[128,768]{1,0:T(8,128)(2,1)S(1)}, u32[]{:S(2)}, u32[]{:S(2)}) collective-permute-start(bf16[128,768]{1,0:T(8,128)(2,1)} %get-tuple-element.33), channel_id=1, source_target_pairs={{0,16},{1,65},{2,18},{3,67},{4,20},{5,69},{6,22},{7,71},{8,24},{9,... | collective-permute-start | bytes 589832 | tf_op jit(solution)/shard_map/ppermute | solution.py:307
  119.1 8.5 %collective-permute-start.12 = (bf16[128,768]{1,0:T(8,128)(2,1)}, bf16[128,768]{1,0:T(8,128)(2,1)S(1)}, u32[]{:S(2)}, u32[]{:S(2)}) collective-permute-start(bf16[128,768]{1,0:T(8,128)(2,1)} %get-tuple-element.34), channel_id=1, source_target_pairs={{0,8},{1,33},{2,10},{3,35},{4,12},{5,37},{6,14},{7,39},{8,16},{9,4... | collective-permute-start | bytes 589832 | tf_op jit(solution)/shard_map/ppermute | solution.py:307
  119.3 8.3 %collective-permute-start.13 = (bf16[128,768]{1,0:T(8,128)(2,1)S(1)}, bf16[128,768]{1,0:T(8,128)(2,1)S(1)}, u32[]{:S(2)}, u32[]{:S(2)}) collective-permute-start(bf16[128,768]{1,0:T(8,128)(2,1)S(1)} %get-tuple-element.35), channel_id=1, source_target_pairs={{0,24},{1,97},{2,26},{3,99},{4,28},{5,101},{6,30},{7,103},{8,0},{9... | collective-permute-start | bytes 589832 | tf_op jit(solution)/shard_map/ppermute | solution.py:307
  127.7 8.6 %collective-permute-start.14 = (bf16[32,768]{1,0:T(8,128)(2,1)S(1)}, bf16[32,768]{1,0:T(8,128)(2,1)S(1)}, u32[]{:S(2)}, u32[]{:S(2)}) collective-permute-start(bf16[32,768]{1,0:T(8,128)(2,1)S(1)} %get-tuple-element.41), channel_id=1, source_target_pairs={{0,4},{1,5},{2,6},{3,7},{4,0},{5,1},{6,2},{7,3},{8,12},{9,13},{10,... | collective-permute-start | bytes 147464 | tf_op jit(solution)/shard_map/ppermute | solution.py:56
  128.7 7.6 %collective-permute-start.16 = (bf16[32,768]{1,0:T(8,128)(2,1)S(1)}, bf16[32,768]{1,0:T(8,128)(2,1)S(1)}, u32[]{:S(2)}, u32[]{:S(2)}) collective-permute-start(bf16[32,768]{1,0:T(8,128)(2,1)S(1)} %get-tuple-element.42), channel_id=1, source_target_pairs={{0,6},{1,7},{2,0},{3,1},{4,2},{5,3},{6,4},{7,5},{8,14},{9,15},{10,... | collective-permute-start | bytes 147464 | tf_op jit(solution)/shard_map/ppermute | solution.py:56
  131.2 5.3 %collective-permute-start.15 = (bf16[32,768]{1,0:T(8,128)(2,1)S(1)}, bf16[32,768]{1,0:T(8,128)(2,1)S(1)}, u32[]{:S(2)}, u32[]{:S(2)}) collective-permute-start(bf16[32,768]{1,0:T(8,128)(2,1)S(1)} %get-tuple-element.43), channel_id=1, source_target_pairs={{0,2},{1,3},{2,4},{3,5},{4,6},{5,7},{6,0},{7,1},{8,10},{9,11},{10,... | collective-permute-start | bytes 147464 | tf_op jit(solution)/shard_map/ppermute | solution.py:56
where the time goes:
time: 138 us; the launch traced here: 137 us
  waiting for transfers between devices  48.3 us (35%)
  starting transfers between devices  31.5 us (23%)
  Pallas kernels  22.8 us (17%)
  blocking collectives  15.1 us (11%)
  matrix products  13.7 us (10%)
  local copies, waits for them, and re-layouts  3.78 us (3%)
    pallas_call x5, Pallas kernels, kernel_call(): pl.pallas_call(body, grid_spec=pltpu.PrefetchScalarGridSpec(num_scalar_pr...  22.8 us
    all_to_all x2, waiting for transfers between devices, exchanged(): return lax.all_to_all(blocks, CHIP, split_axis=0, concat_axis=0, tiled=True)  22.4 us
    ppermute x3, waiting for transfers between devices, per_device(): lax.ppermute(x, ALL, shift(0, hops))  20.3 us
    all_to_all x2, starting transfers between devices, exchanged(): return lax.all_to_all(blocks, CHIP, split_axis=0, concat_axis=0, tiled=True)  16.4 us
    all_to_all x1, blocking collectives, exchanged(): return lax.all_to_all(blocks, CHIP, split_axis=0, concat_axis=0, tiled=True)  15.1 us
    dot_general x3, matrix products, dot(): lax.dot_general(left, right, (dims, ((), ())), preferred_element_type=F32)  13.7 us
    ppermute x3, waiting for transfers between devices, per_device(): sent = [lax.ppermute(x, ALL, shift(1, hops)) for x, hops in zip(sent, HOPS)]  4.66 us
    ppermute x3, starting transfers between devices, per_device(): sent = [lax.ppermute(x, ALL, shift(1, hops)) for x, hops in zip(sent, HOPS)]  4.25 us
  transfers between devices with their start and end apart: 19, of which 8 were waited for; matrix products, arithmetic and copies ran while one was open for 6% of the time, Pallas kernels for 16%

commit v1 on v0

--- a/solution.py
+++ b/solution.py
@@ -84,36 +84,70 @@
     )(scalars, *arrays)
 
 
-def turn_kernel(core_ref, passages_ref, queries_ref, kept_ref, given_ref, kept_q_ref, given_q_ref):
+def main_kernel(
+    core_ref, passages_ref, adapter_ref, queries_ref,
+    pa_ref, kept_ref, given_ref, kept_q_ref, given_q_ref,
+    slab_ref, held_ref, turned_ref, acc_ref, in_sems, out_sems,
+):
     low = core_ref[0] == 0
-    step = pl.program_id(0)
-    lanes, width = 128, passages_ref.shape[1]
-    run = 32
-    base = pl.multiple_of(step * (width // 2), width // 2)
-    unit = (
-        lax.broadcasted_iota(jnp.int32, (lanes, lanes), 0)
-        == lax.broadcasted_iota(jnp.int32, (lanes, lanes), 1)
-    ).astype(BF16)
-    for tile in range(width // lanes):
-        here = passages_ref[:, tile * lanes : (tile + 1) * lanes]
-        turned = dot(unit, here, ((1,), (1,))).astype(BF16)
-        for part in range(2):
-            first = turned[2 * part * run : (2 * part + 1) * run]
-            second = turned[(2 * part + 1) * run : (2 * part + 2) * run]
-            at = (2 * tile + part) * run
-            kept_ref[pl.ds(base + at, run), :] = jnp.where(low, first, second)
-            given_ref[at : at + run, :] = jnp.where(low, second, first)
+    parts = in_sems.shape[1]
+    span = slab_ref.shape[1] // parts
+    lanes, run = 128, 32
+    arrivals, leaving = [], []
+    for k in range(parts):
+        at = slice(k * span, (k + 1) * span)
+        arrivals.append(
+            (
+                pltpu.make_async_copy(passages_ref.at[:, at], slab_ref.at[:, at], in_sems.at[0, k]),
+                pltpu.make_async_copy(adapter_ref.at[at], held_ref.at[at], in_sems.at[1, k]),
+            )
+        )
+    for copy in itertools.chain(*arrivals):
+        copy.start()
     line = lax.broadcasted_iota(jnp.int32, (2 * lanes, lanes), 0)
     lane = lax.broadcasted_iota(jnp.int32, (2 * lanes, lanes), 1)
     source = lane // run * (2 * run) + lane % run
     mine = core_ref[0] * run
     pick = (line == source + mine).astype(BF16)
     leave = (line == source + run - mine).astype(BF16)
-    for tile in range(width // (2 * lanes)):
+    for tile in range(queries_ref.shape[1] // (2 * lanes)):
         here = queries_ref[:, tile * 2 * lanes : (tile + 1) * 2 * lanes]
-        to = pl.ds(pl.multiple_of(base + tile * lanes, lanes), lanes)
+        to = slice(tile * lanes, (tile + 1) * lanes)
         kept_q_ref[:, to] = dot(here, pick, ((1,), (0,))).astype(BF16)
         given_q_ref[:, to] = dot(here, leave, ((1,), (0,))).astype(BF16)
+    unit = (
+        lax.broadcasted_iota(jnp.int32, (lanes, lanes), 0)
+        == lax.broadcasted_iota(jnp.int32, (lanes, lanes), 1)
+    ).astype(BF16)
+    for k in range(parts):
+        at = slice(k * span, (k + 1) * span)
+        arrivals[k][0].wait()
+        for tile in range(k * span // lanes, (k + 1) * span // lanes):
+            here = slab_ref[:, tile * lanes : (tile + 1) * lanes]
+            turned = dot(unit, here, ((1,), (1,))).astype(BF16)
+            for part in range(2):
+                first = turned[2 * part * run : (2 * part + 1) * run]
+                second = turned[(2 * part + 1) * run : (2 * part + 2) * run]
+                to = slice((2 * tile + part) * run, (2 * tile + part + 1) * run)
+                turned_ref[0, to, :] = jnp.where(low, first, second)
+                turned_ref[1, to, :] = jnp.where(low, second, first)
+        rows = slice(k * span // 2, (k + 1) * span // 2)
+        for which, ref in enumerate((kept_ref, given_ref)):
+            copy = pltpu.make_async_copy(
+                turned_ref.at[which, rows], ref.at[rows], out_sems.at[which, k]
+            )
+            copy.start()
+            leaving.append(copy)
+        arrivals[k][1].wait()
+        part = dot(slab_ref[:, at], held_ref[at, :], ((1,), (0,)))
+        if k == 0:
+            acc_ref[...] = part
+        elif k < parts - 1:
+            acc_ref[...] += part
+        else:
+            pa_ref[...] = (acc_ref[...] + part).astype(BF16)
+    for copy in leaving:
+        copy.wait()
 
 
 def score_kernel(scale, here_ref, qa_ref, own_ref, other_ref, wanted_ref, scores_ref, stats_ref):
@@ -161,29 +195,40 @@
 
 
 def grad_kernel(where_ref, kept_ref, got_ref, mine_ref, theirs_ref, *refs):
-    outs, (left_ref, sum_ref, sems) = refs[:-3], refs[-3:]
+    outs, (left_ref, sum_ref, sent_ref, in_sems, out_sems) = refs[:SIDE], refs[SIDE:]
     slab = kept_ref.shape[1]
     piece = kept_ref.shape[0] // (SIDE * SIDE)
     low = where_ref[0] == 0
-    copies = []
+    arrivals, leaving = [], []
     for k, hops in enumerate((*HOPS, 0)):
         place = lax.rem(where_ref[1] + hops, SIDE)
-        copies.append([])
+        arrivals.append([])
         for j in range(SIDE):
             index = jnp.where(low, place * SIDE + j, j * SIDE + place)
             rows = pl.ds(pl.multiple_of(index * piece, piece), piece)
-            for half, ref in enumerate((kept_ref, got_ref)):
-                to = left_ref.at[k, j * piece : (j + 1) * piece, half * slab : (half + 1) * slab]
-                copies[-1].append(pltpu.make_async_copy(ref.at[rows], to, sems.at[k, 2 * j + half]))
-                copies[-1][-1].start()
+            for which, ref in enumerate((kept_ref, got_ref)):
+                to = left_ref.at[which, k, j * piece : (j + 1) * piece]
+                copy = pltpu.make_async_copy(ref.at[rows], to, in_sems.at[k, 2 * j + which])
+                arrivals[-1].append(copy)
+    for copy in itertools.chain(*arrivals):
+        copy.start()
     for k in range(2):
         ours, yours = slice(k * slab, (k + 1) * slab), slice((1 - k) * slab, (2 - k) * slab)
         both = mine_ref[ours, :].astype(F32) + theirs_ref[yours, :].astype(F32)
         sum_ref[ours, :] = both.astype(BF16)
     for k, out in enumerate(outs):
-        for copy in copies[k]:
+        for copy in arrivals[k]:
             copy.wait()
-        out[...] = dot(left_ref[k], sum_ref[...], ((1,), (0,))).astype(BF16)
+        block = dot(left_ref[0, k], sum_ref[:slab, :], ((1,), (0,)))
+        block += dot(left_ref[1, k], sum_ref[slab:, :], ((1,), (0,)))
+        if k < SIDE - 1:
+            sent_ref[k] = block.astype(BF16)
+            leaving.append(pltpu.make_async_copy(sent_ref.at[k], out, out_sems.at[k]))
+            leaving[-1].start()
+        else:
+            out[...] = block.astype(BF16)
+    for copy in leaving:
+        copy.wait()
 
 
 def join_kernel(stop_ref, own_ref, far_ref, next_ref, last_ref, line_ref, *outs):
@@ -228,28 +273,34 @@
         jnp.where(core == 0, place[ROUTES[0][k]], place[ROUTES[1][k]]) for k in range(3)
     ]
 
-    parts = 8
-    span = din // parts
+    parts = 4
+    far = pl.BlockSpec(memory_space=pltpu.HBM)
+    dma = pltpu.SemaphoreType.DMA
     local_qa = dot(queries, adapter, ((1,), (0,))).astype(BF16)
     qa = exchanged(jnp.broadcast_to(local_qa[None], (chips, own_rows, width)))
     qa = qa.reshape(half, width)
-    pa = dot(passages, adapter, ((1,), (0,))).astype(BF16)
-    pa_other = to_partner(pa)
-    kept, given, kept_queries, given_queries = kernel_call(
-        turn_kernel,
+    pa, kept, given, kept_queries, given_queries = kernel_call(
+        main_kernel,
         [
-            ((din // 2, slab_rows), BF16),
-            ((din // 2, slab_rows), BF16, pl.BlockSpec((span // 2, slab_rows), lambda i, c: (i, 0))),
+            ((slab_rows, width), BF16),
+            ((din // 2, slab_rows), BF16, far),
+            ((din // 2, slab_rows), BF16, far),
             ((own_rows, din // 2), BF16),
             ((own_rows, din // 2), BF16),
         ],
         core.reshape(1),
-        [
-            (passages, pl.BlockSpec((slab_rows, span), lambda i, c: (0, i))),
-            (queries, pl.BlockSpec((own_rows, span), lambda i, c: (0, i))),
+        [(passages, far), (adapter, far), queries],
+        scratch=[
+            pltpu.VMEM((slab_rows, din), BF16),
+            pltpu.VMEM((din, width), BF16),
+            pltpu.VMEM((2, din // 2, slab_rows), BF16),
+            pltpu.VMEM((slab_rows, width), F32),
+            dma((2, parts)),
+            dma((2, parts)),
         ],
-        grid=(parts,),
-    )
+        limit=28,
+    )
+    pa_other = to_partner(pa)
     got = to_partner(given)
     chip_queries = jnp.concatenate([kept_queries, to_partner(given_queries)], axis=0)
 
@@ -285,16 +336,18 @@
     line = [lax.ppermute(x, ALL, shift(0, hops)) for x, hops in zip(loads, HOPS)]
     line = jnp.concatenate([loads[-1], *line], axis=0)
 
-    far = pl.BlockSpec(memory_space=pltpu.HBM)
+    block = (kept.shape[0] // SIDE, width)
     *sent, own = kernel_call(
         grad_kernel,
-        [((kept.shape[0] // SIDE, width), BF16)] * SIDE,
+        [(block, BF16, far)] * len(HOPS) + [(block, BF16)],
         jnp.stack([core, stops[0]]),
         [(kept, far), (got, far), dpa, dpa_got],
         scratch=[
-            pltpu.VMEM((SIDE, kept.shape[0] // SIDE, 2 * slab_rows), BF16),
+            pltpu.VMEM((2, SIDE, block[0], slab_rows), BF16),
             pltpu.VMEM(dpa.shape, BF16),
-            pltpu.SemaphoreType.DMA((SIDE, 2 * SIDE)),
+            pltpu.VMEM((len(HOPS), *block), BF16),
+            dma((SIDE, 2 * SIDE)),
+            dma((len(HOPS),)),
         ],
     )
     sent = [lax.ppermute(x, ALL, shift(0, hops)) for x, hops in zip(sent, HOPS)]

time: 138 us -> 140 us (1.014)
  matrix products: 13.7 us -> 6.07 us
  waiting for transfers between devices: 48.3 us -> 55.5 us
    all_to_all x2, waiting for transfers between devices: 22.4 us -> 30.8 us  [exchanged(): return lax.all_to_all(blocks, CHIP, split_axis=0, concat_axis=0, tiled=True)]
    dot_general x3 -> x2, matrix products: 13.7 us -> 6.07 us  [dot(): lax.dot_general(left, right, (dims, ((), ())), preferred_element_type=F32)]
    ppermute x3, waiting for transfers between devices: 20.3 us -> 17.5 us  [per_device(): lax.ppermute(x, ALL, shift(0, hops))]
    ppermute x3, starting transfers between devices: 2.53 us -> 4.75 us  [per_device(): lax.ppermute(x, ALL, shift(0, hops))]
    ppermute x3, waiting for transfers between devices: 4.66 us -> 6.23 us  [per_device(): sent = [lax.ppermute(x, ALL, shift(1, hops)) for x, hops in zip(sent, HOPS)]]
  transfers between devices with their start and end apart: 19 -> 19, of which waited for: 8 -> 7; matrix products, arithmetic and copies ran while one was open for 6% -> 6% of each run, Pallas kernels for 16% -> 10%
where the time goes in v1:
time: 140 us; the launch traced here: 138 us
  waiting for transfers between devices  55.5 us (40%)
  starting transfers between devices  32.4 us (23%)
  Pallas kernels  24 us (17%)
  blocking collectives  15.1 us (11%)
  matrix products  6.07 us (4%)
  local copies, waits for them, and re-layouts  3.26 us (2%)
    all_to_all x2, waiting for transfers between devices, exchanged(): return lax.all_to_all(blocks, CHIP, split_axis=0, concat_axis=0, tiled=True)  30.8 us
    pallas_call x5, Pallas kernels, kernel_call(): pl.pallas_call(body, grid_spec=pltpu.PrefetchScalarGridSpec(num_scalar_pr...  24 us
    ppermute x3, waiting for transfers between devices, per_device(): lax.ppermute(x, ALL, shift(0, hops))  17.5 us
    all_to_all x2, starting transfers between devices, exchanged(): return lax.all_to_all(blocks, CHIP, split_axis=0, concat_axis=0, tiled=True)  16.4 us
    all_to_all x1, blocking collectives, exchanged(): return lax.all_to_all(blocks, CHIP, split_axis=0, concat_axis=0, tiled=True)  15.1 us
    ppermute x3, waiting for transfers between devices, per_device(): sent = [lax.ppermute(x, ALL, shift(1, hops)) for x, hops in zip(sent, HOPS)]  6.23 us
    dot_general x2, matrix products, dot(): lax.dot_general(left, right, (dims, ((), ())), preferred_element_type=F32)  6.07 us
    ppermute x3, starting transfers between devices, per_device(): lax.ppermute(x, ALL, shift(0, hops))  4.75 us
  transfers between devices with their start and end apart: 19, of which 7 were waited for; matrix products, arithmetic and copies ran while one was open for 6% of the time, Pallas kernels for 10%

profile of v1, /device:TPU:0, one launch (start us, length us, event | category | flops | bytes accessed | tf_op | source)
XLA Modules:
  0.0 138.2 jit_solution(126830844829492148)
XLA Ops:
  1.5 8.5 %shard_map.67 = (bf16[512,768]{1,0:T(8,128)(2,1)S(1)}, bf16[2048,512]{1,0:T(8,128)(2,1)}, bf16[2048,512]{1,0:T(8,128)(2,1)}, bf16[8,2048]{1,0:T(8,128)(2,1)S(1)}, bf16[8,2048]{1,0:T(8,128)(2,1)S(1)}) custom-call(s32[1]{0:T(128)} %bitcast.1.core_ref, bf16[512,4096]{1,0:T(8,128)(2,1)} %passages_ref.1, bf16[4096,768]{1,0:T(8,128)(2,1)} %adapter_ref.1, ...), custom_call_target="tpu_custom_call" | custom-call | tf_op jit(solution)/shard_map/pallas_call | solution.py:73
  11.0 1.0 broadcast_in_dim.4
  12.0 11.5 %all-to-all-start = ((bf16[64,8,768]{2,1,0:T(8,128)(2,1)}), bf16[64,8,768]{2,1,0:T(8,128)(2,1)S(1)}, u32[]{:S(2)}, u32[]{:S(2)}) async-start(bf16[64,8,768]{2,1,0:T(8,128)(2,1)} %broadcast_in_dim.4), calls=%async_computation | async-start | bytes 1572864 | tf_op jit(solution)/shard_map/all_to_all | solution.py:32
  24.2 15.9 %all-to-all-done = bf16[64,8,768]{2,1,0:T(8,128)(2,1)S(1)} async-done(((bf16[64,8,768]{2,1,0:T(8,128)(2,1)}), bf16[64,8,768]{2,1,0:T(8,128)(2,1)S(1)}, u32[]{:S(2)}, u32[]{:S(2)}) %all-to-all-start) | async-done | bytes 786464 | tf_op jit(solution)/shard_map/all_to_all | solution.py:32
  40.1 2.0 %shard_map.68 = (f32[1024,512]{1,0:T(8,128)S(1)}, f32[8,128]{1,0:T(8,128)S(1)}) custom-call(s32[2]{0:T(128)S(1)} %pad_add_fusion.1.here_ref, bf16[512,768]{1,0:T(8,128)(2,1)S(1)} %bitcast.48, bf16[512,768]{1,0:T(8,128)(2,1)S(1)} %get-tuple-element.23.own_ref, bf16[512,768]{1,0:T(8,128)(2,1)S(1)} %collective-permute-done.1.other_ref, ...), custom_call_target="tpu_custom_call" | custom-call | tf_op jit(solution)/shard_map/pallas_call | solution.py:73
  42.2 15.1 %all_to_all.15.packet_ref = f32[64,8,128]{2,1,0:T(8,128)S(1)} all-to-all(f32[64,8,128]{2,1,0:T(8,128)S(1)} %broadcast_in_dim.5), channel_id=1, replica_groups=mesh['row'=4,'col_0'=4,'col_1'=4,'col_2'=2] {'row','col_0','col_1'}, dimensions={0} | all-to-all | bytes 524288 | tf_op jit(solution)/shard_map/all_to_all | solution.py:32
  57.3 3.7 %shard_map.69 = (bf16[1024,768]{1,0:T(8,128)(2,1)}, bf16[512,768]{1,0:T(8,128)(2,1)}, f32[4,128]{1,0:T(4,128)S(1)}) custom-call(s32[2]{0:T(128)S(1)} %pad_add_fusion.1.here_ref, f32[1024,512]{1,0:T(8,128)S(1)} %get-tuple-element.24.scores_ref, f32[64,8,128]{2,1,0:T(8,128)S(1)} %all_to_all.15.packet_ref, s32[1,512]{1,0:T(1,128)S(1)} %reshape.49.wanted_ref, ...), custom_call_target="tpu_custom_call" | custom-call | tf_op jit(solution)/shard_map/pallas_call | solution.py:73
  60.9 4.9 %all-to-all-start.2 = ((bf16[64,8,768]{2,1,0:T(8,128)(2,1)}), bf16[64,8,768]{2,1,0:T(8,128)(2,1)S(1)}, u32[]{:S(2)}, u32[]{:S(2)}) async-start(bf16[64,8,768]{2,1,0:T(8,128)(2,1)} %bitcast.6), calls=%async_computation.2 | async-start | bytes 1572864 | tf_op jit(solution)/shard_map/all_to_all | solution.py:32
  67.7 14.9 %all-to-all-done.2 = bf16[64,8,768]{2,1,0:T(8,128)(2,1)S(1)} async-done(((bf16[64,8,768]{2,1,0:T(8,128)(2,1)}), bf16[64,8,768]{2,1,0:T(8,128)(2,1)S(1)}, u32[]{:S(2)}, u32[]{:S(2)}) %all-to-all-start.2) | async-done | bytes 786464 | tf_op jit(solution)/shard_map/all_to_all | solution.py:32
  82.8 8.6 %shard_map.70 = (bf16[512,768]{1,0:T(8,128)(2,1)}, bf16[512,768]{1,0:T(8,128)(2,1)}, bf16[512,768]{1,0:T(8,128)(2,1)}, bf16[512,768]{1,0:T(8,128)(2,1)S(1)}) custom-call(s32[2]{0:T(128)S(1)} %pad_add_fusion.where_ref, bf16[2048,512]{1,0:T(8,128)(2,1)} %get-tuple-element.21.kept_ref, bf16[2048,512]{1,0:T(8,128)(2,1)} %collective-permute-done.got_ref, ...), custom_call_target="tpu_custom_call" | custom-call | tf_op jit(solution)/shard_map/pallas_call | solution.py:73
  93.1 2.3 %collective-permute-start.5 = (bf16[512,768]{1,0:T(8,128)(2,1)}, bf16[512,768]{1,0:T(8,128)(2,1)S(1)}, u32[]{:S(2)}, u32[]{:S(2)}) collective-permute-start(bf16[512,768]{1,0:T(8,128)(2,1)} %get-tuple-element.30), channel_id=1, source_target_pairs={{0,96},{1,25},{2,98},{3,27},{4,100},{5,29},{6,102},{7,31},{8,104},... | collective-permute-start | bytes 2359304 | tf_op jit(solution)/shard_map/ppermute | solution.py:353
  95.4 1.0 collective-permute-start.10
  96.4 1.1 collective-permute-start.9
  97.5 14.7 %collective-permute-done.10 = bf16[16,1280]{1,0:T(8,128)(2,1)S(1)} collective-permute-done((bf16[16,1280]{1,0:T(8,128)(2,1)S(1)}, bf16[16,1280]{1,0:T(8,128)(2,1)S(1)}, u32[]{:S(2)}, u32[]{:S(2)}) %collective-permute-start.10) | collective-permute-done | bytes 40992 | tf_op jit(solution)/shard_map/ppermute | solution.py:336
  112.2 2.6 %collective-permute-start.8 = (bf16[16,1280]{1,0:T(8,128)(2,1)S(1)}, bf16[16,1280]{1,0:T(8,128)(2,1)S(1)}, u32[]{:S(2)}, u32[]{:S(2)}) collective-permute-start(bf16[16,1280]{1,0:T(8,128)(2,1)S(1)} %get-tuple-element.50), channel_id=1, source_target_pairs={{0,64},{1,17},{2,66},{3,19},{4,68},{5,21},{6,70},{7,23},{8,72},{9,... | collective-permute-start | bytes 122888 | tf_op jit(solution)/shard_map/ppermute | solution.py:336
  114.8 2.8 %collective-permute-done.8 = bf16[16,1280]{1,0:T(8,128)(2,1)S(1)} collective-permute-done((bf16[16,1280]{1,0:T(8,128)(2,1)S(1)}, bf16[16,1280]{1,0:T(8,128)(2,1)S(1)}, u32[]{:S(2)}, u32[]{:S(2)}) %collective-permute-start.8) | collective-permute-done | bytes 40992 | tf_op jit(solution)/shard_map/ppermute | solution.py:336
  117.7 1.3 shard_map.71
  119.9 1.1 collective-permute-start.12
  121.0 1.3 collective-permute-start.11
  122.9 1.9 %collective-permute-done.13 = bf16[128,768]{1,0:T(8,128)(2,1)S(1)} collective-permute-done((bf16[128,768]{1,0:T(8,128)(2,1)}, bf16[128,768]{1,0:T(8,128)(2,1)S(1)}, u32[]{:S(2)}, u32[]{:S(2)}) %collective-permute-start.13) | collective-permute-done | bytes 196640 | tf_op jit(solution)/shard_map/ppermute | solution.py:360
  124.8 4.3 %collective-permute-done.12 = bf16[128,768]{1,0:T(8,128)(2,1)S(1)} collective-permute-done((bf16[128,768]{1,0:T(8,128)(2,1)}, bf16[128,768]{1,0:T(8,128)(2,1)S(1)}, u32[]{:S(2)}, u32[]{:S(2)}) %collective-permute-start.12) | collective-permute-done | bytes 196640 | tf_op jit(solution)/shard_map/ppermute | solution.py:360
  129.3 1.4 collective-permute-start.16
  131.4 1.0 collective-permute-start.14
  132.4 5.1 %convolution_convert_fusion = bf16[8,4096]{1,0:T(8,128)(2,1)} fusion(bf16[8,768]{1,0:T(8,128)(2,1)S(1)} %reduce_sum.12, bf16[4096,768]{1,0:T(8,128)(2,1)} %adapter_ref.1), kind=kOutput, calls=%fused_computation | convolution fusion | flops 50364416 | bytes 6369280 | tf_op jit(solution)/shard_map/dot_general | solution.py:24
  (49 shorter events, 9.4 us)
Async XLA Ops:
  0.6 0.8 copy-start
  1.5 8.6 %copy-start.1 = (bf16[4096,768]{1,0:T(8,128)(2,1)S(1)}, bf16[4096,768]{1,0:T(8,128)(2,1)}, u32[]{:S(2)}) copy-start(bf16[4096,768]{1,0:T(8,128)(2,1)} %adapter_ref.1) | copy-start | bytes 18874372
  10.0 13.8 %copy-start.2 = (s32[1024]{0:T(1024)S(1)}, s32[1024]{0:T(1024)}, u32[]{:S(2)}) copy-start(s32[1024]{0:T(1024)} %param.7) | copy-start | bytes 12292
  10.0 30.2 %collective-permute-start.1 = (bf16[512,768]{1,0:T(8,128)(2,1)S(1)}, bf16[512,768]{1,0:T(8,128)(2,1)S(1)}, u32[]{:S(2)}, u32[]{:S(2)}) collective-permute-start(bf16[512,768]{1,0:T(8,128)(2,1)S(1)} %get-tuple-element.23.own_ref), channel_id=1, source_target_pairs={{0,1},{1,0},{2,3},{3,2},{4,5},{5,4},{6,7},{7,6},{8,9},{9,8},{10,11... | collective-permute-start | bytes 2359304 | tf_op jit(solution)/shard_map/ppermute | solution.py:28
  12.0 28.2 %all-to-all-start = ((bf16[64,8,768]{2,1,0:T(8,128)(2,1)}), bf16[64,8,768]{2,1,0:T(8,128)(2,1)S(1)}, u32[]{:S(2)}, u32[]{:S(2)}) async-start(bf16[64,8,768]{2,1,0:T(8,128)(2,1)} %broadcast_in_dim.4), calls=%async_computation | async-start | bytes 1572864 | tf_op jit(solution)/shard_map/all_to_all | solution.py:32
  23.5 59.3 %collective-permute-start = (bf16[2048,512]{1,0:T(8,128)(2,1)}, bf16[2048,512]{1,0:T(8,128)(2,1)}, u32[]{:S(2)}, u32[]{:S(2)}) collective-permute-start(bf16[2048,512]{1,0:T(8,128)(2,1)} %get-tuple-element.22), channel_id=1, source_target_pairs={{0,1},{1,0},{2,3},{3,2},{4,5},{5,4},{6,7},{7,6},{8,9},{9,8},{10,11... | collective-permute-start | bytes 6291464 | tf_op jit(solution)/shard_map/ppermute | solution.py:28
  60.9 21.8 %collective-permute-start.2 = (bf16[1024,768]{1,0:T(8,128)(2,1)}, bf16[1024,768]{1,0:T(8,128)(2,1)S(1)}, u32[]{:S(2)}, u32[]{:S(2)}) collective-permute-start(bf16[1024,768]{1,0:T(8,128)(2,1)} %get-tuple-element.26.mine_ref), channel_id=1, source_target_pairs={{0,1},{1,0},{2,3},{3,2},{4,5},{5,4},{6,7},{7,6},{8,9},{9,8},{10,11... | collective-permute-start | bytes 4718600 | tf_op jit(solution)/shard_map/ppermute | solution.py:28
  60.9 21.6 %all-to-all-start.2 = ((bf16[64,8,768]{2,1,0:T(8,128)(2,1)}), bf16[64,8,768]{2,1,0:T(8,128)(2,1)S(1)}, u32[]{:S(2)}, u32[]{:S(2)}) async-start(bf16[64,8,768]{2,1,0:T(8,128)(2,1)} %bitcast.6), calls=%async_computation.2 | async-start | bytes 1572864 | tf_op jit(solution)/shard_map/all_to_all | solution.py:32
  65.9 1.3 collective-permute-start.6
  82.7 12.7 %collective-permute-start.7 = (bf16[8,768]{1,0:T(8,128)(2,1)S(1)}, bf16[8,768]{1,0:T(8,128)(2,1)S(1)}, u32[]{:S(2)}, u32[]{:S(2)}) collective-permute-start(bf16[8,768]{1,0:T(8,128)(2,1)S(1)} %reduce_sum.12), channel_id=1, source_target_pairs={{0,1},{1,0},{2,3},{3,2},{4,5},{5,4},{6,7},{7,6},{8,9},{9,8},{10,11... | collective-permute-start | bytes 36872 | tf_op jit(solution)/shard_map/ppermute | solution.py:28
  91.4 26.3 %collective-permute-start.3 = (bf16[512,768]{1,0:T(8,128)(2,1)}, bf16[512,768]{1,0:T(8,128)(2,1)S(1)}, u32[]{:S(2)}, u32[]{:S(2)}) collective-permute-start(bf16[512,768]{1,0:T(8,128)(2,1)} %get-tuple-element.28), channel_id=1, source_target_pairs={{0,64},{1,17},{2,66},{3,19},{4,68},{5,21},{6,70},{7,23},{8,72},{9,... | collective-permute-start | bytes 2359304 | tf_op jit(solution)/shard_map/ppermute | solution.py:353
  92.1 25.6 %collective-permute-start.4 = (bf16[512,768]{1,0:T(8,128)(2,1)}, bf16[512,768]{1,0:T(8,128)(2,1)S(1)}, u32[]{:S(2)}, u32[]{:S(2)}) collective-permute-start(bf16[512,768]{1,0:T(8,128)(2,1)} %get-tuple-element.29), channel_id=1, source_target_pairs={{0,32},{1,9},{2,34},{3,11},{4,36},{5,13},{6,38},{7,15},{8,40},{9,1... | collective-permute-start | bytes 2359304 | tf_op jit(solution)/shard_map/ppermute | solution.py:353
  93.1 24.6 %collective-permute-start.5 = (bf16[512,768]{1,0:T(8,128)(2,1)}, bf16[512,768]{1,0:T(8,128)(2,1)S(1)}, u32[]{:S(2)}, u32[]{:S(2)}) collective-permute-start(bf16[512,768]{1,0:T(8,128)(2,1)} %get-tuple-element.30), channel_id=1, source_target_pairs={{0,96},{1,25},{2,98},{3,27},{4,100},{5,29},{6,102},{7,31},{8,104},... | collective-permute-start | bytes 2359304 | tf_op jit(solution)/shard_map/ppermute | solution.py:353
  95.4 16.8 %collective-permute-start.10 = (bf16[16,1280]{1,0:T(8,128)(2,1)S(1)}, bf16[16,1280]{1,0:T(8,128)(2,1)S(1)}, u32[]{:S(2)}, u32[]{:S(2)}) collective-permute-start(bf16[16,1280]{1,0:T(8,128)(2,1)S(1)} %get-tuple-element.52), channel_id=1, source_target_pairs={{0,96},{1,25},{2,98},{3,27},{4,100},{5,29},{6,102},{7,31},{8,104},... | collective-permute-start | bytes 122888 | tf_op jit(solution)/shard_map/ppermute | solution.py:336
  96.4 18.4 %collective-permute-start.9 = (bf16[16,1280]{1,0:T(8,128)(2,1)S(1)}, bf16[16,1280]{1,0:T(8,128)(2,1)S(1)}, u32[]{:S(2)}, u32[]{:S(2)}) collective-permute-start(bf16[16,1280]{1,0:T(8,128)(2,1)S(1)} %get-tuple-element.51), channel_id=1, source_target_pairs={{0,32},{1,9},{2,34},{3,11},{4,36},{5,13},{6,38},{7,15},{8,40},{9,1... | collective-permute-start | bytes 122888 | tf_op jit(solution)/shard_map/ppermute | solution.py:336
  112.2 5.5 %collective-permute-start.8 = (bf16[16,1280]{1,0:T(8,128)(2,1)S(1)}, bf16[16,1280]{1,0:T(8,128)(2,1)S(1)}, u32[]{:S(2)}, u32[]{:S(2)}) collective-permute-start(bf16[16,1280]{1,0:T(8,128)(2,1)S(1)} %get-tuple-element.50), channel_id=1, source_target_pairs={{0,64},{1,17},{2,66},{3,19},{4,68},{5,21},{6,70},{7,23},{8,72},{9,... | collective-permute-start | bytes 122888 | tf_op jit(solution)/shard_map/ppermute | solution.py:336
  119.0 5.9 %collective-permute-start.13 = (bf16[128,768]{1,0:T(8,128)(2,1)}, bf16[128,768]{1,0:T(8,128)(2,1)S(1)}, u32[]{:S(2)}, u32[]{:S(2)}) collective-permute-start(bf16[128,768]{1,0:T(8,128)(2,1)} %get-tuple-element.37), channel_id=1, source_target_pairs={{0,24},{1,97},{2,26},{3,99},{4,28},{5,101},{6,30},{7,103},{8,0},{9... | collective-permute-start | bytes 589832 | tf_op jit(solution)/shard_map/ppermute | solution.py:360
  119.9 9.2 %collective-permute-start.12 = (bf16[128,768]{1,0:T(8,128)(2,1)}, bf16[128,768]{1,0:T(8,128)(2,1)S(1)}, u32[]{:S(2)}, u32[]{:S(2)}) collective-permute-start(bf16[128,768]{1,0:T(8,128)(2,1)} %get-tuple-element.36), channel_id=1, source_target_pairs={{0,8},{1,33},{2,10},{3,35},{4,12},{5,37},{6,14},{7,39},{8,16},{9,4... | collective-permute-start | bytes 589832 | tf_op jit(solution)/shard_map/ppermute | solution.py:360
  121.0 8.1 %collective-permute-start.11 = (bf16[128,768]{1,0:T(8,128)(2,1)S(1)}, bf16[128,768]{1,0:T(8,128)(2,1)S(1)}, u32[]{:S(2)}, u32[]{:S(2)}) collective-permute-start(bf16[128,768]{1,0:T(8,128)(2,1)S(1)} %get-tuple-element.35), channel_id=1, source_target_pairs={{0,16},{1,65},{2,18},{3,67},{4,20},{5,69},{6,22},{7,71},{8,24},{9,... | collective-permute-start | bytes 589832 | tf_op jit(solution)/shard_map/ppermute | solution.py:360
  129.3 8.3 %collective-permute-start.16 = (bf16[32,768]{1,0:T(8,128)(2,1)S(1)}, bf16[32,768]{1,0:T(8,128)(2,1)S(1)}, u32[]{:S(2)}, u32[]{:S(2)}) collective-permute-start(bf16[32,768]{1,0:T(8,128)(2,1)S(1)} %get-tuple-element.44), channel_id=1, source_target_pairs={{0,6},{1,7},{2,0},{3,1},{4,2},{5,3},{6,4},{7,5},{8,14},{9,15},{10,... | collective-permute-start | bytes 147464 | tf_op jit(solution)/shard_map/ppermute | solution.py:56
  130.6 6.9 %collective-permute-start.15 = (bf16[32,768]{1,0:T(8,128)(2,1)S(1)}, bf16[32,768]{1,0:T(8,128)(2,1)S(1)}, u32[]{:S(2)}, u32[]{:S(2)}) collective-permute-start(bf16[32,768]{1,0:T(8,128)(2,1)S(1)} %get-tuple-element.45), channel_id=1, source_target_pairs={{0,2},{1,3},{2,4},{3,5},{4,6},{5,7},{6,0},{7,1},{8,10},{9,11},{10,... | collective-permute-start | bytes 147464 | tf_op jit(solution)/shard_map/ppermute | solution.py:56
  131.4 6.2 %collective-permute-start.14 = (bf16[32,768]{1,0:T(8,128)(2,1)S(1)}, bf16[32,768]{1,0:T(8,128)(2,1)S(1)}, u32[]{:S(2)}, u32[]{:S(2)}) collective-permute-start(bf16[32,768]{1,0:T(8,128)(2,1)S(1)} %get-tuple-element.43), channel_id=1, source_target_pairs={{0,4},{1,5},{2,6},{3,7},{4,0},{5,1},{6,2},{7,3},{8,12},{9,13},{10,... | collective-permute-start | bytes 147464 | tf_op jit(solution)/shard_map/ppermute | solution.py:56

commit v2 on v1

--- a/solution.py
+++ b/solution.py
@@ -15,7 +15,7 @@
 SIDE = 4
 SWAP = [(0, 1), (1, 0)]
 HOPS = (2, 1, 3)
-ROUTES = ((0, 1, 2), (1, 0, 2))
+LINE = (0, 1)
 F32 = jnp.float32
 BF16 = jnp.bfloat16
 
@@ -36,26 +36,21 @@
     return ((place[0] * SIDE + place[1]) * SIDE + place[2]) * 2 + core
 
 
-def shift(stage, hops):
+def shift(hops):
     pairs = []
     for *place, core in itertools.product(range(SIDE), range(SIDE), range(SIDE), range(2)):
         there = list(place)
-        axis = ROUTES[core][stage]
+        axis = LINE[core]
         there[axis] = (there[axis] + hops) % SIDE
         pairs.append((number(place, core), number(there, core)))
     return pairs
 
 
-def block(x, which, dim):
-    size = x.shape[dim] // SIDE
-    return lax.dynamic_slice_in_dim(x, which % SIDE * size, size, dim)
-
-
-def dealt(x, place, stage, dim):
-    sent = [
-        lax.ppermute(block(x, place + hops, dim), ALL, shift(stage, hops)) for hops in HOPS
-    ]
-    return [block(x, place, dim), *sent]
+def planes():
+    side = range(SIDE)
+    return [
+        [number((z, x, y), 0) for x in side for y in side] for z in side
+    ] + [[number((z, x, y), 1) for z in side for y in side] for x in side]
 
 
 def kernel_call(body, outs, scalars, ins, *, grid=(), scratch=(), limit=16):
@@ -194,54 +189,90 @@
     dqa_ref[...] = dqa.astype(BF16)
 
 
-def grad_kernel(where_ref, kept_ref, got_ref, mine_ref, theirs_ref, *refs):
-    outs, (left_ref, sum_ref, sent_ref, in_sems, out_sems) = refs[:SIDE], refs[SIDE:]
+def pieces(where_ref, ref, to_ref, away, sems):
+    piece = ref.shape[0] // (SIDE * SIDE)
+    place = lax.rem(where_ref[1] + away, SIDE)
+    copies = []
+    for j in range(SIDE):
+        index = jnp.where(where_ref[0] == 0, place * SIDE + j, j * SIDE + place)
+        rows = pl.ds(pl.multiple_of(index * piece, piece), piece)
+        to = to_ref.at[j * piece : (j + 1) * piece]
+        copies.append(pltpu.make_async_copy(ref.at[rows], to, sems.at[j]))
+    return copies
+
+
+def grad_first_kernel(
+    where_ref, kept_ref, got_ref, mine_ref, theirs_ref, out_ref, sum_ref,
+    left_ref, mine_held, sems, dpa_sems,
+):
     slab = kept_ref.shape[1]
-    piece = kept_ref.shape[0] // (SIDE * SIDE)
-    low = where_ref[0] == 0
-    arrivals, leaving = [], []
-    for k, hops in enumerate((*HOPS, 0)):
-        place = lax.rem(where_ref[1] + hops, SIDE)
-        arrivals.append([])
-        for j in range(SIDE):
-            index = jnp.where(low, place * SIDE + j, j * SIDE + place)
-            rows = pl.ds(pl.multiple_of(index * piece, piece), piece)
-            for which, ref in enumerate((kept_ref, got_ref)):
-                to = left_ref.at[which, k, j * piece : (j + 1) * piece]
-                copy = pltpu.make_async_copy(ref.at[rows], to, in_sems.at[k, 2 * j + which])
-                arrivals[-1].append(copy)
-    for copy in itertools.chain(*arrivals):
-        copy.start()
+    batches = []
+    for k, ref in enumerate((kept_ref, got_ref)):
+        ours = slice(k * slab, (k + 1) * slab)
+        batches.append(
+            [
+                pltpu.make_async_copy(mine_ref.at[ours], mine_held.at[ours], dpa_sems.at[k]),
+                *pieces(where_ref, ref, left_ref.at[k], HOPS[0], sems.at[k]),
+            ]
+        )
+        for copy in batches[-1]:
+            copy.start()
+    block = None
     for k in range(2):
         ours, yours = slice(k * slab, (k + 1) * slab), slice((1 - k) * slab, (2 - k) * slab)
-        both = mine_ref[ours, :].astype(F32) + theirs_ref[yours, :].astype(F32)
-        sum_ref[ours, :] = both.astype(BF16)
-    for k, out in enumerate(outs):
-        for copy in arrivals[k]:
+        for copy in batches[k]:
             copy.wait()
-        block = dot(left_ref[0, k], sum_ref[:slab, :], ((1,), (0,)))
-        block += dot(left_ref[1, k], sum_ref[slab:, :], ((1,), (0,)))
-        if k < SIDE - 1:
-            sent_ref[k] = block.astype(BF16)
-            leaving.append(pltpu.make_async_copy(sent_ref.at[k], out, out_sems.at[k]))
-            leaving[-1].start()
-        else:
-            out[...] = block.astype(BF16)
-    for copy in leaving:
-        copy.wait()
-
-
-def join_kernel(stop_ref, own_ref, far_ref, next_ref, last_ref, line_ref, *outs):
+        both = mine_held[ours, :] + theirs_ref[yours, :]
+        sum_ref[ours, :] = both
+        part = dot(left_ref[k], both, ((1,), (0,)))
+        block = part if block is None else block + part
+    out_ref[...] = block.astype(BF16)
+
+
+def grad_second_kernel(where_ref, kept_ref, got_ref, sum_ref, *refs):
+    *outs, left_ref, sems = refs
+    slab = kept_ref.shape[1]
+    copies = []
+    for n, away in enumerate((*HOPS[1:], 0)):
+        copies.append(
+            [
+                *pieces(where_ref, kept_ref, left_ref.at[0, n], away, sems.at[0, n]),
+                *pieces(where_ref, got_ref, left_ref.at[1, n], away, sems.at[1, n]),
+            ]
+        )
+        for copy in copies[-1]:
+            copy.start()
+    for n, out in enumerate(outs):
+        for copy in copies[n]:
+            copy.wait()
+        block = dot(left_ref[0, n], sum_ref[:slab, :], ((1,), (0,)))
+        block += dot(left_ref[1, n], sum_ref[slab:, :], ((1,), (0,)))
+        out[...] = block.astype(BF16)
+
+
+def query_grad_kernel(none_ref, adapter_ref, dqa_ref, out_ref, held_ref, made_ref, sems, out_sem):
+    parts = sems.shape[0]
+    depth = adapter_ref.shape[0] // parts
+    copies = []
+    for k in range(parts):
+        rows = slice(k * depth, (k + 1) * depth)
+        copies.append(pltpu.make_async_copy(adapter_ref.at[rows], held_ref.at[rows], sems.at[k]))
+        copies[-1].start()
+    for k in range(parts):
+        rows = slice(k * depth, (k + 1) * depth)
+        copies[k].wait()
+        made_ref[:, rows] = dot(dqa_ref[...], held_ref[rows, :], ((1,), (1,))).astype(BF16)
+    copy = pltpu.make_async_copy(made_ref, out_ref, out_sem)
+    copy.start()
+    copy.wait()
+
+
+def join_kernel(none_ref, own_ref, far_ref, next_ref, last_ref, line_ref, out_ref):
     size = own_ref.shape[0]
-    piece = outs[0].shape[0]
-    for out, hops in zip(outs, (*HOPS, 0)):
-        place = lax.rem(stop_ref[0] + hops, SIDE)
-        rows = pl.ds(pl.multiple_of(place * piece, piece), piece)
-        lanes = pl.ds(pl.multiple_of(place * piece, piece), piece)
-        part = dot(line_ref[:, lanes], line_ref[:, size:], ((0,), (0,)))
-        for ref in (own_ref, far_ref, next_ref, last_ref):
-            part += ref[rows, :].astype(F32)
-        out[...] = part.astype(BF16)
+    part = dot(line_ref[:, :size], line_ref[:, size:], ((0,), (0,)))
+    for ref in (own_ref, far_ref, next_ref, last_ref):
+        part += ref[...].astype(F32)
+    out_ref[...] = part.astype(BF16)
 
 
 def line_block(x, which, core):
@@ -249,14 +280,6 @@
     low = lax.dynamic_index_in_dim(cut, which % SIDE, 1, keepdims=False)
     high = lax.dynamic_index_in_dim(cut, which % SIDE, 2, keepdims=False)
     return jnp.where(core == 0, low, high).reshape(x.shape[0], -1)
-
-
-def total(parts):
-    first, *others = parts
-    out = first.astype(F32)
-    for part in others:
-        out = out + part.astype(F32)
-    return out
 
 
 def per_device(queries, passages, adapter, positives):
@@ -269,9 +292,7 @@
     chip, core = lax.axis_index(CHIP), lax.axis_index(CORE)
     here = chip * 2 + core
     place = [lax.axis_index(axis) for axis in CHIP]
-    stops = [
-        jnp.where(core == 0, place[ROUTES[0][k]], place[ROUTES[1][k]]) for k in range(3)
-    ]
+    stop = jnp.where(core == 0, place[LINE[0]], place[LINE[1]])
 
     parts = 4
     far = pl.BlockSpec(memory_space=pltpu.HBM)
@@ -302,7 +323,7 @@
     )
     pa_other = to_partner(pa)
     got = to_partner(given)
-    chip_queries = jnp.concatenate([kept_queries, to_partner(given_queries)], axis=0)
+    got_queries = to_partner(given_queries)
 
     starts = jnp.stack([here * slab_rows, (here ^ 1) * slab_rows])
     wanted = lax.dynamic_index_in_dim(
@@ -323,45 +344,68 @@
         starts,
         [scores, packet, wanted, qa, pa, pa_other],
     )
-    losses = lax.dynamic_slice_in_dim(losses.reshape(half), chip * own_rows, own_rows, 0)
     dpa_got = to_partner(dpa)
     dqa = dqa.reshape(chips, own_rows, width)
     dqa_own = exchanged(dqa)
     dqa_own = jnp.sum(dqa_own.astype(F32), axis=0).astype(BF16)
-    chip_dqa = jnp.concatenate([dqa_own, to_partner(dqa_own)], axis=0)
-    loads = [
-        jnp.concatenate([line_block(chip_queries, stops[0] + hops, core), chip_dqa], axis=1)
-        for hops in (*HOPS, 0)
-    ]
-    line = [lax.ppermute(x, ALL, shift(0, hops)) for x, hops in zip(loads, HOPS)]
+    dqa_own, losses, kept_queries, got_queries = lax.optimization_barrier(
+        (dqa_own, losses, kept_queries, got_queries)
+    )
+    got_dqa = to_partner(dqa_own)
+    losses = lax.dynamic_slice_in_dim(losses.reshape(half), chip * own_rows, own_rows, 0)
+    chip_queries = jnp.concatenate([kept_queries, got_queries], axis=0)
+    blocks = [line_block(chip_queries, stop + hops, core) for hops in (*HOPS, 0)]
+    got_dqa, losses, blocks = lax.optimization_barrier((got_dqa, losses, blocks))
+    chip_dqa = jnp.concatenate([dqa_own, got_dqa], axis=0)
+    loads = [jnp.concatenate([x, chip_dqa], axis=1) for x in blocks]
+    line = [lax.ppermute(x, ALL, shift(hops)) for x, hops in zip(loads, HOPS)]
     line = jnp.concatenate([loads[-1], *line], axis=0)
 
-    block = (kept.shape[0] // SIDE, width)
-    *sent, own = kernel_call(
-        grad_kernel,
-        [(block, BF16, far)] * len(HOPS) + [(block, BF16)],
-        jnp.stack([core, stops[0]]),
-        [(kept, far), (got, far), dpa, dpa_got],
+    block = (din // 2 // SIDE, width)
+
+    where = jnp.stack([core, stop])
+    first, dpa_sum = kernel_call(
+        grad_first_kernel,
+        [(block, BF16), (dpa.shape, BF16)],
+        where,
+        [(kept, far), (got, far), (dpa, far), dpa_got],
         scratch=[
-            pltpu.VMEM((2, SIDE, block[0], slab_rows), BF16),
+            pltpu.VMEM((2, block[0], slab_rows), BF16),
             pltpu.VMEM(dpa.shape, BF16),
-            pltpu.VMEM((len(HOPS), *block), BF16),
-            dma((SIDE, 2 * SIDE)),
-            dma((len(HOPS),)),
+            dma((2, SIDE)),
+            dma((2,)),
         ],
     )
-    sent = [lax.ppermute(x, ALL, shift(0, hops)) for x, hops in zip(sent, HOPS)]
-    *sent, own = kernel_call(
-        join_kernel,
-        [((own.shape[0] // SIDE, width), BF16)] * SIDE,
-        stops[1].reshape(1),
-        [own, *sent, line],
-    )
-    sent = [lax.ppermute(x, ALL, shift(1, hops)) for x, hops in zip(sent, HOPS)]
-    grad = total([own, *sent]).astype(BF16)
-    grad = total(dealt(grad, stops[2], 2, 0))
-
-    query_grad = dot(dqa_own, adapter, ((1,), (1,))).astype(BF16)
+    sent = [lax.ppermute(first, ALL, shift(HOPS[0]))]
+    *last, own = kernel_call(
+        grad_second_kernel,
+        [(block, BF16)] * 3,
+        where,
+        [(kept, far), (got, far), dpa_sum],
+        scratch=[pltpu.VMEM((2, 3, block[0], slab_rows), BF16), dma((2, 3, SIDE))],
+    )
+    sent += [lax.ppermute(x, ALL, shift(hops)) for x, hops in zip(last, HOPS[1:])]
+    (query_grad,) = kernel_call(
+        query_grad_kernel,
+        [((own_rows, din), BF16, far)],
+        jnp.zeros((1,), jnp.int32),
+        [(adapter, far), dqa_own],
+        scratch=[
+            pltpu.VMEM(adapter.shape, BF16),
+            pltpu.VMEM((own_rows, din), BF16),
+            dma((parts,)),
+            dma,
+        ],
+    )
+    line, query_grad = lax.optimization_barrier((line, query_grad))
+    (grad,) = kernel_call(
+        join_kernel, [(block, BF16)], jnp.zeros((1,), jnp.int32), [own, *sent, line]
+    )
+    spread = lax.all_to_all(
+        grad.reshape(SIDE * SIDE, -1, width), ALL, 0, 0, axis_index_groups=planes(), tiled=True
+    )
+    grad = jnp.sum(spread.astype(F32), axis=0)
+
     return (grad, query_grad, losses)
 
 

time: 140 us -> 139 us (level)
  the two profiles are of different devices: /device:TPU:0 before, /device:TPU:5 now
where the time goes in v2:
time: 139 us; the launch traced here: 138 us
  waiting for transfers between devices  38.2 us (27%)
  starting transfers between devices  34.3 us (25%)
  blocking collectives  31.7 us (23%)
  Pallas kernels  27.9 us (20%)
  local copies, waits for them, and re-layouts  3.22 us (2%)
    pallas_call x7, Pallas kernels, kernel_call(): pl.pallas_call(body, grid_spec=pltpu.PrefetchScalarGridSpec(num_scalar_pr...  27.9 us
    all_to_all x2, waiting for transfers between devices, exchanged(): return lax.all_to_all(blocks, CHIP, split_axis=0, concat_axis=0, tiled=True)  23.6 us
    all_to_all x2, starting transfers between devices, exchanged(): return lax.all_to_all(blocks, CHIP, split_axis=0, concat_axis=0, tiled=True)  17.5 us
    all_to_all x1, blocking collectives, per_device(): lax.all_to_all(grad.reshape(SIDE * SIDE, -1, width), ALL, 0, 0, axis_inde...  17.2 us
    ppermute x3, waiting for transfers between devices, per_device(): line = [lax.ppermute(x, ALL, shift(hops)) for x, hops in zip(loads, HOPS)]  14.6 us
    all_to_all x1, blocking collectives, exchanged(): return lax.all_to_all(blocks, CHIP, split_axis=0, concat_axis=0, tiled=True)  14.5 us
    ppermute x5, starting transfers between devices, to_partner(): return lax.ppermute(x, CORE, SWAP)  7.5 us
    ppermute x3, starting transfers between devices, per_device(): line = [lax.ppermute(x, ALL, shift(hops)) for x, hops in zip(loads, HOPS)]  4.38 us
  transfers between devices with their start and end apart: 13, of which 3 were waited for; matrix products, arithmetic and copies ran while one was open for 3% of the time, Pallas kernels for 14%

profile of v2, /device:TPU:5, one launch (start us, length us, event | category | flops | bytes accessed | tf_op | source)
XLA Modules:
  0.0 138.2 jit_solution(8913081668529458931)
XLA Ops:
  0.6 0.8 copy-done
  1.5 8.5 %shard_map.67 = (bf16[512,768]{1,0:T(8,128)(2,1)S(1)}, bf16[2048,512]{1,0:T(8,128)(2,1)}, bf16[2048,512]{1,0:T(8,128)(2,1)}, bf16[8,2048]{1,0:T(8,128)(2,1)S(1)}, bf16[8,2048]{1,0:T(8,128)(2,1)S(1)}) custom-call(s32[1]{0:T(128)} %bitcast.core_ref, bf16[512,4096]{1,0:T(8,128)(2,1)} %passages_ref.1, bf16[4096,768]{1,0:T(8,128)(2,1)} %adapter_ref.3, ...), custom_call_target="tpu_custom_call" | custom-call | tf_op jit(solution)/shard_map/pallas_call | solution.py:68
  10.0 0.8 collective-permute-start.1
  10.7 0.9 convolution_convert_fusion
  11.6 0.9 broadcast_in_dim.4
  12.6 10.9 %all-to-all-start = ((bf16[64,8,768]{2,1,0:T(8,128)(2,1)}), bf16[64,8,768]{2,1,0:T(8,128)(2,1)S(1)}, u32[]{:S(2)}, u32[]{:S(2)}) async-start(bf16[64,8,768]{2,1,0:T(8,128)(2,1)} %broadcast_in_dim.4), calls=%async_computation | async-start | bytes 1572864 | tf_op jit(solution)/shard_map/all_to_all | solution.py:32
  24.6 11.6 %all-to-all-done = bf16[64,8,768]{2,1,0:T(8,128)(2,1)S(1)} async-done(((bf16[64,8,768]{2,1,0:T(8,128)(2,1)}), bf16[64,8,768]{2,1,0:T(8,128)(2,1)S(1)}, u32[]{:S(2)}, u32[]{:S(2)}) %all-to-all-start) | async-done | bytes 786464 | tf_op jit(solution)/shard_map/all_to_all | solution.py:32
  36.2 2.0 %shard_map.68 = (f32[1024,512]{1,0:T(8,128)S(1)}, f32[8,128]{1,0:T(8,128)S(1)}) custom-call(s32[2]{0:T(128)S(1)} %pad_add_fusion.1.here_ref, bf16[512,768]{1,0:T(8,128)(2,1)S(1)} %bitcast.46, bf16[512,768]{1,0:T(8,128)(2,1)S(1)} %get-tuple-element.32.own_ref, bf16[512,768]{1,0:T(8,128)(2,1)S(1)} %collective-permute-done.1.other_ref, ...), custom_call_target="tpu_custom_call" | custom-call | tf_op jit(solution)/shard_map/pallas_call | solution.py:68
  38.2 14.5 %all_to_all.20.packet_ref = f32[64,8,128]{2,1,0:T(8,128)S(1)} all-to-all(f32[64,8,128]{2,1,0:T(8,128)S(1)} %broadcast_in_dim.5), channel_id=1, replica_groups=mesh['row'=4,'col_0'=4,'col_1'=4,'col_2'=2] {'row','col_0','col_1'}, dimensions={0} | all-to-all | bytes 524288 | tf_op jit(solution)/shard_map/all_to_all | solution.py:32
  52.7 3.6 %shard_map.69 = (bf16[1024,768]{1,0:T(8,128)(2,1)}, bf16[512,768]{1,0:T(8,128)(2,1)}, f32[4,128]{1,0:T(4,128)S(1)}) custom-call(s32[2]{0:T(128)S(1)} %pad_add_fusion.1.here_ref, f32[1024,512]{1,0:T(8,128)S(1)} %get-tuple-element.33.scores_ref, f32[64,8,128]{2,1,0:T(8,128)S(1)} %all_to_all.20.packet_ref, s32[1,512]{1,0:T(1,128)S(1)} %reshape.48.wanted_ref, ...), custom_call_target="tpu_custom_call" | custom-call | tf_op jit(solution)/shard_map/pallas_call | solution.py:68
  56.3 2.9 %collective-permute-start.2 = (bf16[1024,768]{1,0:T(8,128)(2,1)}, bf16[1024,768]{1,0:T(8,128)(2,1)S(1)}, u32[]{:S(2)}, u32[]{:S(2)}) collective-permute-start(bf16[1024,768]{1,0:T(8,128)(2,1)} %get-tuple-element.35.mine_ref), channel_id=1, source_target_pairs={{0,1},{1,0},{2,3},{3,2},{4,5},{5,4},{6,7},{7,6},{8,9},{9,8},{10,11... | collective-permute-start | bytes 4718600 | tf_op jit(solution)/shard_map/ppermute | solution.py:28
  59.3 6.6 %all-to-all-start.2 = ((bf16[64,8,768]{2,1,0:T(8,128)(2,1)}), bf16[64,8,768]{2,1,0:T(8,128)(2,1)S(1)}, u32[]{:S(2)}, u32[]{:S(2)}) async-start(bf16[64,8,768]{2,1,0:T(8,128)(2,1)} %bitcast.5), calls=%async_computation.2 | async-start | bytes 1572864 | tf_op jit(solution)/shard_map/all_to_all | solution.py:32
  66.6 12.0 %all-to-all-done.2 = bf16[64,8,768]{2,1,0:T(8,128)(2,1)S(1)} async-done(((bf16[64,8,768]{2,1,0:T(8,128)(2,1)}), bf16[64,8,768]{2,1,0:T(8,128)(2,1)S(1)}, u32[]{:S(2)}, u32[]{:S(2)}) %all-to-all-start.2) | async-done | bytes 786464 | tf_op jit(solution)/shard_map/all_to_all | solution.py:32
  78.8 2.5 %collective-permute-start.7 = (bf16[8,768]{1,0:T(8,128)(2,1)S(1)}, bf16[8,768]{1,0:T(8,128)(2,1)S(1)}, u32[]{:S(2)}, u32[]{:S(2)}) collective-permute-start(bf16[8,768]{1,0:T(8,128)(2,1)S(1)} %reduce_sum.21.dqa_ref), channel_id=1, source_target_pairs={{0,1},{1,0},{2,3},{3,2},{4,5},{5,4},{6,7},{7,6},{8,9},{9,8},{10,11... | collective-permute-start | bytes 36872 | tf_op jit(solution)/shard_map/ppermute | solution.py:28
  81.8 3.4 %shard_map.70 = (bf16[512,768]{1,0:T(8,128)(2,1)S(1)}, bf16[1024,768]{1,0:T(8,128)(2,1)S(1)}) custom-call(s32[2]{0:T(128)S(1)} %pad_add_fusion.where_ref, bf16[2048,512]{1,0:T(8,128)(2,1)} %get-tuple-element.30.kept_ref, bf16[2048,512]{1,0:T(8,128)(2,1)} %collective-permute-done.got_ref, bf16[1024,768]{1,0:T(8,128)(2,1)} %get-tuple-element.35.mine_ref, ...), custom_call_target="tpu_custom_call" | custom-call | tf_op jit(solution)/shard_map/pallas_call | solution.py:68
  85.2 5.5 %shard_map.71 = (bf16[512,768]{1,0:T(8,128)(2,1)S(1)}, bf16[512,768]{1,0:T(8,128)(2,1)S(1)}, bf16[512,768]{1,0:T(8,128)(2,1)S(1)}) custom-call(s32[2]{0:T(128)S(1)} %pad_add_fusion.where_ref, bf16[2048,512]{1,0:T(8,128)(2,1)} %get-tuple-element.30.kept_ref, bf16[2048,512]{1,0:T(8,128)(2,1)} %collective-permute-done.got_ref, ...), custom_call_target="tpu_custom_call" | custom-call | tf_op jit(solution)/shard_map/pallas_call | solution.py:68
  91.4 0.9 collective-permute-start.5
  92.3 3.4 %collective-permute-start.3 = (bf16[512,768]{1,0:T(8,128)(2,1)S(1)}, bf16[512,768]{1,0:T(8,128)(2,1)S(1)}, u32[]{:S(2)}, u32[]{:S(2)}) collective-permute-start(bf16[512,768]{1,0:T(8,128)(2,1)S(1)} %get-tuple-element.38), channel_id=1, source_target_pairs={{0,64},{1,17},{2,66},{3,19},{4,68},{5,21},{6,70},{7,23},{8,72},{9,... | collective-permute-start | bytes 2359304 | tf_op jit(solution)/shard_map/ppermute | solution.py:379
  96.5 1.5 %collective-permute-start.8 = (bf16[16,1280]{1,0:T(8,128)(2,1)S(1)}, bf16[16,1280]{1,0:T(8,128)(2,1)S(1)}, u32[]{:S(2)}, u32[]{:S(2)}) collective-permute-start(bf16[16,1280]{1,0:T(8,128)(2,1)S(1)} %get-tuple-element.65), channel_id=1, source_target_pairs={{0,64},{1,17},{2,66},{3,19},{4,68},{5,21},{6,70},{7,23},{8,72},{9,... | collective-permute-start | bytes 122888 | tf_op jit(solution)/shard_map/ppermute | solution.py:361
  98.0 14.5 %collective-permute-done.10 = bf16[16,1280]{1,0:T(8,128)(2,1)S(1)} collective-permute-done((bf16[16,1280]{1,0:T(8,128)(2,1)S(1)}, bf16[16,1280]{1,0:T(8,128)(2,1)S(1)}, u32[]{:S(2)}, u32[]{:S(2)}) %collective-permute-start.10) | collective-permute-done | bytes 40992 | tf_op jit(solution)/shard_map/ppermute | solution.py:361
  112.5 2.8 %collective-permute-start.9 = (bf16[16,1280]{1,0:T(8,128)(2,1)S(1)}, bf16[16,1280]{1,0:T(8,128)(2,1)S(1)}, u32[]{:S(2)}, u32[]{:S(2)}) collective-permute-start(bf16[16,1280]{1,0:T(8,128)(2,1)S(1)} %get-tuple-element.66), channel_id=1, source_target_pairs={{0,32},{1,9},{2,34},{3,11},{4,36},{5,13},{6,38},{7,15},{8,40},{9,1... | collective-permute-start | bytes 122888 | tf_op jit(solution)/shard_map/ppermute | solution.py:361
  115.3 4.2 %shard_map.72 = bf16[8,4096]{1,0:T(8,128)(2,1)} custom-call(s32[1]{0:T(128)} %constant.76.clone.1.none_ref, bf16[4096,768]{1,0:T(8,128)(2,1)} %adapter_ref.3, bf16[8,768]{1,0:T(8,128)(2,1)S(1)} %reduce_sum.21.dqa_ref), custom_call_target="tpu_custom_call" | custom-call | tf_op jit(solution)/shard_map/pallas_call | solution.py:68
  120.2 17.2 %all_to_all.21 = bf16[16,32,768]{2,1,0:T(8,128)(2,1)S(1)} all-to-all(bf16[16,32,768]{2,1,0:T(8,128)(2,1)S(1)} %bitcast.48), channel_id=1, replica_groups={{0,2,4,6,8,10,12,14,16,18,20,22,24,26,28,30},{32,34,36,38,40,42,44,46,4..., dimensions={0} | all-to-all | bytes 1572864 | tf_op jit(solution)/shard_map/all_to_all | solution.py:404
  137.4 0.7 convert_reduce_fusion
  (38 shorter events, 4.5 us)
Async XLA Ops:
  0.6 0.8 copy-start
  1.5 9.2 %copy-start.1 = (bf16[4096,768]{1,0:T(8,128)(2,1)S(1)}, bf16[4096,768]{1,0:T(8,128)(2,1)}, u32[]{:S(2)}) copy-start(bf16[4096,768]{1,0:T(8,128)(2,1)} %adapter_ref.3) | copy-start | bytes 18874372
  10.0 26.2 %collective-permute-start.1 = (bf16[512,768]{1,0:T(8,128)(2,1)S(1)}, bf16[512,768]{1,0:T(8,128)(2,1)S(1)}, u32[]{:S(2)}, u32[]{:S(2)}) collective-permute-start(bf16[512,768]{1,0:T(8,128)(2,1)S(1)} %get-tuple-element.32.own_ref), channel_id=1, source_target_pairs={{0,1},{1,0},{2,3},{3,2},{4,5},{5,4},{6,7},{7,6},{8,9},{9,8},{10,11... | collective-permute-start | bytes 2359304 | tf_op jit(solution)/shard_map/ppermute | solution.py:28
  11.6 12.5 %copy-start.2 = (s32[1024]{0:T(1024)S(1)}, s32[1024]{0:T(1024)}, u32[]{:S(2)}) copy-start(s32[1024]{0:T(1024)} %param.7) | copy-start | bytes 12292
  12.6 23.6 %all-to-all-start = ((bf16[64,8,768]{2,1,0:T(8,128)(2,1)}), bf16[64,8,768]{2,1,0:T(8,128)(2,1)S(1)}, u32[]{:S(2)}, u32[]{:S(2)}) async-start(bf16[64,8,768]{2,1,0:T(8,128)(2,1)} %broadcast_in_dim.4), calls=%async_computation | async-start | bytes 1572864 | tf_op jit(solution)/shard_map/all_to_all | solution.py:32
  23.5 58.3 %collective-permute-start = (bf16[2048,512]{1,0:T(8,128)(2,1)}, bf16[2048,512]{1,0:T(8,128)(2,1)}, u32[]{:S(2)}, u32[]{:S(2)}) collective-permute-start(bf16[2048,512]{1,0:T(8,128)(2,1)} %get-tuple-element.31), channel_id=1, source_target_pairs={{0,1},{1,0},{2,3},{3,2},{4,5},{5,4},{6,7},{7,6},{8,9},{9,8},{10,11... | collective-permute-start | bytes 6291464 | tf_op jit(solution)/shard_map/ppermute | solution.py:28
  56.3 25.5 %collective-permute-start.2 = (bf16[1024,768]{1,0:T(8,128)(2,1)}, bf16[1024,768]{1,0:T(8,128)(2,1)S(1)}, u32[]{:S(2)}, u32[]{:S(2)}) collective-permute-start(bf16[1024,768]{1,0:T(8,128)(2,1)} %get-tuple-element.35.mine_ref), channel_id=1, source_target_pairs={{0,1},{1,0},{2,3},{3,2},{4,5},{5,4},{6,7},{7,6},{8,9},{9,8},{10,11... | collective-permute-start | bytes 4718600 | tf_op jit(solution)/shard_map/ppermute | solution.py:28
  59.3 19.3 %all-to-all-start.2 = ((bf16[64,8,768]{2,1,0:T(8,128)(2,1)}), bf16[64,8,768]{2,1,0:T(8,128)(2,1)S(1)}, u32[]{:S(2)}, u32[]{:S(2)}) async-start(bf16[64,8,768]{2,1,0:T(8,128)(2,1)} %bitcast.5), calls=%async_computation.2 | async-start | bytes 1572864 | tf_op jit(solution)/shard_map/all_to_all | solution.py:32
  65.8 12.9 %collective-permute-start.6 = (bf16[8,2048]{1,0:T(8,128)(2,1)S(1)}, bf16[8,2048]{1,0:T(8,128)(2,1)S(1)}, u32[]{:S(2)}, u32[]{:S(2)}) collective-permute-start(bf16[8,2048]{1,0:T(8,128)(2,1)S(1)} %get-tuple-element.44), channel_id=1, source_target_pairs={{0,1},{1,0},{2,3},{3,2},{4,5},{5,4},{6,7},{7,6},{8,9},{9,8},{10,11... | collective-permute-start | bytes 98312 | tf_op jit(solution)/shard_map/ppermute | solution.py:28
  78.8 17.6 %collective-permute-start.7 = (bf16[8,768]{1,0:T(8,128)(2,1)S(1)}, bf16[8,768]{1,0:T(8,128)(2,1)S(1)}, u32[]{:S(2)}, u32[]{:S(2)}) collective-permute-start(bf16[8,768]{1,0:T(8,128)(2,1)S(1)} %reduce_sum.21.dqa_ref), channel_id=1, source_target_pairs={{0,1},{1,0},{2,3},{3,2},{4,5},{5,4},{6,7},{7,6},{8,9},{9,8},{10,11... | collective-permute-start | bytes 36872 | tf_op jit(solution)/shard_map/ppermute | solution.py:28
  90.8 28.8 %collective-permute-start.4 = (bf16[512,768]{1,0:T(8,128)(2,1)S(1)}, bf16[512,768]{1,0:T(8,128)(2,1)S(1)}, u32[]{:S(2)}, u32[]{:S(2)}) collective-permute-start(bf16[512,768]{1,0:T(8,128)(2,1)S(1)} %get-tuple-element.39), channel_id=1, source_target_pairs={{0,32},{1,9},{2,34},{3,11},{4,36},{5,13},{6,38},{7,15},{8,40},{9,1... | collective-permute-start | bytes 2359304 | tf_op jit(solution)/shard_map/ppermute | solution.py:387
  91.4 28.2 %collective-permute-start.5 = (bf16[512,768]{1,0:T(8,128)(2,1)S(1)}, bf16[512,768]{1,0:T(8,128)(2,1)S(1)}, u32[]{:S(2)}, u32[]{:S(2)}) collective-permute-start(bf16[512,768]{1,0:T(8,128)(2,1)S(1)} %get-tuple-element.40), channel_id=1, source_target_pairs={{0,96},{1,25},{2,98},{3,27},{4,100},{5,29},{6,102},{7,31},{8,104},... | collective-permute-start | bytes 2359304 | tf_op jit(solution)/shard_map/ppermute | solution.py:387
  92.3 27.3 %collective-permute-start.3 = (bf16[512,768]{1,0:T(8,128)(2,1)S(1)}, bf16[512,768]{1,0:T(8,128)(2,1)S(1)}, u32[]{:S(2)}, u32[]{:S(2)}) collective-permute-start(bf16[512,768]{1,0:T(8,128)(2,1)S(1)} %get-tuple-element.38), channel_id=1, source_target_pairs={{0,64},{1,17},{2,66},{3,19},{4,68},{5,21},{6,70},{7,23},{8,72},{9,... | collective-permute-start | bytes 2359304 | tf_op jit(solution)/shard_map/ppermute | solution.py:379
  96.4 16.1 %collective-permute-start.10 = (bf16[16,1280]{1,0:T(8,128)(2,1)S(1)}, bf16[16,1280]{1,0:T(8,128)(2,1)S(1)}, u32[]{:S(2)}, u32[]{:S(2)}) collective-permute-start(bf16[16,1280]{1,0:T(8,128)(2,1)S(1)} %get-tuple-element.67), channel_id=1, source_target_pairs={{0,96},{1,25},{2,98},{3,27},{4,100},{5,29},{6,102},{7,31},{8,104},... | collective-permute-start | bytes 122888 | tf_op jit(solution)/shard_map/ppermute | solution.py:361
  96.5 23.0 %collective-permute-start.8 = (bf16[16,1280]{1,0:T(8,128)(2,1)S(1)}, bf16[16,1280]{1,0:T(8,128)(2,1)S(1)}, u32[]{:S(2)}, u32[]{:S(2)}) collective-permute-start(bf16[16,1280]{1,0:T(8,128)(2,1)S(1)} %get-tuple-element.65), channel_id=1, source_target_pairs={{0,64},{1,17},{2,66},{3,19},{4,68},{5,21},{6,70},{7,23},{8,72},{9,... | collective-permute-start | bytes 122888 | tf_op jit(solution)/shard_map/ppermute | solution.py:361
  112.5 7.0 %collective-permute-start.9 = (bf16[16,1280]{1,0:T(8,128)(2,1)S(1)}, bf16[16,1280]{1,0:T(8,128)(2,1)S(1)}, u32[]{:S(2)}, u32[]{:S(2)}) collective-permute-start(bf16[16,1280]{1,0:T(8,128)(2,1)S(1)} %get-tuple-element.66), channel_id=1, source_target_pairs={{0,32},{1,9},{2,34},{3,11},{4,36},{5,13},{6,38},{7,15},{8,40},{9,1... | collective-permute-start | bytes 122888 | tf_op jit(solution)/shard_map/ppermute | solution.py:361

commit v3 on v2

--- a/solution.py
+++ b/solution.py
@@ -202,7 +202,7 @@
 
 
 def grad_first_kernel(
-    where_ref, kept_ref, got_ref, mine_ref, theirs_ref, out_ref, sum_ref,
+    where_ref, kept_ref, got_ref, mine_ref, theirs_ref, up_ref, down_ref, sum_ref,
     left_ref, mine_held, sems, dpa_sems,
 ):
     slab = kept_ref.shape[1]
@@ -226,7 +226,18 @@
         sum_ref[ours, :] = both
         part = dot(left_ref[k], both, ((1,), (0,)))
         block = part if block is None else block + part
-    out_ref[...] = block.astype(BF16)
+    size = up_ref.shape[0]
+    up_ref[...] = block[:size].astype(BF16)
+    down_ref[...] = block[size:].astype(BF16)
+
+
+def relay_kernel(none_ref, next_ref, last_ref, up_ref, down_ref, next_out, last_out):
+    size = up_ref.shape[0]
+    top, bottom = slice(0, size), slice(size, 2 * size)
+    next_out[top, :] = (next_ref[top, :].astype(F32) + up_ref[...].astype(F32)).astype(BF16)
+    next_out[bottom, :] = next_ref[bottom, :]
+    last_out[top, :] = last_ref[top, :]
+    last_out[bottom, :] = (last_ref[bottom, :].astype(F32) + down_ref[...].astype(F32)).astype(BF16)
 
 
 def grad_second_kernel(where_ref, kept_ref, got_ref, sum_ref, *refs):
@@ -267,10 +278,10 @@
     copy.wait()
 
 
-def join_kernel(none_ref, own_ref, far_ref, next_ref, last_ref, line_ref, out_ref):
+def join_kernel(none_ref, own_ref, next_ref, last_ref, line_ref, out_ref):
     size = own_ref.shape[0]
     part = dot(line_ref[:, :size], line_ref[:, size:], ((0,), (0,)))
-    for ref in (own_ref, far_ref, next_ref, last_ref):
+    for ref in (own_ref, next_ref, last_ref):
         part += ref[...].astype(F32)
     out_ref[...] = part.astype(BF16)
 
@@ -347,6 +358,36 @@
     dpa_got = to_partner(dpa)
     dqa = dqa.reshape(chips, own_rows, width)
     dqa_own = exchanged(dqa)
+    block = (din // 2 // SIDE, width)
+    half_block = (block[0] // 2, width)
+
+    where = jnp.stack([core, stop])
+    up, down, dpa_sum = kernel_call(
+        grad_first_kernel,
+        [(half_block, BF16)] * 2 + [(dpa.shape, BF16)],
+        where,
+        [(kept, far), (got, far), (dpa, far), dpa_got],
+        scratch=[
+            pltpu.VMEM((2, block[0], slab_rows), BF16),
+            pltpu.VMEM(dpa.shape, BF16),
+            dma((2, SIDE)),
+            dma((2,)),
+        ],
+    )
+    up = lax.ppermute(up, ALL, shift(HOPS[1]))
+    down = lax.ppermute(down, ALL, shift(HOPS[2]))
+    *last, own = kernel_call(
+        grad_second_kernel,
+        [(block, BF16)] * 3,
+        where,
+        [(kept, far), (got, far), dpa_sum],
+        scratch=[pltpu.VMEM((2, 3, block[0], slab_rows), BF16), dma((2, 3, SIDE))],
+    )
+    last = kernel_call(
+        relay_kernel, [(block, BF16)] * 2, jnp.zeros((1,), jnp.int32), [*last, up, down]
+    )
+    sent = [lax.ppermute(x, ALL, shift(hops)) for x, hops in zip(last, HOPS[1:])]
+    dqa_own, own = lax.optimization_barrier((dqa_own, own))
     dqa_own = jnp.sum(dqa_own.astype(F32), axis=0).astype(BF16)
     dqa_own, losses, kept_queries, got_queries = lax.optimization_barrier(
         (dqa_own, losses, kept_queries, got_queries)
@@ -361,30 +402,6 @@
     line = [lax.ppermute(x, ALL, shift(hops)) for x, hops in zip(loads, HOPS)]
     line = jnp.concatenate([loads[-1], *line], axis=0)
 
-    block = (din // 2 // SIDE, width)
-
-    where = jnp.stack([core, stop])
-    first, dpa_sum = kernel_call(
-        grad_first_kernel,
-        [(block, BF16), (dpa.shape, BF16)],
-        where,
-        [(kept, far), (got, far), (dpa, far), dpa_got],
-        scratch=[
-            pltpu.VMEM((2, block[0], slab_rows), BF16),
-            pltpu.VMEM(dpa.shape, BF16),
-            dma((2, SIDE)),
-            dma((2,)),
-        ],
-    )
-    sent = [lax.ppermute(first, ALL, shift(HOPS[0]))]
-    *last, own = kernel_call(
-        grad_second_kernel,
-        [(block, BF16)] * 3,
-        where,
-        [(kept, far), (got, far), dpa_sum],
-        scratch=[pltpu.VMEM((2, 3, block[0], slab_rows), BF16), dma((2, 3, SIDE))],
-    )
-    sent += [lax.ppermute(x, ALL, shift(hops)) for x, hops in zip(last, HOPS[1:])]
     (query_grad,) = kernel_call(
         query_grad_kernel,
         [((own_rows, din), BF16, far)],

time: 139 us -> 126 us (0.906)
  the two profiles are of different devices: /device:TPU:5 before, /device:TPU:0 now
where the time goes in v3:
time: 126 us; the launch traced here: 125 us
  waiting for transfers between devices  31 us (25%)
  blocking collectives  29.2 us (23%)
  Pallas kernels  28.6 us (23%)
  starting transfers between devices  28.2 us (22%)
  local copies, waits for them, and re-layouts  4 us (3%)
  other arithmetic  2.23 us (2%)
    pallas_call x8, Pallas kernels, kernel_call(): pl.pallas_call(body, grid_spec=pltpu.PrefetchScalarGridSpec(num_scalar_pr...  28.6 us
    all_to_all x2, waiting for transfers between devices, exchanged(): return lax.all_to_all(blocks, CHIP, split_axis=0, concat_axis=0, tiled=True)  21.7 us
    all_to_all x2, starting transfers between devices, exchanged(): return lax.all_to_all(blocks, CHIP, split_axis=0, concat_axis=0, tiled=True)  17 us
    all_to_all x1, blocking collectives, exchanged(): return lax.all_to_all(blocks, CHIP, split_axis=0, concat_axis=0, tiled=True)  15.1 us
    all_to_all x1, blocking collectives, per_device(): lax.all_to_all(grad.reshape(SIDE * SIDE, -1, width), ALL, 0, 0, axis_inde...  14.2 us
    ppermute x1, waiting for transfers between devices, per_device(): up = lax.ppermute(up, ALL, shift(HOPS[1]))  5.33 us
    ppermute x3, waiting for transfers between devices, per_device(): line = [lax.ppermute(x, ALL, shift(hops)) for x, hops in zip(loads, HOPS)]  3.93 us
    ppermute x3, starting transfers between devices, per_device(): line = [lax.ppermute(x, ALL, shift(hops)) for x, hops in zip(loads, HOPS)]  3.47 us
  transfers between devices with their start and end apart: 14, of which 6 were waited for; matrix products, arithmetic and copies ran while one was open for 4% of the time, Pallas kernels for 16%

profile of v3, /device:TPU:0, one launch (start us, length us, event | category | flops | bytes accessed | tf_op | source)
XLA Modules:
  0.0 125.1 jit_solution(17978034371616633076)
XLA Ops:
  0.6 0.8 copy-done
  1.5 8.5 %shard_map.67 = (bf16[512,768]{1,0:T(8,128)(2,1)S(1)}, bf16[2048,512]{1,0:T(8,128)(2,1)}, bf16[2048,512]{1,0:T(8,128)(2,1)}, bf16[8,2048]{1,0:T(8,128)(2,1)S(1)}, bf16[8,2048]{1,0:T(8,128)(2,1)S(1)}) custom-call(s32[1]{0:T(128)} %bitcast.3.core_ref, bf16[512,4096]{1,0:T(8,128)(2,1)} %passages_ref.1, bf16[4096,768]{1,0:T(8,128)(2,1)} %adapter_ref.3, ...), custom_call_target="tpu_custom_call" | custom-call | tf_op jit(solution)/shard_map/pallas_call | solution.py:68
  10.1 0.9 convolution_convert_fusion
  11.0 1.0 broadcast_in_dim.4
  12.0 11.5 %all-to-all-start = ((bf16[64,8,768]{2,1,0:T(8,128)(2,1)}), bf16[64,8,768]{2,1,0:T(8,128)(2,1)S(1)}, u32[]{:S(2)}, u32[]{:S(2)}) async-start(bf16[64,8,768]{2,1,0:T(8,128)(2,1)} %broadcast_in_dim.4), calls=%async_computation | async-start | bytes 1572864 | tf_op jit(solution)/shard_map/all_to_all | solution.py:32
  24.2 15.9 %all-to-all-done = bf16[64,8,768]{2,1,0:T(8,128)(2,1)S(1)} async-done(((bf16[64,8,768]{2,1,0:T(8,128)(2,1)}), bf16[64,8,768]{2,1,0:T(8,128)(2,1)S(1)}, u32[]{:S(2)}, u32[]{:S(2)}) %all-to-all-start) | async-done | bytes 786464 | tf_op jit(solution)/shard_map/all_to_all | solution.py:32
  40.1 2.0 %shard_map.68 = (f32[1024,512]{1,0:T(8,128)S(1)}, f32[8,128]{1,0:T(8,128)S(1)}) custom-call(s32[2]{0:T(128)S(1)} %pad_add_fusion.here_ref, bf16[512,768]{1,0:T(8,128)(2,1)S(1)} %bitcast.46, bf16[512,768]{1,0:T(8,128)(2,1)S(1)} %get-tuple-element.35.own_ref, bf16[512,768]{1,0:T(8,128)(2,1)S(1)} %collective-permute-done.other_ref, s32[1,512]{1,0:T(1,128)S(1)} %reshape.51.wanted_ref), custom_call_target="tpu_custom_call" | custom-call | tf_op jit(solution)/shard_map/pallas_call | solution.py:68
  42.2 15.1 %all_to_all.20.packet_ref = f32[64,8,128]{2,1,0:T(8,128)S(1)} all-to-all(f32[64,8,128]{2,1,0:T(8,128)S(1)} %broadcast_in_dim.5), channel_id=1, replica_groups=mesh['row'=4,'col_0'=4,'col_1'=4,'col_2'=2] {'row','col_0','col_1'}, dimensions={0} | all-to-all | bytes 524288 | tf_op jit(solution)/shard_map/all_to_all | solution.py:32
  57.3 3.7 %shard_map.69 = (bf16[1024,768]{1,0:T(8,128)(2,1)}, bf16[512,768]{1,0:T(8,128)(2,1)}, f32[4,128]{1,0:T(4,128)S(1)}) custom-call(s32[2]{0:T(128)S(1)} %pad_add_fusion.here_ref, f32[1024,512]{1,0:T(8,128)S(1)} %get-tuple-element.36.scores_ref, f32[64,8,128]{2,1,0:T(8,128)S(1)} %all_to_all.20.packet_ref, s32[1,512]{1,0:T(1,128)S(1)} %reshape.51.wanted_ref, ...), custom_call_target="tpu_custom_call" | custom-call | tf_op jit(solution)/shard_map/pallas_call | solution.py:68
  60.9 5.5 %all-to-all-start.2 = ((bf16[64,8,768]{2,1,0:T(8,128)(2,1)}), bf16[64,8,768]{2,1,0:T(8,128)(2,1)}, u32[]{:S(2)}, u32[]{:S(2)}) async-start(bf16[64,8,768]{2,1,0:T(8,128)(2,1)} %bitcast.4), calls=%async_computation.2 | async-start | bytes 1572864 | tf_op jit(solution)/shard_map/all_to_all | solution.py:32
  67.1 4.1 %shard_map.70 = (bf16[256,768]{1,0:T(8,128)(2,1)}, bf16[256,768]{1,0:T(8,128)(2,1)S(1)}, bf16[1024,768]{1,0:T(8,128)(2,1)S(1)}) custom-call(s32[2]{0:T(128)S(1)} %pad_add_fusion.1.where_ref, bf16[2048,512]{1,0:T(8,128)(2,1)} %get-tuple-element.39.kept_ref, bf16[2048,512]{1,0:T(8,128)(2,1)} %collective-permute-done.1.got_ref, ...), custom_call_target="tpu_custom_call" | custom-call | tf_op jit(solution)/shard_map/pallas_call | solution.py:68
  71.2 0.7 copy-done.1
  71.9 5.5 %shard_map.71 = (bf16[512,768]{1,0:T(8,128)(2,1)S(1)}, bf16[512,768]{1,0:T(8,128)(2,1)S(1)}, bf16[512,768]{1,0:T(8,128)(2,1)S(1)}) custom-call(s32[2]{0:T(128)S(1)} %pad_add_fusion.1.where_ref, bf16[2048,512]{1,0:T(8,128)(2,1)} %get-tuple-element.39.kept_ref, bf16[2048,512]{1,0:T(8,128)(2,1)} %collective-permute-done.1.got_ref, ...), custom_call_target="tpu_custom_call" | custom-call | tf_op jit(solution)/shard_map/pallas_call | solution.py:68
  77.4 5.8 %all-to-all-done.2 = bf16[64,8,768]{2,1,0:T(8,128)(2,1)} async-done(((bf16[64,8,768]{2,1,0:T(8,128)(2,1)}), bf16[64,8,768]{2,1,0:T(8,128)(2,1)}, u32[]{:S(2)}, u32[]{:S(2)}) %all-to-all-start.2) | async-done | bytes 786464 | tf_op jit(solution)/shard_map/all_to_all | solution.py:32
  83.2 1.3 %reduce_sum.21.dqa_ref = bf16[8,768]{1,0:T(8,128)(2,1)S(1)} reduce(bf16[64,8,768]{2,1,0:T(8,128)(2,1)} %all-to-all-done.2, bf16[]{:T(256)} %constant.86.clone.1), dimensions={0}, to_apply=%region_0.1 | reduce | flops 387072 | bytes 798722 | tf_op jit(solution)/shard_map/reduce_sum | solution.py:391
  84.9 2.9 %collective-permute-start.4 = (bf16[256,768]{1,0:T(8,128)(2,1)}, bf16[256,768]{1,0:T(8,128)(2,1)S(1)}, u32[]{:S(2)}, u32[]{:S(2)}) collective-permute-start(bf16[256,768]{1,0:T(8,128)(2,1)} %copy-done.1), channel_id=1, source_target_pairs={{0,96},{1,25},{2,98},{3,27},{4,100},{5,29},{6,102},{7,31},{8,104},... | collective-permute-start | bytes 1179656 | tf_op jit(solution)/shard_map/ppermute | solution.py:378
  88.4 5.3 %collective-permute-done.3.up_ref = bf16[256,768]{1,0:T(8,128)(2,1)S(1)} collective-permute-done((bf16[256,768]{1,0:T(8,128)(2,1)}, bf16[256,768]{1,0:T(8,128)(2,1)S(1)}, u32[]{:S(2)}, u32[]{:S(2)}) %collective-permute-start.3) | collective-permute-done | bytes 393248 | tf_op jit(solution)/shard_map/ppermute | solution.py:377
  94.1 3.3 %collective-permute-start.6 = (bf16[512,768]{1,0:T(8,128)(2,1)S(1)}, bf16[512,768]{1,0:T(8,128)(2,1)S(1)}, u32[]{:S(2)}, u32[]{:S(2)}) collective-permute-start(bf16[512,768]{1,0:T(8,128)(2,1)S(1)} %get-tuple-element.50), channel_id=1, source_target_pairs={{0,96},{1,25},{2,98},{3,27},{4,100},{5,29},{6,102},{7,31},{8,104},... | collective-permute-start | bytes 2359304 | tf_op jit(solution)/shard_map/ppermute | solution.py:389
  98.1 3.2 %collective-permute-start.11 = (bf16[16,1280]{1,0:T(8,128)(2,1)S(1)}, bf16[16,1280]{1,0:T(8,128)(2,1)S(1)}, u32[]{:S(2)}, u32[]{:S(2)}) collective-permute-start(bf16[16,1280]{1,0:T(8,128)(2,1)S(1)} %get-tuple-element.77), channel_id=1, source_target_pairs={{0,96},{1,25},{2,98},{3,27},{4,100},{5,29},{6,102},{7,31},{8,104},... | collective-permute-start | bytes 122888 | tf_op jit(solution)/shard_map/ppermute | solution.py:402
  101.5 4.2 %shard_map.73 = bf16[8,4096]{1,0:T(8,128)(2,1)} custom-call(s32[1]{0:T(128)} %constant.76.clone.1.none_ref, bf16[4096,768]{1,0:T(8,128)(2,1)} %adapter_ref.3, bf16[8,768]{1,0:T(8,128)(2,1)S(1)} %reduce_sum.21.dqa_ref), custom_call_target="tpu_custom_call" | custom-call | tf_op jit(solution)/shard_map/pallas_call | solution.py:68
  105.7 2.0 %collective-permute-done.10 = bf16[16,1280]{1,0:T(8,128)(2,1)S(1)} collective-permute-done((bf16[16,1280]{1,0:T(8,128)(2,1)S(1)}, bf16[16,1280]{1,0:T(8,128)(2,1)S(1)}, u32[]{:S(2)}, u32[]{:S(2)}) %collective-permute-start.10) | collective-permute-done | bytes 40992 | tf_op jit(solution)/shard_map/ppermute | solution.py:402
  107.8 1.8 %collective-permute-done.9 = bf16[16,1280]{1,0:T(8,128)(2,1)S(1)} collective-permute-done((bf16[16,1280]{1,0:T(8,128)(2,1)S(1)}, bf16[16,1280]{1,0:T(8,128)(2,1)S(1)}, u32[]{:S(2)}, u32[]{:S(2)}) %collective-permute-start.9) | collective-permute-done | bytes 40992 | tf_op jit(solution)/shard_map/ppermute | solution.py:402
  110.2 14.2 %all_to_all.21 = bf16[16,32,768]{2,1,0:T(8,128)(2,1)S(1)} all-to-all(bf16[16,32,768]{2,1,0:T(8,128)(2,1)S(1)} %bitcast.48), channel_id=1, replica_groups={{0,2,4,6,8,10,12,14,16,18,20,22,24,26,28,30},{32,34,36,38,40,42,44,46,4..., dimensions={0} | all-to-all | bytes 1572864 | tf_op jit(solution)/shard_map/all_to_all | solution.py:421
  124.3 0.7 convert_reduce_fusion
  (43 shorter events, 4.2 us)
Async XLA Ops:
  0.6 0.8 copy-start
  1.5 8.6 %copy-start.2 = (bf16[4096,768]{1,0:T(8,128)(2,1)S(1)}, bf16[4096,768]{1,0:T(8,128)(2,1)}, u32[]{:S(2)}) copy-start(bf16[4096,768]{1,0:T(8,128)(2,1)} %adapter_ref.3) | copy-start | bytes 18874372
  10.0 30.2 %collective-permute-start = (bf16[512,768]{1,0:T(8,128)(2,1)S(1)}, bf16[512,768]{1,0:T(8,128)(2,1)S(1)}, u32[]{:S(2)}, u32[]{:S(2)}) collective-permute-start(bf16[512,768]{1,0:T(8,128)(2,1)S(1)} %get-tuple-element.35.own_ref), channel_id=1, source_target_pairs={{0,1},{1,0},{2,3},{3,2},{4,5},{5,4},{6,7},{7,6},{8,9},{9,8},{10,11... | collective-permute-start | bytes 2359304 | tf_op jit(solution)/shard_map/ppermute | solution.py:28
  11.0 12.8 %copy-start.3 = (s32[1024]{0:T(1024)S(1)}, s32[1024]{0:T(1024)}, u32[]{:S(2)}) copy-start(s32[1024]{0:T(1024)} %param.7) | copy-start | bytes 12292
  12.0 28.2 %all-to-all-start = ((bf16[64,8,768]{2,1,0:T(8,128)(2,1)}), bf16[64,8,768]{2,1,0:T(8,128)(2,1)S(1)}, u32[]{:S(2)}, u32[]{:S(2)}) async-start(bf16[64,8,768]{2,1,0:T(8,128)(2,1)} %broadcast_in_dim.4), calls=%async_computation | async-start | bytes 1572864 | tf_op jit(solution)/shard_map/all_to_all | solution.py:32
  23.5 43.6 %collective-permute-start.1 = (bf16[2048,512]{1,0:T(8,128)(2,1)}, bf16[2048,512]{1,0:T(8,128)(2,1)}, u32[]{:S(2)}, u32[]{:S(2)}) collective-permute-start(bf16[2048,512]{1,0:T(8,128)(2,1)} %get-tuple-element.40), channel_id=1, source_target_pairs={{0,1},{1,0},{2,3},{3,2},{4,5},{5,4},{6,7},{7,6},{8,9},{9,8},{10,11... | collective-permute-start | bytes 6291464 | tf_op jit(solution)/shard_map/ppermute | solution.py:28
  60.9 6.2 %collective-permute-start.2 = (bf16[1024,768]{1,0:T(8,128)(2,1)}, bf16[1024,768]{1,0:T(8,128)(2,1)S(1)}, u32[]{:S(2)}, u32[]{:S(2)}) collective-permute-start(bf16[1024,768]{1,0:T(8,128)(2,1)} %get-tuple-element.41.mine_ref), channel_id=1, source_target_pairs={{0,1},{1,0},{2,3},{3,2},{4,5},{5,4},{6,7},{7,6},{8,9},{9,8},{10,11... | collective-permute-start | bytes 4718600 | tf_op jit(solution)/shard_map/ppermute | solution.py:28
  60.9 22.3 %all-to-all-start.2 = ((bf16[64,8,768]{2,1,0:T(8,128)(2,1)}), bf16[64,8,768]{2,1,0:T(8,128)(2,1)}, u32[]{:S(2)}, u32[]{:S(2)}) async-start(bf16[64,8,768]{2,1,0:T(8,128)(2,1)} %bitcast.4), calls=%async_computation.2 | async-start | bytes 1572864 | tf_op jit(solution)/shard_map/all_to_all | solution.py:32
  66.4 18.1 %collective-permute-start.7 = (bf16[8,2048]{1,0:T(8,128)(2,1)S(1)}, bf16[8,2048]{1,0:T(8,128)(2,1)S(1)}, u32[]{:S(2)}, u32[]{:S(2)}) collective-permute-start(bf16[8,2048]{1,0:T(8,128)(2,1)S(1)} %get-tuple-element.54), channel_id=1, source_target_pairs={{0,1},{1,0},{2,3},{3,2},{4,5},{5,4},{6,7},{7,6},{8,9},{9,8},{10,11... | collective-permute-start | bytes 98312 | tf_op jit(solution)/shard_map/ppermute | solution.py:28
  71.1 0.8 copy-start.1
  84.5 9.3 %collective-permute-start.3 = (bf16[256,768]{1,0:T(8,128)(2,1)}, bf16[256,768]{1,0:T(8,128)(2,1)S(1)}, u32[]{:S(2)}, u32[]{:S(2)}) collective-permute-start(bf16[256,768]{1,0:T(8,128)(2,1)} %get-tuple-element.47), channel_id=1, source_target_pairs={{0,32},{1,9},{2,34},{3,11},{4,36},{5,13},{6,38},{7,15},{8,40},{9,1... | collective-permute-start | bytes 1179656 | tf_op jit(solution)/shard_map/ppermute | solution.py:377
  84.9 8.9 %collective-permute-start.4 = (bf16[256,768]{1,0:T(8,128)(2,1)}, bf16[256,768]{1,0:T(8,128)(2,1)S(1)}, u32[]{:S(2)}, u32[]{:S(2)}) collective-permute-start(bf16[256,768]{1,0:T(8,128)(2,1)} %copy-done.1), channel_id=1, source_target_pairs={{0,96},{1,25},{2,98},{3,27},{4,100},{5,29},{6,102},{7,31},{8,104},... | collective-permute-start | bytes 1179656 | tf_op jit(solution)/shard_map/ppermute | solution.py:378
  87.9 10.1 %collective-permute-start.8 = (bf16[8,768]{1,0:T(8,128)(2,1)S(1)}, bf16[8,768]{1,0:T(8,128)(2,1)S(1)}, u32[]{:S(2)}, u32[]{:S(2)}) collective-permute-start(bf16[8,768]{1,0:T(8,128)(2,1)S(1)} %reduce_sum.21.dqa_ref), channel_id=1, source_target_pairs={{0,1},{1,0},{2,3},{3,2},{4,5},{5,4},{6,7},{7,6},{8,9},{9,8},{10,11... | collective-permute-start | bytes 36872 | tf_op jit(solution)/shard_map/ppermute | solution.py:28
  94.0 15.6 %collective-permute-start.5 = (bf16[512,768]{1,0:T(8,128)(2,1)S(1)}, bf16[512,768]{1,0:T(8,128)(2,1)S(1)}, u32[]{:S(2)}, u32[]{:S(2)}) collective-permute-start(bf16[512,768]{1,0:T(8,128)(2,1)S(1)} %get-tuple-element.49), channel_id=1, source_target_pairs={{0,32},{1,9},{2,34},{3,11},{4,36},{5,13},{6,38},{7,15},{8,40},{9,1... | collective-permute-start | bytes 2359304 | tf_op jit(solution)/shard_map/ppermute | solution.py:389
  94.1 15.6 %collective-permute-start.6 = (bf16[512,768]{1,0:T(8,128)(2,1)S(1)}, bf16[512,768]{1,0:T(8,128)(2,1)S(1)}, u32[]{:S(2)}, u32[]{:S(2)}) collective-permute-start(bf16[512,768]{1,0:T(8,128)(2,1)S(1)} %get-tuple-element.50), channel_id=1, source_target_pairs={{0,96},{1,25},{2,98},{3,27},{4,100},{5,29},{6,102},{7,31},{8,104},... | collective-permute-start | bytes 2359304 | tf_op jit(solution)/shard_map/ppermute | solution.py:389
  98.0 9.7 %collective-permute-start.10 = (bf16[16,1280]{1,0:T(8,128)(2,1)S(1)}, bf16[16,1280]{1,0:T(8,128)(2,1)S(1)}, u32[]{:S(2)}, u32[]{:S(2)}) collective-permute-start(bf16[16,1280]{1,0:T(8,128)(2,1)S(1)} %get-tuple-element.76), channel_id=1, source_target_pairs={{0,32},{1,9},{2,34},{3,11},{4,36},{5,13},{6,38},{7,15},{8,40},{9,1... | collective-permute-start | bytes 122888 | tf_op jit(solution)/shard_map/ppermute | solution.py:402
  98.1 9.7 %collective-permute-start.11 = (bf16[16,1280]{1,0:T(8,128)(2,1)S(1)}, bf16[16,1280]{1,0:T(8,128)(2,1)S(1)}, u32[]{:S(2)}, u32[]{:S(2)}) collective-permute-start(bf16[16,1280]{1,0:T(8,128)(2,1)S(1)} %get-tuple-element.77), channel_id=1, source_target_pairs={{0,96},{1,25},{2,98},{3,27},{4,100},{5,29},{6,102},{7,31},{8,104},... | collective-permute-start | bytes 122888 | tf_op jit(solution)/shard_map/ppermute | solution.py:402
  101.3 8.3 %collective-permute-start.9 = (bf16[16,1280]{1,0:T(8,128)(2,1)S(1)}, bf16[16,1280]{1,0:T(8,128)(2,1)S(1)}, u32[]{:S(2)}, u32[]{:S(2)}) collective-permute-start(bf16[16,1280]{1,0:T(8,128)(2,1)S(1)} %get-tuple-element.75), channel_id=1, source_target_pairs={{0,64},{1,17},{2,66},{3,19},{4,68},{5,21},{6,70},{7,23},{8,72},{9,... | collective-permute-start | bytes 122888 | tf_op jit(solution)/shard_map/ppermute | solution.py:402

commit v4 on v3

--- a/solution.py
+++ b/solution.py
@@ -232,17 +232,13 @@
 
 
 def relay_kernel(none_ref, next_ref, last_ref, up_ref, down_ref, next_out, last_out):
-    size = up_ref.shape[0]
-    top, bottom = slice(0, size), slice(size, 2 * size)
-    next_out[top, :] = (next_ref[top, :].astype(F32) + up_ref[...].astype(F32)).astype(BF16)
-    next_out[bottom, :] = next_ref[bottom, :]
-    last_out[top, :] = last_ref[top, :]
-    last_out[bottom, :] = (last_ref[bottom, :].astype(F32) + down_ref[...].astype(F32)).astype(BF16)
+    next_out[...] = (next_ref[...].astype(F32) + up_ref[...].astype(F32)).astype(BF16)
+    last_out[...] = (last_ref[...].astype(F32) + down_ref[...].astype(F32)).astype(BF16)
 
 
 def grad_second_kernel(where_ref, kept_ref, got_ref, sum_ref, *refs):
-    *outs, left_ref, sems = refs
-    slab = kept_ref.shape[1]
+    *halves, own_ref, left_ref, sems = refs
+    slab, size = kept_ref.shape[1], halves[0].shape[0]
     copies = []
     for n, away in enumerate((*HOPS[1:], 0)):
         copies.append(
@@ -253,12 +249,16 @@
         )
         for copy in copies[-1]:
             copy.start()
-    for n, out in enumerate(outs):
+    for n in range(3):
         for copy in copies[n]:
             copy.wait()
         block = dot(left_ref[0, n], sum_ref[:slab, :], ((1,), (0,)))
         block += dot(left_ref[1, n], sum_ref[slab:, :], ((1,), (0,)))
-        out[...] = block.astype(BF16)
+        if n < 2:
+            halves[2 * n][...] = block[:size].astype(BF16)
+            halves[2 * n + 1][...] = block[size:].astype(BF16)
+        else:
+            own_ref[...] = block.astype(BF16)
 
 
 def query_grad_kernel(none_ref, adapter_ref, dqa_ref, out_ref, held_ref, made_ref, sems, out_sem):
@@ -278,12 +278,15 @@
     copy.wait()
 
 
-def join_kernel(none_ref, own_ref, next_ref, last_ref, line_ref, out_ref):
+def join_kernel(none_ref, own_ref, next_top, next_low, last_top, last_low, line_ref, out_ref):
     size = own_ref.shape[0]
     part = dot(line_ref[:, :size], line_ref[:, size:], ((0,), (0,)))
-    for ref in (own_ref, next_ref, last_ref):
-        part += ref[...].astype(F32)
-    out_ref[...] = part.astype(BF16)
+    for k, pair in enumerate(((next_top, last_top), (next_low, last_low))):
+        at = slice(k * size // 2, (k + 1) * size // 2)
+        here = part[at] + own_ref[at, :].astype(F32)
+        for ref in pair:
+            here += ref[...].astype(F32)
+        out_ref[at, :] = here.astype(BF16)
 
 
 def line_block(x, which, core):
@@ -376,32 +379,46 @@
     )
     up = lax.ppermute(up, ALL, shift(HOPS[1]))
     down = lax.ppermute(down, ALL, shift(HOPS[2]))
-    *last, own = kernel_call(
+    next_top, next_low, last_top, last_low, own = kernel_call(
         grad_second_kernel,
-        [(block, BF16)] * 3,
+        [(half_block, BF16)] * 4 + [(block, BF16)],
         where,
         [(kept, far), (got, far), dpa_sum],
         scratch=[pltpu.VMEM((2, 3, block[0], slab_rows), BF16), dma((2, 3, SIDE))],
     )
-    last = kernel_call(
-        relay_kernel, [(block, BF16)] * 2, jnp.zeros((1,), jnp.int32), [*last, up, down]
-    )
-    sent = [lax.ppermute(x, ALL, shift(hops)) for x, hops in zip(last, HOPS[1:])]
+    next_low = lax.ppermute(next_low, ALL, shift(HOPS[1]))
+    last_top = lax.ppermute(last_top, ALL, shift(HOPS[2]))
+    next_top, last_low = kernel_call(
+        relay_kernel,
+        [(half_block, BF16)] * 2,
+        jnp.zeros((1,), jnp.int32),
+        [next_top, last_low, up, down],
+    )
+    next_top = lax.ppermute(next_top, ALL, shift(HOPS[1]))
+    last_low = lax.ppermute(last_low, ALL, shift(HOPS[2]))
     dqa_own, own = lax.optimization_barrier((dqa_own, own))
     dqa_own = jnp.sum(dqa_own.astype(F32), axis=0).astype(BF16)
-    dqa_own, losses, kept_queries, got_queries = lax.optimization_barrier(
-        (dqa_own, losses, kept_queries, got_queries)
+    dqa_own, kept_queries, got_queries = lax.optimization_barrier(
+        (dqa_own, kept_queries, got_queries)
     )
     got_dqa = to_partner(dqa_own)
-    losses = lax.dynamic_slice_in_dim(losses.reshape(half), chip * own_rows, own_rows, 0)
     chip_queries = jnp.concatenate([kept_queries, got_queries], axis=0)
     blocks = [line_block(chip_queries, stop + hops, core) for hops in (*HOPS, 0)]
-    got_dqa, losses, blocks = lax.optimization_barrier((got_dqa, losses, blocks))
+    got_dqa, blocks = lax.optimization_barrier((got_dqa, blocks))
     chip_dqa = jnp.concatenate([dqa_own, got_dqa], axis=0)
     loads = [jnp.concatenate([x, chip_dqa], axis=1) for x in blocks]
     line = [lax.ppermute(x, ALL, shift(hops)) for x, hops in zip(loads, HOPS)]
     line = jnp.concatenate([loads[-1], *line], axis=0)
 
+    (grad,) = kernel_call(
+        join_kernel,
+        [(block, BF16)],
+        jnp.zeros((1,), jnp.int32),
+        [own, next_top, next_low, last_top, last_low, line],
+    )
+    spread = lax.all_to_all(
+        grad.reshape(SIDE * SIDE, -1, width), ALL, 0, 0, axis_index_groups=planes(), tiled=True
+    )
     (query_grad,) = kernel_call(
         query_grad_kernel,
         [((own_rows, din), BF16, far)],
@@ -414,13 +431,8 @@
             dma,
         ],
     )
-    line, query_grad = lax.optimization_barrier((line, query_grad))
-    (grad,) = kernel_call(
-        join_kernel, [(block, BF16)], jnp.zeros((1,), jnp.int32), [own, *sent, line]
-    )
-    spread = lax.all_to_all(
-        grad.reshape(SIDE * SIDE, -1, width), ALL, 0, 0, axis_index_groups=planes(), tiled=True
-    )
+    grad, losses = lax.optimization_barrier((grad, losses))
+    losses = lax.dynamic_slice_in_dim(losses.reshape(half), chip * own_rows, own_rows, 0)
     grad = jnp.sum(spread.astype(F32), axis=0)
 
     return (grad, query_grad, losses)

time: 126 us -> 132 us (1.048)
  waiting for transfers between devices: 31 us -> 45.6 us
  blocking collectives: 29.2 us -> 15.1 us
  starting transfers between devices: 28.2 us -> 34.2 us
    all_to_all x1 -> x0, blocking collectives: 14.2 us -> none  [per_device(): lax.all_to_all(grad.reshape(SIDE * SIDE, -1, width), ALL, 0, 0, axis_inde...]
    ppermute x3, waiting for transfers between devices: 3.93 us -> 13.9 us  [per_device(): line = [lax.ppermute(x, ALL, shift(hops)) for x, hops in zip(loads, HOPS)]]
    all_to_all x0 -> x1, waiting for transfers between devices: none -> 6.69 us  [per_device(): lax.all_to_all(grad.reshape(SIDE * SIDE, -1, width), ALL, 0, 0, axis_inde...]
    all_to_all x0 -> x1, starting transfers between devices: none -> 3.61 us  [per_device(): lax.all_to_all(grad.reshape(SIDE * SIDE, -1, width), ALL, 0, 0, axis_inde...]
    ppermute x2 -> x4, starting transfers between devices: 3.38 us -> 6.53 us  [the longest x1 3.23 us: per_device(): last_top = lax.ppermute(last_top, ALL, shift(HOPS[2]))]
    ppermute x1, waiting for transfers between devices: 5.33 us -> 2.67 us  [per_device(): up = lax.ppermute(up, ALL, shift(HOPS[1]))]
  transfers between devices with their start and end apart: 14 -> 17, of which waited for: 6 -> 7; matrix products, arithmetic and copies ran while one was open for 4% -> 3% of each run, Pallas kernels for 16% -> 14%
where the time goes in v4:
time: 132 us
  waiting for transfers between devices  45.6 us (35%)
  starting transfers between devices  34.2 us (26%)
  Pallas kernels  28.8 us (22%)
  blocking collectives  15.1 us (11%)
  local copies, waits for them, and re-layouts  4.01 us (3%)
  other arithmetic  2.23 us (2%)
    pallas_call x8, Pallas kernels, kernel_call(): pl.pallas_call(body, grid_spec=pltpu.PrefetchScalarGridSpec(num_scalar_pr...  28.8 us
    all_to_all x2, waiting for transfers between devices, exchanged(): return lax.all_to_all(blocks, CHIP, split_axis=0, concat_axis=0, tiled=True)  22.4 us
    all_to_all x2, starting transfers between devices, exchanged(): return lax.all_to_all(blocks, CHIP, split_axis=0, concat_axis=0, tiled=True)  17 us
    all_to_all x1, blocking collectives, exchanged(): return lax.all_to_all(blocks, CHIP, split_axis=0, concat_axis=0, tiled=True)  15.1 us
    ppermute x3, waiting for transfers between devices, per_device(): line = [lax.ppermute(x, ALL, shift(hops)) for x, hops in zip(loads, HOPS)]  13.9 us
    all_to_all x1, waiting for transfers between devices, per_device(): lax.all_to_all(grad.reshape(SIDE * SIDE, -1, width), ALL, 0, 0, axis_inde...  6.69 us
    all_to_all x1, starting transfers between devices, per_device(): lax.all_to_all(grad.reshape(SIDE * SIDE, -1, width), ALL, 0, 0, axis_inde...  3.61 us
    ppermute x1, starting transfers between devices, per_device(): last_top = lax.ppermute(last_top, ALL, shift(HOPS[2]))  3.23 us
  transfers between devices with their start and end apart: 17, of which 7 were waited for; matrix products, arithmetic and copies ran while one was open for 3% of the time, Pallas kernels for 14%

profile of v4, /device:TPU:0, one launch (start us, length us, event | category | flops | bytes accessed | tf_op | source)
XLA Modules:
  0.0 131.9 jit_solution(6643980068793190204)
XLA Ops:
  1.5 8.5 %shard_map.67 = (bf16[512,768]{1,0:T(8,128)(2,1)S(1)}, bf16[2048,512]{1,0:T(8,128)(2,1)}, bf16[2048,512]{1,0:T(8,128)(2,1)}, bf16[8,2048]{1,0:T(8,128)(2,1)S(1)}, bf16[8,2048]{1,0:T(8,128)(2,1)S(1)}) custom-call(s32[1]{0:T(128)} %bitcast.3.core_ref, bf16[512,4096]{1,0:T(8,128)(2,1)} %passages_ref.1, bf16[4096,768]{1,0:T(8,128)(2,1)} %adapter_ref.3, ...), custom_call_target="tpu_custom_call" | custom-call | tf_op jit(solution)/shard_map/pallas_call | solution.py:68
  12.0 11.5 %all-to-all-start = ((bf16[64,8,768]{2,1,0:T(8,128)(2,1)}), bf16[64,8,768]{2,1,0:T(8,128)(2,1)S(1)}, u32[]{:S(2)}, u32[]{:S(2)}) async-start(bf16[64,8,768]{2,1,0:T(8,128)(2,1)} %broadcast_in_dim.4), calls=%async_computation | async-start | bytes 1572864 | tf_op jit(solution)/shard_map/all_to_all | solution.py:32
  24.2 15.9 %all-to-all-done = bf16[64,8,768]{2,1,0:T(8,128)(2,1)S(1)} async-done(((bf16[64,8,768]{2,1,0:T(8,128)(2,1)}), bf16[64,8,768]{2,1,0:T(8,128)(2,1)S(1)}, u32[]{:S(2)}, u32[]{:S(2)}) %all-to-all-start) | async-done | bytes 786464 | tf_op jit(solution)/shard_map/all_to_all | solution.py:32
  40.1 2.0 %shard_map.68 = (f32[1024,512]{1,0:T(8,128)S(1)}, f32[8,128]{1,0:T(8,128)S(1)}) custom-call(s32[2]{0:T(128)S(1)} %pad_add_fusion.here_ref, bf16[512,768]{1,0:T(8,128)(2,1)S(1)} %bitcast.46, bf16[512,768]{1,0:T(8,128)(2,1)S(1)} %get-tuple-element.34.own_ref, bf16[512,768]{1,0:T(8,128)(2,1)S(1)} %collective-permute-done.other_ref, s32[1,512]{1,0:T(1,128)S(1)} %reshape.51.wanted_ref), custom_call_target="tpu_custom_call" | custom-call | tf_op jit(solution)/shard_map/pallas_call | solution.py:68
  42.2 15.1 %all_to_all.20.packet_ref = f32[64,8,128]{2,1,0:T(8,128)S(1)} all-to-all(f32[64,8,128]{2,1,0:T(8,128)S(1)} %broadcast_in_dim.5), channel_id=1, replica_groups=mesh['row'=4,'col_0'=4,'col_1'=4,'col_2'=2] {'row','col_0','col_1'}, dimensions={0} | all-to-all | bytes 524288 | tf_op jit(solution)/shard_map/all_to_all | solution.py:32
  57.3 3.6 %shard_map.69 = (bf16[1024,768]{1,0:T(8,128)(2,1)}, bf16[512,768]{1,0:T(8,128)(2,1)}, f32[4,128]{1,0:T(4,128)S(1)}) custom-call(s32[2]{0:T(128)S(1)} %pad_add_fusion.here_ref, f32[1024,512]{1,0:T(8,128)S(1)} %get-tuple-element.35.scores_ref, f32[64,8,128]{2,1,0:T(8,128)S(1)} %all_to_all.20.packet_ref, s32[1,512]{1,0:T(1,128)S(1)} %reshape.51.wanted_ref, ...), custom_call_target="tpu_custom_call" | custom-call | tf_op jit(solution)/shard_map/pallas_call | solution.py:68
  60.9 5.5 %all-to-all-start.2 = ((bf16[64,8,768]{2,1,0:T(8,128)(2,1)}), bf16[64,8,768]{2,1,0:T(8,128)(2,1)}, u32[]{:S(2)}, u32[]{:S(2)}) async-start(bf16[64,8,768]{2,1,0:T(8,128)(2,1)} %bitcast.4), calls=%async_computation.2 | async-start | bytes 1572864 | tf_op jit(solution)/shard_map/all_to_all | solution.py:32
  67.0 3.4 %shard_map.70 = (bf16[256,768]{1,0:T(8,128)(2,1)S(1)}, bf16[256,768]{1,0:T(8,128)(2,1)S(1)}, bf16[1024,768]{1,0:T(8,128)(2,1)S(1)}) custom-call(s32[2]{0:T(128)S(1)} %pad_add_fusion.1.where_ref, bf16[2048,512]{1,0:T(8,128)(2,1)} %get-tuple-element.38.kept_ref, bf16[2048,512]{1,0:T(8,128)(2,1)} %collective-permute-done.1.got_ref, ...), custom_call_target="tpu_custom_call" | custom-call | tf_op jit(solution)/shard_map/pallas_call | solution.py:68
  71.2 5.5 %shard_map.71 = (bf16[256,768]{1,0:T(8,128)(2,1)S(1)}, bf16[256,768]{1,0:T(8,128)(2,1)S(1)}, bf16[256,768]{1,0:T(8,128)(2,1)S(1)}, bf16[256,768]{1,0:T(8,128)(2,1)S(1)}, bf16[512,768]{1,0:T(8,128)(2,1)S(1)}) custom-call(s32[2]{0:T(128)S(1)} %pad_add_fusion.1.where_ref, bf16[2048,512]{1,0:T(8,128)(2,1)} %get-tuple-element.38.kept_ref, ...), custom_call_target="tpu_custom_call" | custom-call | tf_op jit(solution)/shard_map/pallas_call | solution.py:68
  76.7 6.4 %all-to-all-done.2 = bf16[64,8,768]{2,1,0:T(8,128)(2,1)} async-done(((bf16[64,8,768]{2,1,0:T(8,128)(2,1)}), bf16[64,8,768]{2,1,0:T(8,128)(2,1)}, u32[]{:S(2)}, u32[]{:S(2)}) %all-to-all-start.2) | async-done | bytes 786464 | tf_op jit(solution)/shard_map/all_to_all | solution.py:32
  83.2 1.3 reduce_sum.21.dqa_ref
  85.4 2.9 %collective-permute-start.4 = (bf16[256,768]{1,0:T(8,128)(2,1)S(1)}, bf16[256,768]{1,0:T(8,128)(2,1)S(1)}, u32[]{:S(2)}, u32[]{:S(2)}) collective-permute-start(bf16[256,768]{1,0:T(8,128)(2,1)S(1)} %get-tuple-element.47), channel_id=1, source_target_pairs={{0,96},{1,25},{2,98},{3,27},{4,100},{5,29},{6,102},{7,31},{8,104},... | collective-permute-start | bytes 1179656 | tf_op jit(solution)/shard_map/ppermute | solution.py:381
  88.4 3.2 %collective-permute-start.7 = (bf16[256,768]{1,0:T(8,128)(2,1)S(1)}, bf16[256,768]{1,0:T(8,128)(2,1)S(1)}, u32[]{:S(2)}, u32[]{:S(2)}) collective-permute-start(bf16[256,768]{1,0:T(8,128)(2,1)S(1)} %get-tuple-element.50), channel_id=1, source_target_pairs={{0,96},{1,25},{2,98},{3,27},{4,100},{5,29},{6,102},{7,31},{8,104},... | collective-permute-start | bytes 1179656 | tf_op jit(solution)/shard_map/ppermute | solution.py:390
  91.7 2.7 %collective-permute-done.3.up_ref = bf16[256,768]{1,0:T(8,128)(2,1)S(1)} collective-permute-done((bf16[256,768]{1,0:T(8,128)(2,1)}, bf16[256,768]{1,0:T(8,128)(2,1)S(1)}, u32[]{:S(2)}, u32[]{:S(2)}) %collective-permute-start.3) | collective-permute-done | bytes 393248 | tf_op jit(solution)/shard_map/ppermute | solution.py:380
  94.6 3.2 %collective-permute-start.8 = (bf16[256,768]{1,0:T(8,128)(2,1)S(1)}, bf16[256,768]{1,0:T(8,128)(2,1)S(1)}, u32[]{:S(2)}, u32[]{:S(2)}) collective-permute-start(bf16[256,768]{1,0:T(8,128)(2,1)S(1)} %get-tuple-element.51), channel_id=1, source_target_pairs={{0,96},{1,25},{2,98},{3,27},{4,100},{5,29},{6,102},{7,31},{8,104},... | collective-permute-start | bytes 1179656 | tf_op jit(solution)/shard_map/ppermute | solution.py:398
  97.9 1.3 %collective-permute-start.11 = (bf16[16,1280]{1,0:T(8,128)(2,1)S(1)}, bf16[16,1280]{1,0:T(8,128)(2,1)S(1)}, u32[]{:S(2)}, u32[]{:S(2)}) collective-permute-start(bf16[16,1280]{1,0:T(8,128)(2,1)S(1)} %get-tuple-element.73), channel_id=1, source_target_pairs={{0,64},{1,17},{2,66},{3,19},{4,68},{5,21},{6,70},{7,23},{8,72},{9,... | collective-permute-start | bytes 122888 | tf_op jit(solution)/shard_map/ppermute | solution.py:410
  99.2 6.1 %collective-permute-done.11 = bf16[16,1280]{1,0:T(8,128)(2,1)S(1)} collective-permute-done((bf16[16,1280]{1,0:T(8,128)(2,1)S(1)}, bf16[16,1280]{1,0:T(8,128)(2,1)S(1)}, u32[]{:S(2)}, u32[]{:S(2)}) %collective-permute-start.11) | collective-permute-done | bytes 40992 | tf_op jit(solution)/shard_map/ppermute | solution.py:410
  105.3 1.4 %collective-permute-start.12 = (bf16[16,1280]{1,0:T(8,128)(2,1)S(1)}, bf16[16,1280]{1,0:T(8,128)(2,1)S(1)}, u32[]{:S(2)}, u32[]{:S(2)}) collective-permute-start(bf16[16,1280]{1,0:T(8,128)(2,1)S(1)} %get-tuple-element.74), channel_id=1, source_target_pairs={{0,32},{1,9},{2,34},{3,11},{4,36},{5,13},{6,38},{7,15},{8,40},{9,1... | collective-permute-start | bytes 122888 | tf_op jit(solution)/shard_map/ppermute | solution.py:410
  106.7 3.8 %collective-permute-done.12 = bf16[16,1280]{1,0:T(8,128)(2,1)S(1)} collective-permute-done((bf16[16,1280]{1,0:T(8,128)(2,1)S(1)}, bf16[16,1280]{1,0:T(8,128)(2,1)S(1)}, u32[]{:S(2)}, u32[]{:S(2)}) %collective-permute-start.12) | collective-permute-done | bytes 40992 | tf_op jit(solution)/shard_map/ppermute | solution.py:410
  110.5 4.0 %collective-permute-done.13 = bf16[16,1280]{1,0:T(8,128)(2,1)S(1)} collective-permute-done((bf16[16,1280]{1,0:T(8,128)(2,1)S(1)}, bf16[16,1280]{1,0:T(8,128)(2,1)S(1)}, u32[]{:S(2)}, u32[]{:S(2)}) %collective-permute-start.13) | collective-permute-done | bytes 40992 | tf_op jit(solution)/shard_map/ppermute | solution.py:410
  114.6 1.5 %shard_map.73 = bf16[512,768]{1,0:T(8,128)(2,1)} custom-call(s32[1]{0:T(128)} %constant.76.clone.1.none_ref, bf16[512,768]{1,0:T(8,128)(2,1)S(1)} %get-tuple-element.43.own_ref, bf16[256,768]{1,0:T(8,128)(2,1)S(1)} %collective-permute-done.5.next_top, bf16[256,768]{1,0:T(8,128)(2,1)S(1)} %collective-permute-done.6.next_low, ...), custom_call_target="tpu_custom_call" | custom-call | tf_op jit(solution)/shard_map/pallas_call | solution.py:68
  116.0 3.6 %all-to-all-start.3 = ((bf16[16,32,768]{2,1,0:T(8,128)(2,1)}), bf16[16,32,768]{2,1,0:T(8,128)(2,1)S(1)}, u32[]{:S(2)}, u32[]{:S(2)}) async-start(bf16[16,32,768]{2,1,0:T(8,128)(2,1)} %bitcast.6), calls=%async_computation.3 | async-start | bytes 1572864 | tf_op jit(solution)/shard_map/all_to_all | solution.py:419
  119.6 4.2 %shard_map.74 = bf16[8,4096]{1,0:T(8,128)(2,1)} custom-call(s32[1]{0:T(128)} %constant.76.clone.1.none_ref, bf16[4096,768]{1,0:T(8,128)(2,1)} %adapter_ref.3, bf16[8,768]{1,0:T(8,128)(2,1)S(1)} %reduce_sum.21.dqa_ref), custom_call_target="tpu_custom_call" | custom-call | tf_op jit(solution)/shard_map/pallas_call | solution.py:68
  124.4 6.7 %all-to-all-done.3 = bf16[16,32,768]{2,1,0:T(8,128)(2,1)S(1)} async-done(((bf16[16,32,768]{2,1,0:T(8,128)(2,1)}), bf16[16,32,768]{2,1,0:T(8,128)(2,1)S(1)}, u32[]{:S(2)}, u32[]{:S(2)}) %all-to-all-start.3) | async-done | bytes 786464 | tf_op jit(solution)/shard_map/all_to_all | solution.py:419
  (48 shorter events, 7.6 us)
Async XLA Ops:
  0.6 0.8 copy-start
  1.5 8.6 %copy-start.2 = (bf16[4096,768]{1,0:T(8,128)(2,1)S(1)}, bf16[4096,768]{1,0:T(8,128)(2,1)}, u32[]{:S(2)}) copy-start(bf16[4096,768]{1,0:T(8,128)(2,1)} %adapter_ref.3) | copy-start | bytes 18874372
  10.0 30.2 %collective-permute-start = (bf16[512,768]{1,0:T(8,128)(2,1)S(1)}, bf16[512,768]{1,0:T(8,128)(2,1)S(1)}, u32[]{:S(2)}, u32[]{:S(2)}) collective-permute-start(bf16[512,768]{1,0:T(8,128)(2,1)S(1)} %get-tuple-element.34.own_ref), channel_id=1, source_target_pairs={{0,1},{1,0},{2,3},{3,2},{4,5},{5,4},{6,7},{7,6},{8,9},{9,8},{10,11... | collective-permute-start | bytes 2359304 | tf_op jit(solution)/shard_map/ppermute | solution.py:28
  11.0 12.8 %copy-start.3 = (s32[1024]{0:T(1024)S(1)}, s32[1024]{0:T(1024)}, u32[]{:S(2)}) copy-start(s32[1024]{0:T(1024)} %param.7) | copy-start | bytes 12292
  12.0 28.2 %all-to-all-start = ((bf16[64,8,768]{2,1,0:T(8,128)(2,1)}), bf16[64,8,768]{2,1,0:T(8,128)(2,1)S(1)}, u32[]{:S(2)}, u32[]{:S(2)}) async-start(bf16[64,8,768]{2,1,0:T(8,128)(2,1)} %broadcast_in_dim.4), calls=%async_computation | async-start | bytes 1572864 | tf_op jit(solution)/shard_map/all_to_all | solution.py:32
  23.5 43.5 %collective-permute-start.1 = (bf16[2048,512]{1,0:T(8,128)(2,1)}, bf16[2048,512]{1,0:T(8,128)(2,1)}, u32[]{:S(2)}, u32[]{:S(2)}) collective-permute-start(bf16[2048,512]{1,0:T(8,128)(2,1)} %get-tuple-element.39), channel_id=1, source_target_pairs={{0,1},{1,0},{2,3},{3,2},{4,5},{5,4},{6,7},{7,6},{8,9},{9,8},{10,11... | collective-permute-start | bytes 6291464 | tf_op jit(solution)/shard_map/ppermute | solution.py:28
  60.9 6.1 %collective-permute-start.2 = (bf16[1024,768]{1,0:T(8,128)(2,1)}, bf16[1024,768]{1,0:T(8,128)(2,1)S(1)}, u32[]{:S(2)}, u32[]{:S(2)}) collective-permute-start(bf16[1024,768]{1,0:T(8,128)(2,1)} %get-tuple-element.40.mine_ref), channel_id=1, source_target_pairs={{0,1},{1,0},{2,3},{3,2},{4,5},{5,4},{6,7},{7,6},{8,9},{9,8},{10,11... | collective-permute-start | bytes 4718600 | tf_op jit(solution)/shard_map/ppermute | solution.py:28
  60.9 22.3 %all-to-all-start.2 = ((bf16[64,8,768]{2,1,0:T(8,128)(2,1)}), bf16[64,8,768]{2,1,0:T(8,128)(2,1)}, u32[]{:S(2)}, u32[]{:S(2)}) async-start(bf16[64,8,768]{2,1,0:T(8,128)(2,1)} %bitcast.4), calls=%async_computation.2 | async-start | bytes 1572864 | tf_op jit(solution)/shard_map/all_to_all | solution.py:32
  66.4 18.1 %collective-permute-start.9 = (bf16[8,2048]{1,0:T(8,128)(2,1)S(1)}, bf16[8,2048]{1,0:T(8,128)(2,1)S(1)}, u32[]{:S(2)}, u32[]{:S(2)}) collective-permute-start(bf16[8,2048]{1,0:T(8,128)(2,1)S(1)} %get-tuple-element.54), channel_id=1, source_target_pairs={{0,1},{1,0},{2,3},{3,2},{4,5},{5,4},{6,7},{7,6},{8,9},{9,8},{10,11... | collective-permute-start | bytes 98312 | tf_op jit(solution)/shard_map/ppermute | solution.py:28
  70.4 0.8 copy-start.1
  85.0 6.7 %collective-permute-start.10 = (bf16[8,768]{1,0:T(8,128)(2,1)S(1)}, bf16[8,768]{1,0:T(8,128)(2,1)S(1)}, u32[]{:S(2)}, u32[]{:S(2)}) collective-permute-start(bf16[8,768]{1,0:T(8,128)(2,1)S(1)} %reduce_sum.21.dqa_ref), channel_id=1, source_target_pairs={{0,1},{1,0},{2,3},{3,2},{4,5},{5,4},{6,7},{7,6},{8,9},{9,8},{10,11... | collective-permute-start | bytes 36872 | tf_op jit(solution)/shard_map/ppermute | solution.py:28
  85.1 9.3 %collective-permute-start.3 = (bf16[256,768]{1,0:T(8,128)(2,1)}, bf16[256,768]{1,0:T(8,128)(2,1)S(1)}, u32[]{:S(2)}, u32[]{:S(2)}) collective-permute-start(bf16[256,768]{1,0:T(8,128)(2,1)} %copy-done.1), channel_id=1, source_target_pairs={{0,32},{1,9},{2,34},{3,11},{4,36},{5,13},{6,38},{7,15},{8,40},{9,1... | collective-permute-start | bytes 1179656 | tf_op jit(solution)/shard_map/ppermute | solution.py:380
  85.4 8.9 %collective-permute-start.4 = (bf16[256,768]{1,0:T(8,128)(2,1)S(1)}, bf16[256,768]{1,0:T(8,128)(2,1)S(1)}, u32[]{:S(2)}, u32[]{:S(2)}) collective-permute-start(bf16[256,768]{1,0:T(8,128)(2,1)S(1)} %get-tuple-element.47), channel_id=1, source_target_pairs={{0,96},{1,25},{2,98},{3,27},{4,100},{5,29},{6,102},{7,31},{8,104},... | collective-permute-start | bytes 1179656 | tf_op jit(solution)/shard_map/ppermute | solution.py:381
  88.4 26.1 %collective-permute-start.6 = (bf16[256,768]{1,0:T(8,128)(2,1)S(1)}, bf16[256,768]{1,0:T(8,128)(2,1)S(1)}, u32[]{:S(2)}, u32[]{:S(2)}) collective-permute-start(bf16[256,768]{1,0:T(8,128)(2,1)S(1)} %get-tuple-element.49), channel_id=1, source_target_pairs={{0,32},{1,9},{2,34},{3,11},{4,36},{5,13},{6,38},{7,15},{8,40},{9,1... | collective-permute-start | bytes 1179656 | tf_op jit(solution)/shard_map/ppermute | solution.py:389
  88.4 26.1 %collective-permute-start.7 = (bf16[256,768]{1,0:T(8,128)(2,1)S(1)}, bf16[256,768]{1,0:T(8,128)(2,1)S(1)}, u32[]{:S(2)}, u32[]{:S(2)}) collective-permute-start(bf16[256,768]{1,0:T(8,128)(2,1)S(1)} %get-tuple-element.50), channel_id=1, source_target_pairs={{0,96},{1,25},{2,98},{3,27},{4,100},{5,29},{6,102},{7,31},{8,104},... | collective-permute-start | bytes 1179656 | tf_op jit(solution)/shard_map/ppermute | solution.py:390
  94.5 20.0 %collective-permute-start.5 = (bf16[256,768]{1,0:T(8,128)(2,1)S(1)}, bf16[256,768]{1,0:T(8,128)(2,1)S(1)}, u32[]{:S(2)}, u32[]{:S(2)}) collective-permute-start(bf16[256,768]{1,0:T(8,128)(2,1)S(1)} %get-tuple-element.48), channel_id=1, source_target_pairs={{0,32},{1,9},{2,34},{3,11},{4,36},{5,13},{6,38},{7,15},{8,40},{9,1... | collective-permute-start | bytes 1179656 | tf_op jit(solution)/shard_map/ppermute | solution.py:397
  94.6 19.9 %collective-permute-start.8 = (bf16[256,768]{1,0:T(8,128)(2,1)S(1)}, bf16[256,768]{1,0:T(8,128)(2,1)S(1)}, u32[]{:S(2)}, u32[]{:S(2)}) collective-permute-start(bf16[256,768]{1,0:T(8,128)(2,1)S(1)} %get-tuple-element.51), channel_id=1, source_target_pairs={{0,96},{1,25},{2,98},{3,27},{4,100},{5,29},{6,102},{7,31},{8,104},... | collective-permute-start | bytes 1179656 | tf_op jit(solution)/shard_map/ppermute | solution.py:398
  97.9 7.4 %collective-permute-start.11 = (bf16[16,1280]{1,0:T(8,128)(2,1)S(1)}, bf16[16,1280]{1,0:T(8,128)(2,1)S(1)}, u32[]{:S(2)}, u32[]{:S(2)}) collective-permute-start(bf16[16,1280]{1,0:T(8,128)(2,1)S(1)} %get-tuple-element.73), channel_id=1, source_target_pairs={{0,64},{1,17},{2,66},{3,19},{4,68},{5,21},{6,70},{7,23},{8,72},{9,... | collective-permute-start | bytes 122888 | tf_op jit(solution)/shard_map/ppermute | solution.py:410
  105.3 5.2 %collective-permute-start.12 = (bf16[16,1280]{1,0:T(8,128)(2,1)S(1)}, bf16[16,1280]{1,0:T(8,128)(2,1)S(1)}, u32[]{:S(2)}, u32[]{:S(2)}) collective-permute-start(bf16[16,1280]{1,0:T(8,128)(2,1)S(1)} %get-tuple-element.74), channel_id=1, source_target_pairs={{0,32},{1,9},{2,34},{3,11},{4,36},{5,13},{6,38},{7,15},{8,40},{9,1... | collective-permute-start | bytes 122888 | tf_op jit(solution)/shard_map/ppermute | solution.py:410
  110.5 4.0 %collective-permute-start.13 = (bf16[16,1280]{1,0:T(8,128)(2,1)S(1)}, bf16[16,1280]{1,0:T(8,128)(2,1)S(1)}, u32[]{:S(2)}, u32[]{:S(2)}) collective-permute-start(bf16[16,1280]{1,0:T(8,128)(2,1)S(1)} %get-tuple-element.75), channel_id=1, source_target_pairs={{0,96},{1,25},{2,98},{3,27},{4,100},{5,29},{6,102},{7,31},{8,104},... | collective-permute-start | bytes 122888 | tf_op jit(solution)/shard_map/ppermute | solution.py:410
  116.0 15.1 %all-to-all-start.3 = ((bf16[16,32,768]{2,1,0:T(8,128)(2,1)}), bf16[16,32,768]{2,1,0:T(8,128)(2,1)S(1)}, u32[]{:S(2)}, u32[]{:S(2)}) async-start(bf16[16,32,768]{2,1,0:T(8,128)(2,1)} %bitcast.6), calls=%async_computation.3 | async-start | bytes 1572864 | tf_op jit(solution)/shard_map/all_to_all | solution.py:419

commit v5 on v4

--- a/solution.py
+++ b/solution.py
@@ -53,7 +53,7 @@
     ] + [[number((z, x, y), 1) for z in side for y in side] for x in side]
 
 
-def kernel_call(body, outs, scalars, ins, *, grid=(), scratch=(), limit=16):
+def kernel_call(body, outs, scalars, ins, *, grid=(), scratch=(), limit=24):
     room = pl.BlockSpec(memory_space=pltpu.VMEM)
     arrays, in_specs = [], []
     for entry in ins:
@@ -232,8 +232,8 @@
 
 
 def relay_kernel(none_ref, next_ref, last_ref, up_ref, down_ref, next_out, last_out):
-    next_out[...] = (next_ref[...].astype(F32) + up_ref[...].astype(F32)).astype(BF16)
-    last_out[...] = (last_ref[...].astype(F32) + down_ref[...].astype(F32)).astype(BF16)
+    next_out[...] = next_ref[...] + up_ref[...]
+    last_out[...] = last_ref[...] + down_ref[...]
 
 
 def grad_second_kernel(where_ref, kept_ref, got_ref, sum_ref, *refs):
@@ -278,15 +278,22 @@
     copy.wait()
 
 
-def join_kernel(none_ref, own_ref, next_top, next_low, last_top, last_low, line_ref, out_ref):
+def join_kernel(
+    none_ref, own_ref, next_top, next_low, last_top, last_low, line_ref, out_ref, made_ref, sems
+):
     size = own_ref.shape[0]
+    copies = []
     part = dot(line_ref[:, :size], line_ref[:, size:], ((0,), (0,)))
     for k, pair in enumerate(((next_top, last_top), (next_low, last_low))):
         at = slice(k * size // 2, (k + 1) * size // 2)
         here = part[at] + own_ref[at, :].astype(F32)
         for ref in pair:
             here += ref[...].astype(F32)
-        out_ref[at, :] = here.astype(BF16)
+        made_ref[at, :] = here.astype(BF16)
+        copies.append(pltpu.make_async_copy(made_ref.at[at], out_ref.at[at], sems.at[k]))
+        copies[-1].start()
+    for copy in copies:
+        copy.wait()
 
 
 def line_block(x, which, core):
@@ -412,9 +419,10 @@
 
     (grad,) = kernel_call(
         join_kernel,
-        [(block, BF16)],
+        [(block, BF16, far)],
         jnp.zeros((1,), jnp.int32),
         [own, next_top, next_low, last_top, last_low, line],
+        scratch=[pltpu.VMEM(block, BF16), dma((2,))],
     )
     spread = lax.all_to_all(
         grad.reshape(SIDE * SIDE, -1, width), ALL, 0, 0, axis_index_groups=planes(), tiled=True

time: 132 us -> 132 us (level)
  no operation moved by 1% of the time
where the time goes in v5:
time: 132 us
  waiting for transfers between devices  45.6 us (35%)
  starting transfers between devices  34.3 us (26%)
  Pallas kernels  28.6 us (22%)
  blocking collectives  15.1 us (11%)
  local copies, waits for them, and re-layouts  4.01 us (3%)
  other arithmetic  2.23 us (2%)
    pallas_call x8, Pallas kernels, kernel_call(): pl.pallas_call(body, grid_spec=pltpu.PrefetchScalarGridSpec(num_scalar_pr...  28.6 us
    all_to_all x2, waiting for transfers between devices, exchanged(): return lax.all_to_all(blocks, CHIP, split_axis=0, concat_axis=0, tiled=True)  22.4 us
    all_to_all x2, starting transfers between devices, exchanged(): return lax.all_to_all(blocks, CHIP, split_axis=0, concat_axis=0, tiled=True)  17 us
    all_to_all x1, blocking collectives, exchanged(): return lax.all_to_all(blocks, CHIP, split_axis=0, concat_axis=0, tiled=True)  15.1 us
    ppermute x3, waiting for transfers between devices, per_device(): line = [lax.ppermute(x, ALL, shift(hops)) for x, hops in zip(loads, HOPS)]  13.9 us
    all_to_all x1, waiting for transfers between devices, per_device(): lax.all_to_all(grad.reshape(SIDE * SIDE, -1, width), ALL, 0, 0, axis_inde...  6.69 us
    all_to_all x1, starting transfers between devices, per_device(): lax.all_to_all(grad.reshape(SIDE * SIDE, -1, width), ALL, 0, 0, axis_inde...  3.62 us
    ppermute x1, starting transfers between devices, per_device(): last_top = lax.ppermute(last_top, ALL, shift(HOPS[2]))  3.23 us
  transfers between devices with their start and end apart: 17, of which 7 were waited for; matrix products, arithmetic and copies ran while one was open for 3% of the time, Pallas kernels for 14%

profile of v5, /device:TPU:0, one launch (start us, length us, event | category | flops | bytes accessed | tf_op | source)
XLA Modules:
  0.0 131.7 jit_solution(2746230322853700753)
XLA Ops:
  1.5 8.5 %shard_map.67 = (bf16[512,768]{1,0:T(8,128)(2,1)S(1)}, bf16[2048,512]{1,0:T(8,128)(2,1)}, bf16[2048,512]{1,0:T(8,128)(2,1)}, bf16[8,2048]{1,0:T(8,128)(2,1)S(1)}, bf16[8,2048]{1,0:T(8,128)(2,1)S(1)}) custom-call(s32[1]{0:T(128)} %bitcast.3.core_ref, bf16[512,4096]{1,0:T(8,128)(2,1)} %passages_ref.1, bf16[4096,768]{1,0:T(8,128)(2,1)} %adapter_ref.3, ...), custom_call_target="tpu_custom_call" | custom-call | tf_op jit(solution)/shard_map/pallas_call | solution.py:68
  12.0 11.5 %all-to-all-start = ((bf16[64,8,768]{2,1,0:T(8,128)(2,1)}), bf16[64,8,768]{2,1,0:T(8,128)(2,1)S(1)}, u32[]{:S(2)}, u32[]{:S(2)}) async-start(bf16[64,8,768]{2,1,0:T(8,128)(2,1)} %broadcast_in_dim.4), calls=%async_computation | async-start | bytes 1572864 | tf_op jit(solution)/shard_map/all_to_all | solution.py:32
  24.2 15.9 %all-to-all-done = bf16[64,8,768]{2,1,0:T(8,128)(2,1)S(1)} async-done(((bf16[64,8,768]{2,1,0:T(8,128)(2,1)}), bf16[64,8,768]{2,1,0:T(8,128)(2,1)S(1)}, u32[]{:S(2)}, u32[]{:S(2)}) %all-to-all-start) | async-done | bytes 786464 | tf_op jit(solution)/shard_map/all_to_all | solution.py:32
  40.1 2.0 %shard_map.68 = (f32[1024,512]{1,0:T(8,128)S(1)}, f32[8,128]{1,0:T(8,128)S(1)}) custom-call(s32[2]{0:T(128)S(1)} %pad_add_fusion.here_ref, bf16[512,768]{1,0:T(8,128)(2,1)S(1)} %bitcast.46, bf16[512,768]{1,0:T(8,128)(2,1)S(1)} %get-tuple-element.34.own_ref, bf16[512,768]{1,0:T(8,128)(2,1)S(1)} %collective-permute-done.other_ref, s32[1,512]{1,0:T(1,128)S(1)} %reshape.51.wanted_ref), custom_call_target="tpu_custom_call" | custom-call | tf_op jit(solution)/shard_map/pallas_call | solution.py:68
  42.2 15.1 %all_to_all.20.packet_ref = f32[64,8,128]{2,1,0:T(8,128)S(1)} all-to-all(f32[64,8,128]{2,1,0:T(8,128)S(1)} %broadcast_in_dim.5), channel_id=1, replica_groups=mesh['row'=4,'col_0'=4,'col_1'=4,'col_2'=2] {'row','col_0','col_1'}, dimensions={0} | all-to-all | bytes 524288 | tf_op jit(solution)/shard_map/all_to_all | solution.py:32
  57.3 3.6 %shard_map.69 = (bf16[1024,768]{1,0:T(8,128)(2,1)}, bf16[512,768]{1,0:T(8,128)(2,1)}, f32[4,128]{1,0:T(4,128)S(1)}) custom-call(s32[2]{0:T(128)S(1)} %pad_add_fusion.here_ref, f32[1024,512]{1,0:T(8,128)S(1)} %get-tuple-element.35.scores_ref, f32[64,8,128]{2,1,0:T(8,128)S(1)} %all_to_all.20.packet_ref, s32[1,512]{1,0:T(1,128)S(1)} %reshape.51.wanted_ref, ...), custom_call_target="tpu_custom_call" | custom-call | tf_op jit(solution)/shard_map/pallas_call | solution.py:68
  60.9 5.5 %all-to-all-start.2 = ((bf16[64,8,768]{2,1,0:T(8,128)(2,1)}), bf16[64,8,768]{2,1,0:T(8,128)(2,1)}, u32[]{:S(2)}, u32[]{:S(2)}) async-start(bf16[64,8,768]{2,1,0:T(8,128)(2,1)} %bitcast.4), calls=%async_computation.2 | async-start | bytes 1572864 | tf_op jit(solution)/shard_map/all_to_all | solution.py:32
  67.0 3.4 %shard_map.70 = (bf16[256,768]{1,0:T(8,128)(2,1)S(1)}, bf16[256,768]{1,0:T(8,128)(2,1)S(1)}, bf16[1024,768]{1,0:T(8,128)(2,1)S(1)}) custom-call(s32[2]{0:T(128)S(1)} %pad_add_fusion.1.where_ref, bf16[2048,512]{1,0:T(8,128)(2,1)} %get-tuple-element.38.kept_ref, bf16[2048,512]{1,0:T(8,128)(2,1)} %collective-permute-done.1.got_ref, ...), custom_call_target="tpu_custom_call" | custom-call | tf_op jit(solution)/shard_map/pallas_call | solution.py:68
  71.2 5.5 %shard_map.71 = (bf16[256,768]{1,0:T(8,128)(2,1)S(1)}, bf16[256,768]{1,0:T(8,128)(2,1)S(1)}, bf16[256,768]{1,0:T(8,128)(2,1)S(1)}, bf16[256,768]{1,0:T(8,128)(2,1)S(1)}, bf16[512,768]{1,0:T(8,128)(2,1)S(1)}) custom-call(s32[2]{0:T(128)S(1)} %pad_add_fusion.1.where_ref, bf16[2048,512]{1,0:T(8,128)(2,1)} %get-tuple-element.38.kept_ref, ...), custom_call_target="tpu_custom_call" | custom-call | tf_op jit(solution)/shard_map/pallas_call | solution.py:68
  76.7 6.4 %all-to-all-done.2 = bf16[64,8,768]{2,1,0:T(8,128)(2,1)} async-done(((bf16[64,8,768]{2,1,0:T(8,128)(2,1)}), bf16[64,8,768]{2,1,0:T(8,128)(2,1)}, u32[]{:S(2)}, u32[]{:S(2)}) %all-to-all-start.2) | async-done | bytes 786464 | tf_op jit(solution)/shard_map/all_to_all | solution.py:32
  83.2 1.3 reduce_sum.21.dqa_ref
  85.4 2.9 %collective-permute-start.4 = (bf16[256,768]{1,0:T(8,128)(2,1)S(1)}, bf16[256,768]{1,0:T(8,128)(2,1)S(1)}, u32[]{:S(2)}, u32[]{:S(2)}) collective-permute-start(bf16[256,768]{1,0:T(8,128)(2,1)S(1)} %get-tuple-element.47), channel_id=1, source_target_pairs={{0,96},{1,25},{2,98},{3,27},{4,100},{5,29},{6,102},{7,31},{8,104},... | collective-permute-start | bytes 1179656 | tf_op jit(solution)/shard_map/ppermute | solution.py:388
  88.4 3.2 %collective-permute-start.7 = (bf16[256,768]{1,0:T(8,128)(2,1)S(1)}, bf16[256,768]{1,0:T(8,128)(2,1)S(1)}, u32[]{:S(2)}, u32[]{:S(2)}) collective-permute-start(bf16[256,768]{1,0:T(8,128)(2,1)S(1)} %get-tuple-element.50), channel_id=1, source_target_pairs={{0,96},{1,25},{2,98},{3,27},{4,100},{5,29},{6,102},{7,31},{8,104},... | collective-permute-start | bytes 1179656 | tf_op jit(solution)/shard_map/ppermute | solution.py:397
  91.7 2.7 %collective-permute-done.3.up_ref = bf16[256,768]{1,0:T(8,128)(2,1)S(1)} collective-permute-done((bf16[256,768]{1,0:T(8,128)(2,1)}, bf16[256,768]{1,0:T(8,128)(2,1)S(1)}, u32[]{:S(2)}, u32[]{:S(2)}) %collective-permute-start.3) | collective-permute-done | bytes 393248 | tf_op jit(solution)/shard_map/ppermute | solution.py:387
  94.5 3.2 %collective-permute-start.8 = (bf16[256,768]{1,0:T(8,128)(2,1)S(1)}, bf16[256,768]{1,0:T(8,128)(2,1)S(1)}, u32[]{:S(2)}, u32[]{:S(2)}) collective-permute-start(bf16[256,768]{1,0:T(8,128)(2,1)S(1)} %get-tuple-element.51), channel_id=1, source_target_pairs={{0,96},{1,25},{2,98},{3,27},{4,100},{5,29},{6,102},{7,31},{8,104},... | collective-permute-start | bytes 1179656 | tf_op jit(solution)/shard_map/ppermute | solution.py:405
  97.8 1.3 %collective-permute-start.11 = (bf16[16,1280]{1,0:T(8,128)(2,1)S(1)}, bf16[16,1280]{1,0:T(8,128)(2,1)S(1)}, u32[]{:S(2)}, u32[]{:S(2)}) collective-permute-start(bf16[16,1280]{1,0:T(8,128)(2,1)S(1)} %get-tuple-element.73), channel_id=1, source_target_pairs={{0,64},{1,17},{2,66},{3,19},{4,68},{5,21},{6,70},{7,23},{8,72},{9,... | collective-permute-start | bytes 122888 | tf_op jit(solution)/shard_map/ppermute | solution.py:417
  99.1 6.1 %collective-permute-done.11 = bf16[16,1280]{1,0:T(8,128)(2,1)S(1)} collective-permute-done((bf16[16,1280]{1,0:T(8,128)(2,1)S(1)}, bf16[16,1280]{1,0:T(8,128)(2,1)S(1)}, u32[]{:S(2)}, u32[]{:S(2)}) %collective-permute-start.11) | collective-permute-done | bytes 40992 | tf_op jit(solution)/shard_map/ppermute | solution.py:417
  105.2 1.4 %collective-permute-start.12 = (bf16[16,1280]{1,0:T(8,128)(2,1)S(1)}, bf16[16,1280]{1,0:T(8,128)(2,1)S(1)}, u32[]{:S(2)}, u32[]{:S(2)}) collective-permute-start(bf16[16,1280]{1,0:T(8,128)(2,1)S(1)} %get-tuple-element.74), channel_id=1, source_target_pairs={{0,32},{1,9},{2,34},{3,11},{4,36},{5,13},{6,38},{7,15},{8,40},{9,1... | collective-permute-start | bytes 122888 | tf_op jit(solution)/shard_map/ppermute | solution.py:417
  106.6 3.8 %collective-permute-done.12 = bf16[16,1280]{1,0:T(8,128)(2,1)S(1)} collective-permute-done((bf16[16,1280]{1,0:T(8,128)(2,1)S(1)}, bf16[16,1280]{1,0:T(8,128)(2,1)S(1)}, u32[]{:S(2)}, u32[]{:S(2)}) %collective-permute-start.12) | collective-permute-done | bytes 40992 | tf_op jit(solution)/shard_map/ppermute | solution.py:417
  110.4 4.0 %collective-permute-done.13 = bf16[16,1280]{1,0:T(8,128)(2,1)S(1)} collective-permute-done((bf16[16,1280]{1,0:T(8,128)(2,1)S(1)}, bf16[16,1280]{1,0:T(8,128)(2,1)S(1)}, u32[]{:S(2)}, u32[]{:S(2)}) %collective-permute-start.13) | collective-permute-done | bytes 40992 | tf_op jit(solution)/shard_map/ppermute | solution.py:417
  114.5 1.4 %shard_map.73 = bf16[512,768]{1,0:T(8,128)(2,1)} custom-call(s32[1]{0:T(128)} %constant.76.clone.1.none_ref, bf16[512,768]{1,0:T(8,128)(2,1)S(1)} %get-tuple-element.43.own_ref, bf16[256,768]{1,0:T(8,128)(2,1)S(1)} %collective-permute-done.5.next_top, bf16[256,768]{1,0:T(8,128)(2,1)S(1)} %collective-permute-done.6.next_low, ...), custom_call_target="tpu_custom_call" | custom-call | tf_op jit(solution)/shard_map/pallas_call | solution.py:68
  115.8 3.6 %all-to-all-start.3 = ((bf16[16,32,768]{2,1,0:T(8,128)(2,1)}), bf16[16,32,768]{2,1,0:T(8,128)(2,1)S(1)}, u32[]{:S(2)}, u32[]{:S(2)}) async-start(bf16[16,32,768]{2,1,0:T(8,128)(2,1)} %bitcast.49), calls=%async_computation.3 | async-start | bytes 1572864 | tf_op jit(solution)/shard_map/all_to_all | solution.py:427
  119.5 4.2 %shard_map.74 = bf16[8,4096]{1,0:T(8,128)(2,1)} custom-call(s32[1]{0:T(128)} %constant.76.clone.1.none_ref, bf16[4096,768]{1,0:T(8,128)(2,1)} %adapter_ref.3, bf16[8,768]{1,0:T(8,128)(2,1)S(1)} %reduce_sum.21.dqa_ref), custom_call_target="tpu_custom_call" | custom-call | tf_op jit(solution)/shard_map/pallas_call | solution.py:68
  124.2 6.7 %all-to-all-done.3 = bf16[16,32,768]{2,1,0:T(8,128)(2,1)S(1)} async-done(((bf16[16,32,768]{2,1,0:T(8,128)(2,1)}), bf16[16,32,768]{2,1,0:T(8,128)(2,1)S(1)}, u32[]{:S(2)}, u32[]{:S(2)}) %all-to-all-start.3) | async-done | bytes 786464 | tf_op jit(solution)/shard_map/all_to_all | solution.py:427
  (48 shorter events, 7.5 us)
Async XLA Ops:
  0.6 0.8 copy-start
  1.5 8.6 %copy-start.2 = (bf16[4096,768]{1,0:T(8,128)(2,1)S(1)}, bf16[4096,768]{1,0:T(8,128)(2,1)}, u32[]{:S(2)}) copy-start(bf16[4096,768]{1,0:T(8,128)(2,1)} %adapter_ref.3) | copy-start | bytes 18874372
  10.0 30.2 %collective-permute-start = (bf16[512,768]{1,0:T(8,128)(2,1)S(1)}, bf16[512,768]{1,0:T(8,128)(2,1)S(1)}, u32[]{:S(2)}, u32[]{:S(2)}) collective-permute-start(bf16[512,768]{1,0:T(8,128)(2,1)S(1)} %get-tuple-element.34.own_ref), channel_id=1, source_target_pairs={{0,1},{1,0},{2,3},{3,2},{4,5},{5,4},{6,7},{7,6},{8,9},{9,8},{10,11... | collective-permute-start | bytes 2359304 | tf_op jit(solution)/shard_map/ppermute | solution.py:28
  11.0 12.8 %copy-start.3 = (s32[1024]{0:T(1024)S(1)}, s32[1024]{0:T(1024)}, u32[]{:S(2)}) copy-start(s32[1024]{0:T(1024)} %param.7) | copy-start | bytes 12292
  12.0 28.2 %all-to-all-start = ((bf16[64,8,768]{2,1,0:T(8,128)(2,1)}), bf16[64,8,768]{2,1,0:T(8,128)(2,1)S(1)}, u32[]{:S(2)}, u32[]{:S(2)}) async-start(bf16[64,8,768]{2,1,0:T(8,128)(2,1)} %broadcast_in_dim.4), calls=%async_computation | async-start | bytes 1572864 | tf_op jit(solution)/shard_map/all_to_all | solution.py:32
  23.5 43.5 %collective-permute-start.1 = (bf16[2048,512]{1,0:T(8,128)(2,1)}, bf16[2048,512]{1,0:T(8,128)(2,1)}, u32[]{:S(2)}, u32[]{:S(2)}) collective-permute-start(bf16[2048,512]{1,0:T(8,128)(2,1)} %get-tuple-element.39), channel_id=1, source_target_pairs={{0,1},{1,0},{2,3},{3,2},{4,5},{5,4},{6,7},{7,6},{8,9},{9,8},{10,11... | collective-permute-start | bytes 6291464 | tf_op jit(solution)/shard_map/ppermute | solution.py:28
  60.9 6.1 %collective-permute-start.2 = (bf16[1024,768]{1,0:T(8,128)(2,1)}, bf16[1024,768]{1,0:T(8,128)(2,1)S(1)}, u32[]{:S(2)}, u32[]{:S(2)}) collective-permute-start(bf16[1024,768]{1,0:T(8,128)(2,1)} %get-tuple-element.40.mine_ref), channel_id=1, source_target_pairs={{0,1},{1,0},{2,3},{3,2},{4,5},{5,4},{6,7},{7,6},{8,9},{9,8},{10,11... | collective-permute-start | bytes 4718600 | tf_op jit(solution)/shard_map/ppermute | solution.py:28
  60.9 22.3 %all-to-all-start.2 = ((bf16[64,8,768]{2,1,0:T(8,128)(2,1)}), bf16[64,8,768]{2,1,0:T(8,128)(2,1)}, u32[]{:S(2)}, u32[]{:S(2)}) async-start(bf16[64,8,768]{2,1,0:T(8,128)(2,1)} %bitcast.4), calls=%async_computation.2 | async-start | bytes 1572864 | tf_op jit(solution)/shard_map/all_to_all | solution.py:32
  66.4 18.1 %collective-permute-start.9 = (bf16[8,2048]{1,0:T(8,128)(2,1)S(1)}, bf16[8,2048]{1,0:T(8,128)(2,1)S(1)}, u32[]{:S(2)}, u32[]{:S(2)}) collective-permute-start(bf16[8,2048]{1,0:T(8,128)(2,1)S(1)} %get-tuple-element.54), channel_id=1, source_target_pairs={{0,1},{1,0},{2,3},{3,2},{4,5},{5,4},{6,7},{7,6},{8,9},{9,8},{10,11... | collective-permute-start | bytes 98312 | tf_op jit(solution)/shard_map/ppermute | solution.py:28
  70.4 0.8 copy-start.1
  85.0 6.7 %collective-permute-start.10 = (bf16[8,768]{1,0:T(8,128)(2,1)S(1)}, bf16[8,768]{1,0:T(8,128)(2,1)S(1)}, u32[]{:S(2)}, u32[]{:S(2)}) collective-permute-start(bf16[8,768]{1,0:T(8,128)(2,1)S(1)} %reduce_sum.21.dqa_ref), channel_id=1, source_target_pairs={{0,1},{1,0},{2,3},{3,2},{4,5},{5,4},{6,7},{7,6},{8,9},{9,8},{10,11... | collective-permute-start | bytes 36872 | tf_op jit(solution)/shard_map/ppermute | solution.py:28
  85.1 9.3 %collective-permute-start.3 = (bf16[256,768]{1,0:T(8,128)(2,1)}, bf16[256,768]{1,0:T(8,128)(2,1)S(1)}, u32[]{:S(2)}, u32[]{:S(2)}) collective-permute-start(bf16[256,768]{1,0:T(8,128)(2,1)} %copy-done.1), channel_id=1, source_target_pairs={{0,32},{1,9},{2,34},{3,11},{4,36},{5,13},{6,38},{7,15},{8,40},{9,1... | collective-permute-start | bytes 1179656 | tf_op jit(solution)/shard_map/ppermute | solution.py:387
  85.4 8.9 %collective-permute-start.4 = (bf16[256,768]{1,0:T(8,128)(2,1)S(1)}, bf16[256,768]{1,0:T(8,128)(2,1)S(1)}, u32[]{:S(2)}, u32[]{:S(2)}) collective-permute-start(bf16[256,768]{1,0:T(8,128)(2,1)S(1)} %get-tuple-element.47), channel_id=1, source_target_pairs={{0,96},{1,25},{2,98},{3,27},{4,100},{5,29},{6,102},{7,31},{8,104},... | collective-permute-start | bytes 1179656 | tf_op jit(solution)/shard_map/ppermute | solution.py:388
  88.4 26.0 %collective-permute-start.6 = (bf16[256,768]{1,0:T(8,128)(2,1)S(1)}, bf16[256,768]{1,0:T(8,128)(2,1)S(1)}, u32[]{:S(2)}, u32[]{:S(2)}) collective-permute-start(bf16[256,768]{1,0:T(8,128)(2,1)S(1)} %get-tuple-element.49), channel_id=1, source_target_pairs={{0,32},{1,9},{2,34},{3,11},{4,36},{5,13},{6,38},{7,15},{8,40},{9,1... | collective-permute-start | bytes 1179656 | tf_op jit(solution)/shard_map/ppermute | solution.py:396
  88.4 26.0 %collective-permute-start.7 = (bf16[256,768]{1,0:T(8,128)(2,1)S(1)}, bf16[256,768]{1,0:T(8,128)(2,1)S(1)}, u32[]{:S(2)}, u32[]{:S(2)}) collective-permute-start(bf16[256,768]{1,0:T(8,128)(2,1)S(1)} %get-tuple-element.50), channel_id=1, source_target_pairs={{0,96},{1,25},{2,98},{3,27},{4,100},{5,29},{6,102},{7,31},{8,104},... | collective-permute-start | bytes 1179656 | tf_op jit(solution)/shard_map/ppermute | solution.py:397
  94.4 20.0 %collective-permute-start.5 = (bf16[256,768]{1,0:T(8,128)(2,1)S(1)}, bf16[256,768]{1,0:T(8,128)(2,1)S(1)}, u32[]{:S(2)}, u32[]{:S(2)}) collective-permute-start(bf16[256,768]{1,0:T(8,128)(2,1)S(1)} %get-tuple-element.48), channel_id=1, source_target_pairs={{0,32},{1,9},{2,34},{3,11},{4,36},{5,13},{6,38},{7,15},{8,40},{9,1... | collective-permute-start | bytes 1179656 | tf_op jit(solution)/shard_map/ppermute | solution.py:404
  94.5 19.9 %collective-permute-start.8 = (bf16[256,768]{1,0:T(8,128)(2,1)S(1)}, bf16[256,768]{1,0:T(8,128)(2,1)S(1)}, u32[]{:S(2)}, u32[]{:S(2)}) collective-permute-start(bf16[256,768]{1,0:T(8,128)(2,1)S(1)} %get-tuple-element.51), channel_id=1, source_target_pairs={{0,96},{1,25},{2,98},{3,27},{4,100},{5,29},{6,102},{7,31},{8,104},... | collective-permute-start | bytes 1179656 | tf_op jit(solution)/shard_map/ppermute | solution.py:405
  97.8 7.4 %collective-permute-start.11 = (bf16[16,1280]{1,0:T(8,128)(2,1)S(1)}, bf16[16,1280]{1,0:T(8,128)(2,1)S(1)}, u32[]{:S(2)}, u32[]{:S(2)}) collective-permute-start(bf16[16,1280]{1,0:T(8,128)(2,1)S(1)} %get-tuple-element.73), channel_id=1, source_target_pairs={{0,64},{1,17},{2,66},{3,19},{4,68},{5,21},{6,70},{7,23},{8,72},{9,... | collective-permute-start | bytes 122888 | tf_op jit(solution)/shard_map/ppermute | solution.py:417
  105.2 5.2 %collective-permute-start.12 = (bf16[16,1280]{1,0:T(8,128)(2,1)S(1)}, bf16[16,1280]{1,0:T(8,128)(2,1)S(1)}, u32[]{:S(2)}, u32[]{:S(2)}) collective-permute-start(bf16[16,1280]{1,0:T(8,128)(2,1)S(1)} %get-tuple-element.74), channel_id=1, source_target_pairs={{0,32},{1,9},{2,34},{3,11},{4,36},{5,13},{6,38},{7,15},{8,40},{9,1... | collective-permute-start | bytes 122888 | tf_op jit(solution)/shard_map/ppermute | solution.py:417
  110.4 4.0 %collective-permute-start.13 = (bf16[16,1280]{1,0:T(8,128)(2,1)S(1)}, bf16[16,1280]{1,0:T(8,128)(2,1)S(1)}, u32[]{:S(2)}, u32[]{:S(2)}) collective-permute-start(bf16[16,1280]{1,0:T(8,128)(2,1)S(1)} %get-tuple-element.75), channel_id=1, source_target_pairs={{0,96},{1,25},{2,98},{3,27},{4,100},{5,29},{6,102},{7,31},{8,104},... | collective-permute-start | bytes 122888 | tf_op jit(solution)/shard_map/ppermute | solution.py:417
  115.8 15.1 %all-to-all-start.3 = ((bf16[16,32,768]{2,1,0:T(8,128)(2,1)}), bf16[16,32,768]{2,1,0:T(8,128)(2,1)S(1)}, u32[]{:S(2)}, u32[]{:S(2)}) async-start(bf16[16,32,768]{2,1,0:T(8,128)(2,1)} %bitcast.49), calls=%async_computation.3 | async-start | bytes 1572864 | tf_op jit(solution)/shard_map/all_to_all | solution.py:427
